TPU v7x, 256 devices: a whole 4x4x8 slice. The times are simulated.
256 devices in a mesh: seq: 32 (over z_hi, x, core), uly: 8 (over y, z_lo).
Axes of the slice: x: 4, y: 4, z: 8 (z_hi: 4, z_lo: 2; z = z_hi * 2 + z_lo), core: 2. Of those that a mesh axis runs over, the one named last changes fastest.
Arguments:
- normed: bfloat16 [32768, 5376], P('seq', 'uly'), may hold values from -6 to 6
- q_raw: bfloat16 [32768, 2048], P('seq', 'uly'), may hold values from -6 to 6
- key_weight: bfloat16 [5376, 1024], P('uly', 'seq'), may hold values from -0.078125 to 0.078125
- value_weight: bfloat16 [5376, 1024], P('uly', 'seq'), may hold values from -0.078125 to 0.078125
- q_gain: float32 [128], replicated, may hold values from 0.1 to 1.9
- k_gain: float32 [128], replicated, may hold values from 0.1 to 1.9
- segment_ids: int32 [32768], replicated, may hold values from 0 to 1, as said below
- grad_out: bfloat16 [32768, 2048], P('seq', 'uly'), may hold values from -6 to 6
Outputs:
- attention: bfloat16 [32768, 2048], P('seq', 'uly')
- grad_normed: bfloat16 [32768, 5376], P('seq', 'uly')
- grad_q: bfloat16 [32768, 2048], P('seq', 'uly')
- grad_key_weight: float32 [5376, 1024], P('uly', 'seq')
- grad_value_weight: float32 [5376, 1024], P('uly', 'seq')
Inputs may be any that keep to these rules, and one draw needn't show every extreme that they name: `segment_ids`: 0 up to one position and 1 from it on; that position lies between 8192 and 24576.
All inputs are finite; a program needn't handle non-finite values.
Results may differ from a plain program's by a relative error of at most 0.025.
Values may be sent and summed in bfloat16 or wider, within the bound.
A program may use at most 128 MiB of HBM per device.

v0:
```python
import jax
import jax.numpy as jnp
from jax import lax
from jax.sharding import PartitionSpec as P

HD = 128
WINDOW = 1024


epsilon = 1e-06
query_scale = 168.0 ** (-0.5)


def from_behind(array, axis, by):
    devices = lax.axis_size(axis)
    pairs = [(i, i + by) for i in range(devices) if 0 <= i + by < devices]
    return lax.ppermute(array, axis, pairs)


def normalize(raw_vals, gain, factor):
    mean_sq = jnp.mean(raw_vals * raw_vals, axis=-1, keepdims=True)
    return raw_vals * lax.rsqrt(mean_sq + epsilon) * gain * factor


def attend_block(
    queries, key_block, value_block, grad_block, query_pos, key_pos, query_seg, key_seg
):
    scores = jnp.einsum("bhge,lhe->hgbl", queries, key_block, preferred_element_type=jnp.float32)
    allowed = (
        (key_pos[None, :] <= query_pos[:, None])
        & (key_pos[None, :] > query_pos[:, None] - WINDOW)
        & (key_seg[None, :] == query_seg[:, None])
    )
    exp_scores = jnp.where(allowed[None, None], jnp.exp(scores), 0.0)
    probs = exp_scores / jnp.sum(exp_scores, axis=-1, keepdims=True)
    weights = probs.astype(jnp.bfloat16)
    attended = jnp.einsum(
        "hgbl,lhe->bhge", weights, value_block, preferred_element_type=jnp.float32
    ).astype(jnp.bfloat16)
    dprob = jnp.einsum(
        "bhge,lhe->hgbl", grad_block, value_block, preferred_element_type=jnp.float32
    )
    delta_row = jnp.sum(probs * dprob, axis=-1, keepdims=True)
    dscore = (probs * (dprob - delta_row)).astype(jnp.bfloat16)
    dquery = jnp.einsum("hgbl,lhe->bhge", dscore, key_block, preferred_element_type=jnp.float32)
    dkey = jnp.einsum("hgbl,bhge->lhe", dscore, queries, preferred_element_type=jnp.float32)
    dvalue = jnp.einsum("hgbl,bhge->lhe", weights, grad_block, preferred_element_type=jnp.float32)
    return (attended, dquery, dkey, dvalue)


def body(normed, q_raw, key_weight, value_weight, q_gain, k_gain, segment_ids, grad_out):
    rows_here = normed.shape[0]
    heads_here = q_raw.shape[1] // (2 * HD)
    seq_index = lax.axis_index("seq")
    base_row = seq_index * rows_here
    weight_pair = (
        lax.all_gather(key_weight, "seq", axis=1, tiled=True),
        lax.all_gather(value_weight, "seq", axis=1, tiled=True),
    )
    key_term = jnp.dot(normed, weight_pair[0], preferred_element_type=jnp.float32)
    value_term = jnp.dot(normed, weight_pair[1], preferred_element_type=jnp.float32)
    key_raw, value_raw = (
        lax.psum_scatter(
            key_term.astype(jnp.bfloat16), "uly", scatter_dimension=1, tiled=True
        ).astype(jnp.float32),
        lax.psum_scatter(
            value_term.astype(jnp.bfloat16), "uly", scatter_dimension=1, tiled=True
        ).astype(jnp.float32),
    )
    key_in = key_raw.reshape(rows_here, heads_here, HD)
    keys_bf = normalize(key_in, k_gain, 1.0).astype(jnp.bfloat16)
    values_bf = value_raw.reshape(rows_here, heads_here, HD).astype(jnp.bfloat16)
    query_in = q_raw.astype(jnp.float32).reshape(rows_here, heads_here, 2, HD)
    queries = normalize(query_in, q_gain, query_scale).astype(jnp.bfloat16)
    grad_heads = grad_out.reshape(rows_here, heads_here, 2, HD)
    stacked = jnp.stack([keys_bf, values_bf])
    pieces = []
    distance = 1
    pieces.append(from_behind(stacked, "seq", distance))
    pieces.append(stacked)
    extended = jnp.concatenate(pieces, axis=1)
    block_rows = min(512, rows_here)
    span_rows = block_rows + WINDOW
    count_blocks = rows_here // block_rows
    seg_pad = jnp.concatenate([jnp.full((WINDOW,), -1, jnp.int32), segment_ids])
    query_seg_all = lax.dynamic_slice_in_dim(segment_ids, base_row, rows_here, 0)
    key_seg_all = lax.dynamic_slice_in_dim(seg_pad, base_row, WINDOW + rows_here, 0)

    def step(grad_acc, block_index):
        begin_row = block_index * block_rows
        query_pos = base_row + begin_row + jnp.arange(block_rows, dtype=jnp.int32)
        key_pos = base_row + begin_row - WINDOW + jnp.arange(span_rows, dtype=jnp.int32)
        key_block = lax.dynamic_slice_in_dim(extended, begin_row, span_rows, 1)
        attended, dquery, dkey, dvalue = attend_block(
            lax.dynamic_slice_in_dim(queries, begin_row, block_rows, 0),
            key_block[0],
            key_block[1],
            lax.dynamic_slice_in_dim(grad_heads, begin_row, block_rows, 0),
            query_pos,
            key_pos,
            lax.dynamic_slice_in_dim(query_seg_all, begin_row, block_rows, 0),
            lax.dynamic_slice_in_dim(key_seg_all, begin_row, span_rows, 0),
        )
        update = jnp.stack([dkey, dvalue])
        grad_acc = lax.dynamic_update_slice_in_dim(
            grad_acc,
            lax.dynamic_slice_in_dim(grad_acc, begin_row, span_rows, 1) + update,
            begin_row,
            1,
        )
        return (grad_acc, (attended, dquery))

    zero_acc = jnp.zeros((2, WINDOW + rows_here, heads_here, HD), jnp.float32)
    grad_acc, (attended, dquery) = lax.scan(
        step, zero_acc, jnp.arange(count_blocks, dtype=jnp.int32)
    )
    attention = attended.reshape(rows_here, 2 * heads_here * HD)
    dquery = dquery.reshape(rows_here, heads_here, 2, HD)
    own_grads = grad_acc[:, WINDOW:]
    offset_row = 0
    distance = 1
    first_row = max(0, distance * rows_here - WINDOW)
    piece_rows = rows_here - first_row
    outgoing = grad_acc[:, offset_row : offset_row + piece_rows]
    returned = from_behind(outgoing.astype(jnp.bfloat16), "seq", -distance).astype(outgoing.dtype)
    own_grads = own_grads.at[:, first_row:].add(returned)
    _, pull_query = jax.vjp(lambda raw_vals: normalize(raw_vals, q_gain, query_scale), query_in)
    grad_q = pull_query(dquery)[0].astype(jnp.bfloat16).reshape(rows_here, 2 * heads_here * HD)
    _, pull_key = jax.vjp(lambda raw_vals: normalize(raw_vals, k_gain, 1.0), key_in)
    key_grad = pull_key(own_grads[0])[0].astype(jnp.bfloat16).reshape(rows_here, heads_here * HD)
    value_grad = own_grads[1].astype(jnp.bfloat16).reshape(rows_here, heads_here * HD)
    key_all, value_all = (
        lax.all_gather(key_grad, "uly", axis=1, tiled=True),
        lax.all_gather(value_grad, "uly", axis=1, tiled=True),
    )
    dims_last = (((1,), (1,)), ((), ()))
    total = lax.dot_general(key_all, weight_pair[0], dims_last, preferred_element_type=jnp.float32)
    total = total + lax.dot_general(
        value_all, weight_pair[1], dims_last, preferred_element_type=jnp.float32
    )
    grad_normed = total.astype(jnp.bfloat16)
    dims_first = (((0,), (0,)), ((), ()))
    key_part = lax.dot_general(normed, key_all, dims_first, preferred_element_type=jnp.float32)
    value_part = lax.dot_general(normed, value_all, dims_first, preferred_element_type=jnp.float32)
    grad_key_weight = lax.psum_scatter(
        key_part.astype(jnp.bfloat16), "seq", scatter_dimension=1, tiled=True
    ).astype(jnp.float32)
    grad_value_weight = lax.psum_scatter(
        value_part.astype(jnp.bfloat16), "seq", scatter_dimension=1, tiled=True
    ).astype(jnp.float32)
    return (attention, grad_normed, grad_q, grad_key_weight, grad_value_weight)


def solution(mesh):
    return jax.shard_map(
        body,
        mesh=mesh,
        in_specs=(
            P("seq", "uly"),
            P("seq", "uly"),
            P("uly", "seq"),
            P("uly", "seq"),
            P(),
            P(),
            P(),
            P("seq", "uly"),
        ),
        out_specs=(
            P("seq", "uly"),
            P("seq", "uly"),
            P("seq", "uly"),
            P("uly", "seq"),
            P("uly", "seq"),
        ),
        check_vma=False,
    )
```

profile of v0, /device:TPU:2, one launch (start us, length us, event | category | flops | bytes accessed | tf_op | source)
XLA Modules:
  0.0 659.2 jit_solution(17294904801628966147)
XLA Ops:
  8.7 57.0 %all-gather.6.cloned.1.call-done = bf16[672,1024]{0,1:T(8,128)(2,1)} async-done(((bf16[672,32]{0,1:T(8,128)(2,1)}), bf16[672,1024]{0,1:T(8,128)(2,1)}) %all-gather.6.cloned.1.call-update) | async-done | bytes 1376272 | tf_op jit(solution)/shard_map/all_gather | solution.py:57
  65.7 3.3 convolution_convert_fusion.1
  69.0 2.6 copy.101
  71.6 46.9 %all-gather.8.cloned.1.call-done = bf16[672,1024]{0,1:T(8,128)(2,1)} async-done(((bf16[672,32]{0,1:T(8,128)(2,1)}), bf16[672,1024]{0,1:T(8,128)(2,1)}) %all-gather.8.cloned.1.call-update) | async-done | bytes 1376272 | tf_op jit(solution)/shard_map/all_gather | solution.py:58
  118.6 3.3 convolution_convert_fusion
  121.8 2.6 copy.103
  125.9 48.5 %reduce-scatter.13.cloned.1.call-done = bf16[128,1024]{1,0:T(8,128)(2,1)} async-done(((bf16[1024,1024]{1,0:T(8,128)(2,1)}), bf16[128,1024]{1,0:T(8,128)(2,1)}) %reduce-scatter.13.cloned.1.call-update) | async-done | bytes 262160
  175.8 55.4 %reduce-scatter.15.cloned.1.call-done = bf16[128,1024]{1,0:T(8,128)(2,1)} async-done(((bf16[1024,1024]{1,0:T(8,128)(2,1)}), bf16[128,1024]{1,0:T(8,128)(2,1)}) %reduce-scatter.15.cloned.1.call-update) | async-done | bytes 262160
  231.1 1.8 copy.104
  233.1 1.8 pad_maximum_fusion
  234.9 2.1 collective-permute-start
  237.8 2.0 copy.79
  240.8 4.9 collective-permute-done
  245.8 2.2 maximum_maximum_fusion
  249.4 79.3 %while.19 = (s32[]{:T(128)}, f32[2,2048,1,128]{3,1,2,0:T(8,128)}, bf16[2,512,1,2,128]{4,3,1,0,2:T(2,128)(2,1)}, f32[2,512,1,2,128]{1,4,3,2,0:T(8,128)}, s32[2]{0...) while((s32[]{:T(128)}, f32[2,2048,1,128]{3,1,2,0:T(8,128)}, ...), condition=%wide.region_7.8_spmd, body=%wide.region_4.7_spmd.sunk | while | flops 2447507968 | bytes 149759104 | solution.py:114
  251.7 5.4 fusion.90
  257.2 5.3 fusion.92
  262.5 2.0 fusion.93
  264.5 3.2 convolution_bitcast_fusion.3
  267.7 2.7 fusion.91
  271.7 1.9 copy.127
  273.5 2.7 maximum_add_fusion.2
  276.3 1.9 copy.128
  280.6 2.5 fusion.95
  283.1 4.7 fusion.94
  291.4 5.4 fusion.90
  296.9 5.3 fusion.92
  302.2 2.0 fusion.93
  304.2 3.2 convolution_bitcast_fusion.3
  307.4 2.7 fusion.91
  311.4 1.9 copy.127
  313.2 2.7 maximum_add_fusion.2
  315.9 1.9 copy.128
  320.3 2.5 fusion.95
  322.8 4.7 fusion.94
  330.1 2.1 collective-permute-start.1
  332.2 6.5 collective-permute-done.1
  342.2 67.5 %all-gather.10.cloned.1.call-done = bf16[1024,1024]{1,0:T(8,128)(2,1)} async-done(((bf16[1024,128]{1,0:T(8,128)(2,1)}), bf16[1024,1024]{1,0:T(8,128)(2,1)}) %all-gather.10.cloned.1.call-update) | async-done | bytes 2097168 | tf_op jit(solution)/shard_map/all_gather | solution.py:133
  409.7 3.2 fusion.46
  414.6 51.5 %all-gather.12.cloned.1.call-done = bf16[1,1024,1,1024]{3,1,2,0:T(8,128)(2,1)} async-done(((bf16[1,1024,1,128]{3,1,2,0:T(8,128)(2,1)}), bf16[1,1024,1,1024]{3,1,2,0:T(8,128)(2,1)}) %all-gather.12.cloned.1.call-update) | async-done | bytes 2097168 | tf_op jit(solution)/shard_map/all_gather | solution.py:134
  466.0 4.3 fusion.47
  470.3 2.6 copy.107
  474.3 1.8 copy.85
  476.1 1.6 copy.87
  481.7 3.9 fusion.41
  485.6 2.7 add_convert_fusion
  488.3 70.8 %reduce-scatter.17.cloned.1.call-done = bf16[32,672]{1,0:T(8,128)(2,1)} async-done(((bf16[1024,672]{1,0:T(8,128)(2,1)}), bf16[32,672]{1,0:T(8,128)(2,1)}) %reduce-scatter.17.cloned.1.call-update) | async-done | bytes 43024
  560.8 89.9 %reduce-scatter.19.cloned.1.call-done = bf16[32,672]{1,0:T(8,128)(2,1)} async-done(((bf16[1024,672]{1,0:T(8,128)(2,1)}), bf16[32,672]{1,0:T(8,128)(2,1)}) %reduce-scatter.19.cloned.1.call-update) | async-done | bytes 43024
  (166 shorter events, 36.1 us)
Async XLA Ops:
  7.2 58.5 %copy-start = (bf16[1024,672]{0,1:T(8,128)(2,1)S(1)}, bf16[1024,672]{0,1:T(8,128)(2,1)}, u32[]{:S(2)}) copy-start(bf16[1024,672]{0,1:T(8,128)(2,1)} %param.14) | copy-start | bytes 4128772
  7.2 58.5 %all-gather.6.cloned.1.call-start = ((), (), s32[]{:S(2)}) async-start(), calls=%async_computation.4 | async-start | bytes 1622016 | tf_op jit(solution)/shard_map/all_gather | solution.py:57
  7.9 110.7 %all-gather.8.cloned.1.call-start = ((), (), s32[]{:S(2)}) async-start(), calls=%async_computation.5 | async-start | bytes 1622016 | tf_op jit(solution)/shard_map/all_gather | solution.py:58
  8.7 165.7 %reduce-scatter.13.cloned.1.call-start = ((), (), s32[]{:S(2)}) async-start(), calls=%async_computation.8 | async-start | bytes 2359296
  71.6 159.6 %reduce-scatter.15.cloned.1.call-start = ((), (), s32[]{:S(2)}) async-start(), calls=%async_computation.9 | async-start | bytes 2359296
  124.4 285.3 %all-gather.10.cloned.1.call-start = ((), (), s32[]{:S(2)}) async-start(), calls=%async_computation.6 | async-start | bytes 2359296 | tf_op jit(solution)/shard_map/all_gather | solution.py:133
  125.7 114.1 %copy-start.9 = (bf16[1024,256]{0,1:T(8,128)(2,1)}, bf16[1024,256]{0,1:T(8,128)(2,1)S(1)}, u32[]{:S(2)}) copy-start(bf16[1024,256]{0,1:T(8,128)(2,1)S(1)} %copy.78) | copy-start | bytes 1572868
  125.7 107.3 %copy-start.27 = (f32[128]{0:T(128)S(1)}, f32[128]{0:T(128)}, u32[]{:S(2)}) copy-start(f32[128]{0:T(128)} %param.19) | copy-start | bytes 1540
  125.8 114.0 %copy-start.7 = (f32[1024,256]{0,1:T(8,128)}, f32[1024,256]{0,1:T(8,128)S(1)}, u32[]{:S(2)}) copy-start(f32[1024,256]{0,1:T(8,128)S(1)} %convert_element_type.99) | copy-start | bytes 3145732
  125.9 113.9 %copy-start.21 = (f32[1024,2]{0,1:T(2,128)}, f32[1024,2]{0,1:T(2,128)S(1)}, u32[]{:S(2)}) copy-start(f32[1024,2]{0,1:T(2,128)S(1)} %multiply_reduce_fusion.1) | copy-start | bytes 24580
  125.9 113.9 %copy-start.29 = (f32[128]{0:T(128)S(1)}, f32[128]{0:T(128)}, u32[]{:S(2)}) copy-start(f32[128]{0:T(128)} %param.18) | copy-start | bytes 1540
  175.5 65.3 %copy-start.11 = (bf16[1024,128]{1,0:T(8,128)(2,1)}, bf16[1024,128]{1,0:T(8,128)(2,1)S(1)}, u32[]{:S(2)}) copy-start(bf16[1024,128]{1,0:T(8,128)(2,1)S(1)} %copy.102) | copy-start | bytes 786436
  175.7 59.2 %copy-start.25 = (f32[1024]{0:T(1024)}, f32[1024]{0:T(1024)S(1)}, u32[]{:S(2)}) copy-start(f32[1024]{0:T(1024)S(1)} %fusion.52) | copy-start | bytes 12292
  175.8 59.2 %copy-start.23 = (f32[1024]{0:T(1024)}, f32[1024]{0:T(1024)S(1)}, u32[]{:S(2)}) copy-start(f32[1024]{0:T(1024)S(1)} %fusion.59) | copy-start | bytes 12292
  234.9 10.8 %collective-permute-start = (bf16[2,1024,1,128]{3,1,2,0:T(8,128)(2,1)}, bf16[2,1024,1,128]{3,1,2,0:T(8,128)(2,1)}, u32[]{:S(2)}, u32[]{:S(2)}) collective-permute-start(bf16[2,1024,1,128]{3,1,2,0:T(8,128)(2,1)} %pad_maximum_fusion), channel_id=1, source_target_pairs={{0,8},{8,16},{16,24},{24,32},{32,40},{40,48},{48,56},{56,64},{64,7... | collective-permute-start | bytes 1572872 | tf_op jit(solution)/shard_map/ppermute | solution.py:17
  240.8 8.5 %dynamic-slice-start = ((s32[32768]{0:T(1024)}, s32[]{:T(128)}), s32[1024]{0:T(1024)S(1)}, s32[]{:S(2)}) async-start(s32[32768]{0:T(1024)} %param.20, s32[]{:T(128)} %select_n.34), calls=%async_computation.14 | async-start | bytes 8704 | tf_op jit(solution)/shard_map/dynamic_slice | solution.py:86
  251.7 5.4 copy-start.3
  257.2 5.3 slice-start
  257.2 5.3 slice-start.1
  257.2 5.3 copy-start.4
  264.5 3.3 copy-start.1
  264.5 3.3 copy-start.15
  267.7 2.7 copy-start.6
  278.1 2.5 copy-start.2
  280.6 2.5 copy-start.5
  283.1 4.9 copy-start.16
  291.4 5.4 copy-start.3
  296.8 5.3 slice-start
  296.8 5.3 slice-start.1
  296.8 5.3 copy-start.4
  304.2 3.3 copy-start.1
  304.2 3.3 copy-start.15
  307.4 2.7 copy-start.6
  320.3 2.5 copy-start.5
  322.8 4.9 copy-start.16
  328.7 11.3 %copy-start.12 = (bf16[1024,128]{1,0:T(8,128)(2,1)S(1)}, bf16[1024,128]{1,0:T(8,128)(2,1)}, u32[]{:S(2)}) copy-start(bf16[1024,128]{1,0:T(8,128)(2,1)} %copy-done.11) | copy-start | bytes 786436
  328.7 11.3 %copy-start.28 = (f32[128]{0:T(128)S(1)}, f32[128]{0:T(128)}, u32[]{:S(2)}) copy-start(f32[128]{0:T(128)} %param.19) | copy-start | bytes 1540
  328.7 11.5 %copy-start.26 = (f32[1024]{0:T(1024)S(1)}, f32[1024]{0:T(1024)}, u32[]{:S(2)}) copy-start(f32[1024]{0:T(1024)} %copy-done.25) | copy-start | bytes 12292
  328.7 11.5 %copy-start.24 = (f32[1024]{0:T(1024)S(1)}, f32[1024]{0:T(1024)}, u32[]{:S(2)}) copy-start(f32[1024]{0:T(1024)} %copy-done.23) | copy-start | bytes 12292
  330.1 8.6 %collective-permute-start.1 = (bf16[2,1024,1,128]{3,1,2,0:T(8,128)(2,1)S(1)}, bf16[2,1024,1,128]{3,1,2,0:T(8,128)(2,1)S(1)}, u32[]{:S(2)}, u32[]{:S(2)}) collective-permute-start(bf16[2,1024,1,128]{3,1,2,0:T(8,128)(2,1)S(1)} %slice.69), channel_id=1, source_target_pairs={{8,0},{16,8},{24,16},{32,24},{40,32},{48,40},{56,48},{64,56},{72,6... | collective-permute-start | bytes 1572872 | tf_op jit(solution)/shard_map/ppermute | solution.py:17
  341.3 124.7 %all-gather.12.cloned.1.call-start = ((), (), s32[]{:S(2)}) async-start(), calls=%async_computation.7 | async-start | bytes 2359296 | tf_op jit(solution)/shard_map/all_gather | solution.py:134
  342.1 216.9 %reduce-scatter.17.cloned.1.call-start = ((), (), s32[]{:S(2)}) async-start(), calls=%async_computation.10 | async-start | bytes 1622016
  414.5 236.2 %reduce-scatter.19.cloned.1.call-start = ((), (), s32[]{:S(2)}) async-start(), calls=%async_computation.11 | async-start | bytes 1622016
  470.3 2.7 copy-start.30
  470.3 2.7 copy-start.13
  476.1 3.2 copy-start.8
  481.7 3.9 copy-start.31
  481.7 3.9 copy-start.32
  (9 other events, 12.7 us)
Sparse Core Ops, SparseCore 0:
  10.6 55.0 all-gather.5
  68.2 50.2 all-gather.7
  121.1 53.2 reduce-scatter.12
  176.8 54.2 reduce-scatter.14
  341.4 68.2 all-gather.9
  411.9 54.1 all-gather.11
  469.9 89.1 reduce-scatter.16
  562.9 87.7 reduce-scatter.18
where the time goes:
time: 661 us; the launch traced here: 659 us
  waiting for transfers between devices  500 us (76%)
  matrix products  68.2 us (10%)
  local copies, waits for them, and re-layouts  50 us (8%)
  other arithmetic  20.2 us (3%)
  between operations  14.5 us (2%)
    unnamed x12, waiting for transfers between devices  266 us
    all_gather x1, waiting for transfers between devices, body(): lax.all_gather(key_grad, 'uly', axis=1, tiled=True)  67.5 us
    all_gather x1, waiting for transfers between devices, body(): lax.all_gather(key_weight, 'seq', axis=1, tiled=True)  57 us
    all_gather x1, waiting for transfers between devices, body(): lax.all_gather(value_grad, 'uly', axis=1, tiled=True)  51.5 us
    all_gather x1, waiting for transfers between devices, body(): lax.all_gather(value_weight, 'seq', axis=1, tiled=True)  46.9 us
    unnamed x63, local copies, waits for them, and re-layouts  22.4 us
  transfers between devices with their start and end apart: 10, of which 10 were waited for; matrix products, arithmetic and copies ran while one was open for 7% of the time, Pallas kernels for 0%

commit v1 on v0

--- a/solution.py
+++ b/solution.py
@@ -20,6 +20,15 @@
 def normalize(raw_vals, gain, factor):
     mean_sq = jnp.mean(raw_vals * raw_vals, axis=-1, keepdims=True)
     return raw_vals * lax.rsqrt(mean_sq + epsilon) * gain * factor
+
+
+def exchange(blocks, axis):
+    return lax.all_to_all(blocks, axis, 0, 0)
+
+
+def gather_all(block, axis):
+    count = lax.axis_size(axis)
+    return exchange(jnp.broadcast_to(block[None], (count,) + block.shape), axis)
 
 
 def attend_block(
@@ -50,23 +59,23 @@
 
 def body(normed, q_raw, key_weight, value_weight, q_gain, k_gain, segment_ids, grad_out):
     rows_here = normed.shape[0]
+    feats = normed.shape[1]
     heads_here = q_raw.shape[1] // (2 * HD)
+    n_seq = lax.axis_size("seq")
+    n_uly = lax.axis_size("uly")
+    col_block = key_weight.shape[1]
     seq_index = lax.axis_index("seq")
     base_row = seq_index * rows_here
-    weight_pair = (
-        lax.all_gather(key_weight, "seq", axis=1, tiled=True),
-        lax.all_gather(value_weight, "seq", axis=1, tiled=True),
-    )
-    key_term = jnp.dot(normed, weight_pair[0], preferred_element_type=jnp.float32)
-    value_term = jnp.dot(normed, weight_pair[1], preferred_element_type=jnp.float32)
-    key_raw, value_raw = (
-        lax.psum_scatter(
-            key_term.astype(jnp.bfloat16), "uly", scatter_dimension=1, tiled=True
-        ).astype(jnp.float32),
-        lax.psum_scatter(
-            value_term.astype(jnp.bfloat16), "uly", scatter_dimension=1, tiled=True
-        ).astype(jnp.float32),
-    )
+    pair_local = jnp.stack([key_weight, value_weight], axis=1)
+    gathered = gather_all(pair_local, "seq")
+    weight_all = gathered.transpose(1, 2, 0, 3).reshape(feats, 2, n_uly, heads_here * HD)
+    terms = jnp.einsum(
+        "tf,fkhc->htkc", normed, weight_all, preferred_element_type=jnp.float32
+    ).astype(jnp.bfloat16)
+    received = exchange(terms, "uly")
+    raw_pair = jnp.sum(received.astype(jnp.float32), axis=0)
+    key_raw = raw_pair[:, 0]
+    value_raw = raw_pair[:, 1]
     key_in = key_raw.reshape(rows_here, heads_here, HD)
     keys_bf = normalize(key_in, k_gain, 1.0).astype(jnp.bfloat16)
     values_bf = value_raw.reshape(rows_here, heads_here, HD).astype(jnp.bfloat16)
@@ -129,25 +138,17 @@
     _, pull_key = jax.vjp(lambda raw_vals: normalize(raw_vals, k_gain, 1.0), key_in)
     key_grad = pull_key(own_grads[0])[0].astype(jnp.bfloat16).reshape(rows_here, heads_here * HD)
     value_grad = own_grads[1].astype(jnp.bfloat16).reshape(rows_here, heads_here * HD)
-    key_all, value_all = (
-        lax.all_gather(key_grad, "uly", axis=1, tiled=True),
-        lax.all_gather(value_grad, "uly", axis=1, tiled=True),
-    )
-    dims_last = (((1,), (1,)), ((), ()))
-    total = lax.dot_general(key_all, weight_pair[0], dims_last, preferred_element_type=jnp.float32)
-    total = total + lax.dot_general(
-        value_all, weight_pair[1], dims_last, preferred_element_type=jnp.float32
-    )
-    grad_normed = total.astype(jnp.bfloat16)
-    dims_first = (((0,), (0,)), ((), ()))
-    key_part = lax.dot_general(normed, key_all, dims_first, preferred_element_type=jnp.float32)
-    value_part = lax.dot_general(normed, value_all, dims_first, preferred_element_type=jnp.float32)
-    grad_key_weight = lax.psum_scatter(
-        key_part.astype(jnp.bfloat16), "seq", scatter_dimension=1, tiled=True
-    ).astype(jnp.float32)
-    grad_value_weight = lax.psum_scatter(
-        value_part.astype(jnp.bfloat16), "seq", scatter_dimension=1, tiled=True
-    ).astype(jnp.float32)
+    grads_all = gather_all(jnp.stack([key_grad, value_grad], axis=1), "uly")
+    grad_normed = jnp.einsum(
+        "htkc,fkhc->tf", grads_all, weight_all, preferred_element_type=jnp.float32
+    ).astype(jnp.bfloat16)
+    weight_part = jnp.einsum(
+        "tf,htkc->fkhc", normed, grads_all, preferred_element_type=jnp.float32
+    ).astype(jnp.bfloat16)
+    to_owner = weight_part.reshape(feats, 2, n_seq, col_block).transpose(2, 0, 1, 3)
+    summed = jnp.sum(exchange(to_owner, "seq").astype(jnp.float32), axis=0)
+    grad_key_weight = summed[:, 0]
+    grad_value_weight = summed[:, 1]
     return (attention, grad_normed, grad_q, grad_key_weight, grad_value_weight)
 
 

time: 661 us -> 394 us (0.60)
  waiting for transfers between devices: 500 us -> 114 us
  blocking collectives: 0 us -> 138 us
  starting transfers between devices: 4.56 us -> 19.4 us
  between operations: 14.5 us -> 1.12 us
  matrix products: 68.2 us -> 57 us
  local copies, waits for them, and re-layouts: 50 us -> 39.8 us
    unnamed x12 -> x0, waiting for transfers between devices: 266 us -> none
    all_gather x4 -> x0, waiting for transfers between devices: 223 us -> none  [the longest x1 67.5 us: body(): lax.all_gather(key_grad, 'uly', axis=1, tiled=True)]
    all_to_all x0 -> x2, blocking collectives: none -> 138 us  [exchange(): return lax.all_to_all(blocks, axis, 0, 0)]
    all_to_all x0 -> x2, waiting for transfers between devices: none -> 101 us  [exchange(): return lax.all_to_all(blocks, axis, 0, 0)]
    all_to_all x0 -> x2, starting transfers between devices: none -> 15.4 us  [exchange(): return lax.all_to_all(blocks, axis, 0, 0)]
    unnamed x63 -> x55, local copies, waits for them, and re-layouts: 22.4 us -> 9.52 us
    convert_element_type x0 -> x3, local copies, waits for them, and re-layouts: none -> 7.09 us  [the longest x1 4.61 us: body(): weight_part = jnp.einsum('tf,htkc->fkhc', normed, grads_all, preferred_el...]
    dot_general x6 -> x3, matrix products: 20.6 us -> 15.2 us  [the longest x1 7.3 us: body(): jnp.einsum('htkc,fkhc->tf', grads_all, weight_all, preferred_element_type...]
  transfers between devices with their start and end apart: 10 -> 4, of which waited for: 10 -> 4; matrix products, arithmetic and copies ran while one was open for 7% -> 6% of each run, Pallas kernels for 0% -> 0%
where the time goes in v1:
time: 394 us; the launch traced here: 391 us
  blocking collectives  138 us (35%)
  waiting for transfers between devices  114 us (29%)
  matrix products  57 us (14%)
  local copies, waits for them, and re-layouts  39.8 us (10%)
  other arithmetic  20.3 us (5%)
  starting transfers between devices  19.4 us (5%)
    all_to_all x2, blocking collectives, exchange(): return lax.all_to_all(blocks, axis, 0, 0)  138 us
    all_to_all x2, waiting for transfers between devices, exchange(): return lax.all_to_all(blocks, axis, 0, 0)  101 us
    all_to_all x2, starting transfers between devices, exchange(): return lax.all_to_all(blocks, axis, 0, 0)  15.4 us
    ppermute x2, waiting for transfers between devices, from_behind(): return lax.ppermute(array, axis, pairs)  13.1 us
    dot_general x2, matrix products, attend_block(): jnp.einsum('bhge,lhe->hgbl', queries, key_block, preferred_element_type=j...  10.9 us
    dot_general x2, matrix products, attend_block(): jnp.einsum('bhge,lhe->hgbl', grad_block, value_block, preferred_element_t...  10.6 us
    unnamed x55, local copies, waits for them, and re-layouts  9.52 us
  transfers between devices with their start and end apart: 4, of which 4 were waited for; matrix products, arithmetic and copies ran while one was open for 6% of the time, Pallas kernels for 0%

profile of v1, /device:TPU:2, one launch (start us, length us, event | category | flops | bytes accessed | tf_op | source)
XLA Modules:
  0.0 391.3 jit_solution(13356692624314235337)
XLA Ops:
  2.0 84.6 %all_to_all.20 = bf16[32,672,2,32]{1,3,2,0:T(8,128)(2,1)S(1)} all-to-all(bf16[32,672,2,32]{1,3,2,0:T(8,128)(2,1)S(1)} %broadcast_in_dim.88), channel_id=1, replica_groups=mesh['seq'=32,'uly'=8] {'seq'}, dimensions={0} | all-to-all | bytes 5505024 | tf_op jit(solution)/shard_map/all_to_all | solution.py:26
  86.8 1.7 copy-done.12
  88.5 3.6 convert_bitcast_fusion
  92.1 2.4 copy.83
  94.6 4.9 %all-to-all-start.1 = ((bf16[8,1024,2,128]{1,3,2,0:T(8,128)(2,1)}), bf16[8,1024,2,128]{1,3,2,0:T(8,128)(2,1)}, u32[]{:S(2)}, u32[]{:S(2)}) async-start(bf16[8,1024,2,128]{1,3,2,0:T(8,128)(2,1)} %copy.83), calls=%async_computation.1 | async-start | bytes 8388608 | tf_op jit(solution)/shard_map/all_to_all | solution.py:26
  100.0 48.6 %all-to-all-done.1 = bf16[8,1024,2,128]{1,3,2,0:T(8,128)(2,1)} async-done(((bf16[8,1024,2,128]{1,3,2,0:T(8,128)(2,1)}), bf16[8,1024,2,128]{1,3,2,0:T(8,128)(2,1)}, u32[]{:S(2)}, u32[]{:S(2)}) %all-to-all-start.1) | async-done | bytes 4194336 | tf_op jit(solution)/shard_map/all_to_all | solution.py:26
  148.6 3.2 convert_reduce_fusion
  153.4 2.1 collective-permute-start
  157.6 6.4 %collective-permute-done = bf16[2,1024,1,128]{1,3,2,0:T(8,128)(2,1)} collective-permute-done((bf16[2,1024,1,128]{1,3,2,0:T(8,128)(2,1)S(1)}, bf16[2,1024,1,128]{1,3,2,0:T(8,128)(2,1)}, u32[]{:S(2)}, u32[]{:S(2)}) %collective-permute-start) | collective-permute-done | bytes 524320 | tf_op jit(solution)/shard_map/ppermute | solution.py:17
  164.0 2.2 maximum_maximum_fusion
  166.1 1.6 broadcast_in_dim.85
  167.8 55.8 %while.19 = (s32[]{:T(128)}, f32[2,2048,1,128]{1,3,2,0:T(8,128)}, bf16[2,512,1,2,128]{4,3,1,0,2:T(2,128)(2,1)}, f32[2,512,1,2,128]{1,4,3,2,0:T(8,128)}, s32[2]{0...) while((s32[]{:T(128)}, f32[2,2048,1,128]{1,3,2,0:T(8,128)}, ...), condition=%wide.region_6.7_spmd, body=%wide.region_3.6_spmd.sunk | while | flops 2447507968 | bytes 113059336 | solution.py:123
  169.2 1.1 compare_and_fusion.2
  170.3 5.5 %fusion.78 = (f32[2,512]{1,0:T(2,128)S(1)}, f32[1536,512,2]{1,0,2:T(8,128)}) fusion(pred[512,1536]{0,1:T(8,128)(4,1)S(1)} %compare_and_fusion.2, bf16[1024,1,2,128]{0,3,2,1:T(8,128)(2,1)} %get-tuple-element.399, s32[]{:T(128)S(6)} %select_n.65, bf16[2,2048,1,128]{1,3,2,0:T(8,128)(2,1)} %get-tuple-element.403, s32[]{:T(128)S(6)} %select_n.64), kind=kOutput, calls=%fused_computation.7.clone.1 | convolution fusion | flops 405797888 | bytes 7737352 | tf_op jit(solution)/shard_map/while/body/eval_jaxpr/bhge,lhe->hgbl/dot_general | solution.py:37
  175.8 5.3 %fusion.80 = (f32[2,512]{1,0:T(2,128)S(1)}, f32[1536,512,2]{1,0,2:T(8,128)S(1)}) fusion(f32[2,512]{1,0:T(2,128)S(1)} %get-tuple-element.354, f32[1536,512,2]{1,0,2:T(8,128)} %get-tuple-element.355, pred[512,1536]{0,1:T(8,128)(4,1)} %copy-done.1, bf16[1024,1,2,128]{0,3,2,1:T(8,128)(2,1)} %get-tuple-element.404, s32[]{:T(128)S(6)} %select_n.65, ...), kind=kOutput, calls=%fused_computation.3.clone.1 | convolution fusion | flops 408943616 | bytes 14032908 | tf_op jit(solution)/shard_map/while/body/eval_jaxpr/bhge,lhe->hgbl/dot_general | solution.py:49
  181.1 2.0 fusion.81
  183.1 2.2 convolution_bitcast_fusion.3
  185.3 1.8 fusion.79
  187.4 2.7 fusion.84
  190.1 3.5 fusion.83
  193.7 1.1 copy.128
  197.1 1.1 compare_and_fusion.2
  198.2 5.5 %fusion.78 = (f32[2,512]{1,0:T(2,128)S(1)}, f32[1536,512,2]{1,0,2:T(8,128)}) fusion(pred[512,1536]{0,1:T(8,128)(4,1)S(1)} %compare_and_fusion.2, bf16[1024,1,2,128]{0,3,2,1:T(8,128)(2,1)} %get-tuple-element.399, s32[]{:T(128)S(6)} %select_n.65, bf16[2,2048,1,128]{1,3,2,0:T(8,128)(2,1)} %get-tuple-element.403, s32[]{:T(128)S(6)} %select_n.64), kind=kOutput, calls=%fused_computation.7.clone.1 | convolution fusion | flops 405797888 | bytes 7737352 | tf_op jit(solution)/shard_map/while/body/eval_jaxpr/bhge,lhe->hgbl/dot_general | solution.py:37
  203.7 5.3 %fusion.80 = (f32[2,512]{1,0:T(2,128)S(1)}, f32[1536,512,2]{1,0,2:T(8,128)S(1)}) fusion(f32[2,512]{1,0:T(2,128)S(1)} %get-tuple-element.354, f32[1536,512,2]{1,0,2:T(8,128)} %get-tuple-element.355, pred[512,1536]{0,1:T(8,128)(4,1)} %copy-done.1, bf16[1024,1,2,128]{0,3,2,1:T(8,128)(2,1)} %get-tuple-element.404, s32[]{:T(128)S(6)} %select_n.65, ...), kind=kOutput, calls=%fused_computation.3.clone.1 | convolution fusion | flops 408943616 | bytes 14032908 | tf_op jit(solution)/shard_map/while/body/eval_jaxpr/bhge,lhe->hgbl/dot_general | solution.py:49
  209.0 2.0 fusion.81
  211.0 2.2 convolution_bitcast_fusion.3
  213.2 1.8 fusion.79
  215.4 2.7 fusion.84
  218.0 3.5 fusion.83
  221.6 1.1 copy.128
  223.6 1.4 slice.103
  225.0 1.9 collective-permute-start.1
  226.9 6.7 %collective-permute-done.1 = bf16[2,1024,1,128]{1,3,2,0:T(8,128)(2,1)S(1)} collective-permute-done((bf16[2,1024,1,128]{1,3,2,0:T(8,128)(2,1)S(1)}, bf16[2,1024,1,128]{1,3,2,0:T(8,128)(2,1)S(1)}, u32[]{:S(2)}, u32[]{:S(2)}) %collective-permute-start.1) | collective-permute-done | bytes 524320 | tf_op jit(solution)/shard_map/ppermute | solution.py:17
  233.6 1.4 convert_add_fusion
  236.5 53.4 %all_to_all.21 = bf16[8,1024,2,128]{3,1,2,0:T(8,128)(2,1)S(1)} all-to-all(bf16[8,1024,2,128]{3,1,2,0:T(8,128)(2,1)S(1)} %broadcast_in_dim.90), channel_id=1, replica_groups=mesh['seq'=32,'uly'=8] {'uly'}, dimensions={0} | all-to-all | bytes 8388608 | tf_op jit(solution)/shard_map/all_to_all | solution.py:26
  289.8 1.9 copy-done.11
  291.8 4.3 %convert_bitcast_fusion.1 = bf16[672,2,8,128]{3,0,1,2:T(8,128)(2,1)} fusion(bf16[8,1024,2,128]{3,1,2,0:T(8,128)(2,1)S(1)} %all_to_all.21, bf16[1024,672]{0,1:T(8,128)(2,1)S(1)} %copy-done), kind=kOutput, calls=%fused_computation.51 | convolution fusion | flops 2819948544 | bytes 8323072 | tf_op jit(solution)/shard_map/tf,htkc->fkhc/dot_general | solution.py:145
  296.1 4.6 %copy.94 = bf16[672,2,8,128]{0,3,2,1:T(8,128)(2,1)} copy(bf16[672,2,8,128]{3,0,1,2:T(8,128)(2,1)} %convert_bitcast_fusion.1) | data formatting | bytes 5505024 | tf_op jit(solution)/shard_map/convert_element_type | solution.py:147
  300.7 3.9 copy.95
  304.6 10.5 %all-to-all-start.3 = ((bf16[32,672,2,32]{1,3,2,0:T(8,128)(2,1)}), bf16[32,672,2,32]{1,3,2,0:T(8,128)(2,1)}, u32[]{:S(2)}, u32[]{:S(2)}) async-start(bf16[32,672,2,32]{1,3,2,0:T(8,128)(2,1)} %copy.95), calls=%async_computation.3 | async-start | bytes 6291456 | tf_op jit(solution)/shard_map/all_to_all | solution.py:26
  315.1 2.5 copy.92
  317.6 3.2 copy.91
  320.8 2.6 copy.93
  323.4 1.4 copy.120
  324.8 1.5 multiply_reduce_fusion
  328.5 7.3 %bitcast_convert_fusion = bf16[1024,672]{0,1:T(8,128)(2,1)} fusion(bf16[8,1024,2,128]{3,1,2,0:T(8,128)(2,1)} %copy-done.11, bf16[672,2,8,128]{0,3,2,1:T(8,128)(2,1)} %bitcast.245), kind=kOutput, calls=%fused_computation.50 | convolution fusion | flops 2819260416 | bytes 8323072 | tf_op jit(solution)/shard_map/htkc,fkhc->tf/dot_general | solution.py:142
  335.8 52.4 %all-to-all-done.3 = bf16[32,672,2,32]{1,3,2,0:T(8,128)(2,1)} async-done(((bf16[32,672,2,32]{1,3,2,0:T(8,128)(2,1)}), bf16[32,672,2,32]{1,3,2,0:T(8,128)(2,1)}, u32[]{:S(2)}, u32[]{:S(2)}) %all-to-all-start.3) | async-done | bytes 2752544 | tf_op jit(solution)/shard_map/all_to_all | solution.py:26
  388.3 2.4 convert_reduce_fusion.1
  (126 shorter events, 14.0 us)
Async XLA Ops:
  0.6 87.9 %copy-start = (bf16[1024,672]{0,1:T(8,128)(2,1)S(1)}, bf16[1024,672]{0,1:T(8,128)(2,1)}, u32[]{:S(2)}) copy-start(bf16[1024,672]{0,1:T(8,128)(2,1)} %param.14) | copy-start | bytes 4128772
  86.8 1.7 copy-start.12
  94.6 4.9 %copy-start.13 = (bf16[1024,256]{1,0:T(8,128)(2,1)S(1)}, bf16[1024,256]{1,0:T(8,128)(2,1)}, u32[]{:S(2)}) copy-start(bf16[1024,256]{1,0:T(8,128)(2,1)} %param.15) | copy-start | bytes 1572868
  94.6 54.0 %all-to-all-start.1 = ((bf16[8,1024,2,128]{1,3,2,0:T(8,128)(2,1)}), bf16[8,1024,2,128]{1,3,2,0:T(8,128)(2,1)}, u32[]{:S(2)}, u32[]{:S(2)}) async-start(bf16[8,1024,2,128]{1,3,2,0:T(8,128)(2,1)} %copy.83), calls=%async_computation.1 | async-start | bytes 8388608 | tf_op jit(solution)/shard_map/all_to_all | solution.py:26
  99.7 56.8 %copy-start.9 = (bf16[1024,256]{0,1:T(8,128)(2,1)}, bf16[1024,256]{0,1:T(8,128)(2,1)S(1)}, u32[]{:S(2)}) copy-start(bf16[1024,256]{0,1:T(8,128)(2,1)S(1)} %copy.80) | copy-start | bytes 1572868
  99.9 51.9 %copy-start.7 = (f32[1024,256]{0,1:T(8,128)}, f32[1024,256]{0,1:T(8,128)S(1)}, u32[]{:S(2)}) copy-start(f32[1024,256]{0,1:T(8,128)S(1)} %convert_element_type.91) | copy-start | bytes 3145732
  100.0 56.6 %copy-start.20 = (f32[1024,2]{0,1:T(2,128)}, f32[1024,2]{0,1:T(2,128)S(1)}, u32[]{:S(2)}) copy-start(f32[1024,2]{0,1:T(2,128)S(1)} %multiply_reduce_fusion.1) | copy-start | bytes 24580
  100.0 52.8 %copy-start.26 = (f32[128]{0:T(128)S(1)}, f32[128]{0:T(128)}, u32[]{:S(2)}) copy-start(f32[128]{0:T(128)} %param.19) | copy-start | bytes 1540
  100.0 55.5 %copy-start.14 = (bf16[1024,256]{1,0:T(8,128)(2,1)S(1)}, bf16[1024,256]{1,0:T(8,128)(2,1)}, u32[]{:S(2)}) copy-start(bf16[1024,256]{1,0:T(8,128)(2,1)} %param.21) | copy-start | bytes 1572868
  148.6 6.9 %copy-start.17 = (s32[32768]{0:T(1024)S(1)}, s32[32768]{0:T(1024)}, u32[]{:S(2)}) copy-start(s32[32768]{0:T(1024)} %param.20) | copy-start | bytes 393220
  151.8 1.0 copy-start.5
  151.8 4.8 %copy-start.28 = (f32[128]{0:T(128)S(1)}, f32[128]{0:T(128)}, u32[]{:S(2)}) copy-start(f32[128]{0:T(128)} %param.18) | copy-start | bytes 1540
  151.9 1.1 copy-start.24
  152.8 0.6 copy-start.22
  153.4 10.6 %collective-permute-start = (bf16[2,1024,1,128]{1,3,2,0:T(8,128)(2,1)S(1)}, bf16[2,1024,1,128]{1,3,2,0:T(8,128)(2,1)}, u32[]{:S(2)}, u32[]{:S(2)}) collective-permute-start(bf16[2,1024,1,128]{1,3,2,0:T(8,128)(2,1)S(1)} %pad_maximum_fusion), channel_id=1, source_target_pairs={{0,8},{8,16},{16,24},{24,32},{32,40},{40,48},{48,56},{56,64},{64,7... | collective-permute-start | bytes 1572872 | tf_op jit(solution)/shard_map/ppermute | solution.py:17
  155.5 12.2 %dynamic-slice-start = ((s32[32768]{0:T(1024)}, s32[]{:T(128)}), s32[1024]{0:T(1024)S(1)}, s32[]{:S(2)}) async-start(s32[32768]{0:T(1024)} %param.20, s32[]{:T(128)} %select_n.34), calls=%async_computation.6 | async-start | bytes 8704 | tf_op jit(solution)/shard_map/dynamic_slice | solution.py:95
  156.6 11.2 %copy-start.18 = (f32[1024,2]{0,1:T(2,128)}, f32[1024,2]{0,1:T(2,128)S(1)}, u32[]{:S(2)}) copy-start(f32[1024,2]{0,1:T(2,128)S(1)} %fusion.52) | copy-start | bytes 24580
  170.3 5.5 %copy-start.1 = (pred[512,1536]{0,1:T(8,128)(4,1)}, pred[512,1536]{0,1:T(8,128)(4,1)S(1)}, u32[]{:S(2)}) copy-start(pred[512,1536]{0,1:T(8,128)(4,1)S(1)} %compare_and_fusion.2) | copy-start | bytes 2359300 | tf_op jit(solution)/shard_map/while
  175.8 5.3 %slice-start = ((s8[6291456]{0:T(1024)(128)(4,1)}), s8[2097152]{0:T(1024)(128)(4,1)S(1)}, s32[]{:S(2)}) async-start(s8[6291456]{0:T(1024)(128)(4,1)} %bitcast.235), calls=%async_computation.4 | async-start | bytes 4194304 | tf_op jit(solution)/shard_map/while
  175.8 5.3 %slice-start.1 = ((s8[6291456]{0:T(1024)(128)(4,1)}), s8[4194304]{0:T(1024)(128)(4,1)S(1)}, s32[]{:S(2)}) async-start(s8[6291456]{0:T(1024)(128)(4,1)} %bitcast.235), calls=%async_computation.5 | async-start | bytes 8388608 | tf_op jit(solution)/shard_map/while
  175.8 5.3 %copy-start.2 = (pred[512,1536]{0,1:T(8,128)(4,1)S(1)}, pred[512,1536]{0,1:T(8,128)(4,1)}, u32[]{:S(2)}) copy-start(pred[512,1536]{0,1:T(8,128)(4,1)} %copy-done.1) | copy-start | bytes 2359300 | tf_op jit(solution)/shard_map/while
  183.1 2.2 copy-start.15
  185.3 1.8 copy-start.3
  187.4 2.7 copy-start.4
  198.2 5.5 %copy-start.1 = (pred[512,1536]{0,1:T(8,128)(4,1)}, pred[512,1536]{0,1:T(8,128)(4,1)S(1)}, u32[]{:S(2)}) copy-start(pred[512,1536]{0,1:T(8,128)(4,1)S(1)} %compare_and_fusion.2) | copy-start | bytes 2359300 | tf_op jit(solution)/shard_map/while
  203.7 5.3 %slice-start = ((s8[6291456]{0:T(1024)(128)(4,1)}), s8[2097152]{0:T(1024)(128)(4,1)S(1)}, s32[]{:S(2)}) async-start(s8[6291456]{0:T(1024)(128)(4,1)} %bitcast.235), calls=%async_computation.4 | async-start | bytes 4194304 | tf_op jit(solution)/shard_map/while
  203.7 5.3 %slice-start.1 = ((s8[6291456]{0:T(1024)(128)(4,1)}), s8[4194304]{0:T(1024)(128)(4,1)S(1)}, s32[]{:S(2)}) async-start(s8[6291456]{0:T(1024)(128)(4,1)} %bitcast.235), calls=%async_computation.5 | async-start | bytes 8388608 | tf_op jit(solution)/shard_map/while
  203.7 5.3 %copy-start.2 = (pred[512,1536]{0,1:T(8,128)(4,1)S(1)}, pred[512,1536]{0,1:T(8,128)(4,1)}, u32[]{:S(2)}) copy-start(pred[512,1536]{0,1:T(8,128)(4,1)} %copy-done.1) | copy-start | bytes 2359300 | tf_op jit(solution)/shard_map/while
  211.0 2.2 copy-start.15
  213.2 1.8 copy-start.3
  215.3 2.7 copy-start.4
  223.6 11.4 %copy-start.6 = (f32[1024,2,128]{0,2,1:T(8,128)S(1)}, f32[1024,2,128]{0,2,1:T(8,128)}, u32[]{:S(2)}) copy-start(f32[1024,2,128]{0,2,1:T(8,128)} %copy-done.5) | copy-start | bytes 3145732
  223.6 11.4 %copy-start.27 = (f32[128]{0:T(128)S(1)}, f32[128]{0:T(128)}, u32[]{:S(2)}) copy-start(f32[128]{0:T(128)} %param.19) | copy-start | bytes 1540
  223.6 11.6 %copy-start.25 = (f32[1024]{0:T(1024)S(1)}, f32[1024]{0:T(1024)}, u32[]{:S(2)}) copy-start(f32[1024]{0:T(1024)} %copy-done.24) | copy-start | bytes 12292
  223.6 11.6 %copy-start.23 = (f32[1024]{0:T(1024)S(1)}, f32[1024]{0:T(1024)}, u32[]{:S(2)}) copy-start(f32[1024]{0:T(1024)} %copy-done.22) | copy-start | bytes 12292
  225.0 8.6 %collective-permute-start.1 = (bf16[2,1024,1,128]{1,3,2,0:T(8,128)(2,1)S(1)}, bf16[2,1024,1,128]{1,3,2,0:T(8,128)(2,1)S(1)}, u32[]{:S(2)}, u32[]{:S(2)}) collective-permute-start(bf16[2,1024,1,128]{1,3,2,0:T(8,128)(2,1)S(1)} %slice.103), channel_id=1, source_target_pairs={{8,0},{16,8},{24,16},{32,24},{40,32},{48,40},{56,48},{64,56},{72,6... | collective-permute-start | bytes 1572872 | tf_op jit(solution)/shard_map/ppermute | solution.py:17
  289.8 1.9 copy-start.11
  304.6 10.5 %copy-start.29 = (f32[128]{0:T(128)S(1)}, f32[128]{0:T(128)}, u32[]{:S(2)}) copy-start(f32[128]{0:T(128)} %param.18) | copy-start | bytes 1540
  304.6 83.7 %all-to-all-start.3 = ((bf16[32,672,2,32]{1,3,2,0:T(8,128)(2,1)}), bf16[32,672,2,32]{1,3,2,0:T(8,128)(2,1)}, u32[]{:S(2)}, u32[]{:S(2)}) async-start(bf16[32,672,2,32]{1,3,2,0:T(8,128)(2,1)} %copy.95), calls=%async_computation.3 | async-start | bytes 6291456 | tf_op jit(solution)/shard_map/all_to_all | solution.py:26
  317.6 7.2 %copy-start.8 = (f32[1024,256]{0,1:T(8,128)S(1)}, f32[1024,256]{0,1:T(8,128)}, u32[]{:S(2)}) copy-start(f32[1024,256]{0,1:T(8,128)} %copy-done.7) | copy-start | bytes 3145732
  320.8 5.5 %copy-start.21 = (f32[1024,2]{0,1:T(2,128)S(1)}, f32[1024,2]{0,1:T(2,128)}, u32[]{:S(2)}) copy-start(f32[1024,2]{0,1:T(2,128)} %copy-done.20) | copy-start | bytes 24580
  320.8 5.6 %copy-start.10 = (bf16[1024,256]{0,1:T(8,128)(2,1)S(1)}, bf16[1024,256]{0,1:T(8,128)(2,1)}, u32[]{:S(2)}) copy-start(bf16[1024,256]{0,1:T(8,128)(2,1)} %copy-done.9) | copy-start | bytes 1572868
  320.8 5.6 %copy-start.19 = (f32[1024,2]{0,1:T(2,128)S(1)}, f32[1024,2]{0,1:T(2,128)}, u32[]{:S(2)}) copy-start(f32[1024,2]{0,1:T(2,128)} %copy-done.18) | copy-start | bytes 24580
  324.8 2.8 copy-start.16

commit v2 on v1

--- a/solution.py
+++ b/solution.py
@@ -29,6 +29,28 @@
 def gather_all(block, axis):
     count = lax.axis_size(axis)
     return exchange(jnp.broadcast_to(block[None], (count,) + block.shape), axis)
+
+
+SEQ = ("chip", "core")
+SWAP = [(0, 1), (1, 0)]
+
+
+def gather_seq(block):
+    mine = gather_all(block, "chip")
+    other = lax.ppermute(mine, "core", SWAP)
+    first = lax.axis_index("core") == 0
+    pair = jnp.where(first, jnp.stack([mine, other], 1), jnp.stack([other, mine], 1))
+    return pair.reshape((-1,) + block.shape)
+
+
+def reduce_seq(blocks):
+    chips = blocks.shape[0] // 2
+    split = blocks.reshape((chips, 2) + blocks.shape[1:])
+    core = lax.axis_index("core")
+    keep = jnp.take(split, core, axis=1)
+    send = jnp.take(split, 1 - core, axis=1)
+    pair = (keep.astype(jnp.float32) + lax.ppermute(send, "core", SWAP).astype(jnp.float32))
+    return jnp.sum(exchange(pair.astype(jnp.bfloat16), "chip").astype(jnp.float32), axis=0)
 
 
 def attend_block(
@@ -61,13 +83,13 @@
     rows_here = normed.shape[0]
     feats = normed.shape[1]
     heads_here = q_raw.shape[1] // (2 * HD)
-    n_seq = lax.axis_size("seq")
+    n_seq = lax.axis_size(SEQ)
     n_uly = lax.axis_size("uly")
     col_block = key_weight.shape[1]
-    seq_index = lax.axis_index("seq")
+    seq_index = lax.axis_index(SEQ)
     base_row = seq_index * rows_here
     pair_local = jnp.stack([key_weight, value_weight], axis=1)
-    gathered = gather_all(pair_local, "seq")
+    gathered = gather_seq(pair_local)
     weight_all = gathered.transpose(1, 2, 0, 3).reshape(feats, 2, n_uly, heads_here * HD)
     terms = jnp.einsum(
         "tf,fkhc->htkc", normed, weight_all, preferred_element_type=jnp.float32
@@ -85,7 +107,7 @@
     stacked = jnp.stack([keys_bf, values_bf])
     pieces = []
     distance = 1
-    pieces.append(from_behind(stacked, "seq", distance))
+    pieces.append(from_behind(stacked, SEQ, distance))
     pieces.append(stacked)
     extended = jnp.concatenate(pieces, axis=1)
     block_rows = min(512, rows_here)
@@ -131,7 +153,7 @@
     first_row = max(0, distance * rows_here - WINDOW)
     piece_rows = rows_here - first_row
     outgoing = grad_acc[:, offset_row : offset_row + piece_rows]
-    returned = from_behind(outgoing.astype(jnp.bfloat16), "seq", -distance).astype(outgoing.dtype)
+    returned = from_behind(outgoing.astype(jnp.bfloat16), SEQ, -distance).astype(outgoing.dtype)
     own_grads = own_grads.at[:, first_row:].add(returned)
     _, pull_query = jax.vjp(lambda raw_vals: normalize(raw_vals, q_gain, query_scale), query_in)
     grad_q = pull_query(dquery)[0].astype(jnp.bfloat16).reshape(rows_here, 2 * heads_here * HD)
@@ -146,32 +168,34 @@
         "tf,htkc->fkhc", normed, grads_all, preferred_element_type=jnp.float32
     ).astype(jnp.bfloat16)
     to_owner = weight_part.reshape(feats, 2, n_seq, col_block).transpose(2, 0, 1, 3)
-    summed = jnp.sum(exchange(to_owner, "seq").astype(jnp.float32), axis=0)
+    summed = reduce_seq(to_owner)
     grad_key_weight = summed[:, 0]
     grad_value_weight = summed[:, 1]
     return (attention, grad_normed, grad_q, grad_key_weight, grad_value_weight)
 
 
 def solution(mesh):
+    n_seq, n_uly = mesh.shape["seq"], mesh.shape["uly"]
+    fine = jax.sharding.Mesh(mesh.devices.reshape(n_seq // 2, 2, n_uly), ("chip", "core", "uly"))
     return jax.shard_map(
         body,
-        mesh=mesh,
+        mesh=fine,
         in_specs=(
-            P("seq", "uly"),
-            P("seq", "uly"),
-            P("uly", "seq"),
-            P("uly", "seq"),
+            P(SEQ, "uly"),
+            P(SEQ, "uly"),
+            P("uly", SEQ),
+            P("uly", SEQ),
             P(),
             P(),
             P(),
-            P("seq", "uly"),
+            P(SEQ, "uly"),
         ),
         out_specs=(
-            P("seq", "uly"),
-            P("seq", "uly"),
-            P("seq", "uly"),
-            P("uly", "seq"),
-            P("uly", "seq"),
+            P(SEQ, "uly"),
+            P(SEQ, "uly"),
+            P(SEQ, "uly"),
+            P("uly", SEQ),
+            P("uly", SEQ),
         ),
         check_vma=False,
     )

time: 394 us -> 339 us (0.86)
  blocking collectives: 138 us -> 48.3 us
  waiting for transfers between devices: 114 us -> 140 us
  other arithmetic: 20.3 us -> 26.3 us
    all_to_all x2 -> x1, blocking collectives: 138 us -> 48.3 us  [exchange(): return lax.all_to_all(blocks, axis, 0, 0)]
    all_to_all x2 -> x3, waiting for transfers between devices: 101 us -> 120 us  [exchange(): return lax.all_to_all(blocks, axis, 0, 0)]
    ppermute x0 -> x2, waiting for transfers between devices: none -> 7.04 us  [the longest x1 3.54 us: gather_seq(): other = lax.ppermute(mine, 'core', SWAP)]
    all_to_all x2 -> x3, starting transfers between devices: 15.4 us -> 19.2 us  [exchange(): return lax.all_to_all(blocks, axis, 0, 0)]
    unnamed x55 -> x53, local copies, waits for them, and re-layouts: 9.52 us -> 7.49 us
  transfers between devices with their start and end apart: 4 -> 7, of which waited for: 4 -> 7; matrix products, arithmetic and copies ran while one was open for 6% -> 7% of each run, Pallas kernels for 0% -> 0%
where the time goes in v2:
time: 339 us; the launch traced here: 338 us
  waiting for transfers between devices  140 us (41%)
  matrix products  59 us (17%)
  blocking collectives  48.3 us (14%)
  local copies, waits for them, and re-layouts  38 us (11%)
  other arithmetic  26.3 us (8%)
  starting transfers between devices  23.3 us (7%)
    all_to_all x3, waiting for transfers between devices, exchange(): return lax.all_to_all(blocks, axis, 0, 0)  120 us
    all_to_all x1, blocking collectives, exchange(): return lax.all_to_all(blocks, axis, 0, 0)  48.3 us
    all_to_all x3, starting transfers between devices, exchange(): return lax.all_to_all(blocks, axis, 0, 0)  19.2 us
    ppermute x2, waiting for transfers between devices, from_behind(): return lax.ppermute(array, axis, pairs)  13.1 us
    dot_general x2, matrix products, attend_block(): jnp.einsum('bhge,lhe->hgbl', queries, key_block, preferred_element_type=j...  10.9 us
    dot_general x2, matrix products, attend_block(): jnp.einsum('bhge,lhe->hgbl', grad_block, value_block, preferred_element_t...  10.5 us
    unnamed x53, local copies, waits for them, and re-layouts  7.49 us
    dot_general x1, matrix products, body(): jnp.einsum('htkc,fkhc->tf', grads_all, weight_all, preferred_element_type...  7.3 us
  transfers between devices with their start and end apart: 7, of which 7 were waited for; matrix products, arithmetic and copies ran while one was open for 7% of the time, Pallas kernels for 0%

profile of v2, /device:TPU:2, one launch (start us, length us, event | category | flops | bytes accessed | tf_op | source)
XLA Modules:
  0.0 337.9 jit_solution(12215802813795700717)
XLA Ops:
  1.8 48.3 %all_to_all.20 = bf16[16,672,2,32]{1,3,2,0:T(8,128)(2,1)S(1)} all-to-all(bf16[16,672,2,32]{1,3,2,0:T(8,128)(2,1)S(1)} %broadcast_in_dim.97), channel_id=1, replica_groups=mesh['chip'=16,'core'=2,'uly'=8] {'chip'}, dimensions={0} | all-to-all | bytes 2752512 | tf_op jit(solution)/shard_map/all_to_all | solution.py:26
  50.1 3.5 %collective-permute-done = bf16[16,672,2,32]{1,3,2,0:T(8,128)(2,1)} collective-permute-done((bf16[16,672,2,32]{1,3,2,0:T(8,128)(2,1)S(1)}, bf16[16,672,2,32]{1,3,2,0:T(8,128)(2,1)}, u32[]{:S(2)}, u32[]{:S(2)}) %collective-permute-start) | collective-permute-done | bytes 1376288 | tf_op jit(solution)/shard_map/ppermute | solution.py:40
  53.6 2.3 maximum_select_fusion
  56.2 1.6 copy-done.11
  57.8 3.6 %convert_bitcast_fusion = bf16[8,1024,2,128]{1,3,0,2:T(8,128)(2,1)S(1)} fusion(bf16[672,2,8,128]{0,3,2,1:T(8,128)(2,1)S(1)} %bitcast.260, bf16[1024,672]{0,1:T(8,128)(2,1)S(1)} %copy-done), kind=kOutput, calls=%fused_computation.46 | convolution fusion | flops 2820669440 | bytes 8323072 | tf_op jit(solution)/shard_map/tf,fkhc->htkc/dot_general | solution.py:94
  61.4 2.5 copy.113
  63.9 7.3 %all-to-all-start.1 = ((bf16[8,1024,2,128]{1,3,2,0:T(8,128)(2,1)}), bf16[8,1024,2,128]{1,3,2,0:T(8,128)(2,1)}, u32[]{:S(2)}, u32[]{:S(2)}) async-start(bf16[8,1024,2,128]{1,3,2,0:T(8,128)(2,1)} %copy.113), calls=%async_computation.1 | async-start | bytes 8388608 | tf_op jit(solution)/shard_map/all_to_all | solution.py:26
  71.8 49.4 %all-to-all-done.1 = bf16[8,1024,2,128]{1,3,2,0:T(8,128)(2,1)} async-done(((bf16[8,1024,2,128]{1,3,2,0:T(8,128)(2,1)}), bf16[8,1024,2,128]{1,3,2,0:T(8,128)(2,1)}, u32[]{:S(2)}, u32[]{:S(2)}) %all-to-all-start.1) | async-done | bytes 4194336 | tf_op jit(solution)/shard_map/all_to_all | solution.py:26
  121.1 3.2 convert_reduce_fusion
  125.9 2.1 collective-permute-start.1
  130.1 6.4 %collective-permute-done.1 = bf16[2,1024,1,128]{1,3,2,0:T(8,128)(2,1)} collective-permute-done((bf16[2,1024,1,128]{1,3,2,0:T(8,128)(2,1)S(1)}, bf16[2,1024,1,128]{1,3,2,0:T(8,128)(2,1)}, u32[]{:S(2)}, u32[]{:S(2)}) %collective-permute-start.1) | collective-permute-done | bytes 524320 | tf_op jit(solution)/shard_map/ppermute | solution.py:17
  136.5 2.2 maximum_maximum_fusion
  138.7 1.6 broadcast_in_dim.94
  140.3 55.6 %while.20 = (s32[]{:T(128)}, f32[2,2048,1,128]{1,3,2,0:T(8,128)}, bf16[2,512,1,2,128]{4,3,1,0,2:T(2,128)(2,1)}, f32[2,512,1,2,128]{1,4,3,2,0:T(8,128)}, s32[2]{0...) while((s32[]{:T(128)}, f32[2,2048,1,128]{1,3,2,0:T(8,128)}, ...), condition=%wide.region_6.7_spmd, body=%wide.region_3.6_spmd.sunk | while | flops 2447507968 | bytes 113059336 | solution.py:145
  142.8 5.4 %fusion.79 = (f32[2,512]{1,0:T(2,128)S(1)}, f32[1536,512,2]{1,0,2:T(8,128)}) fusion(pred[512,1536]{0,1:T(8,128)(4,1)S(1)} %compare_and_fusion.2, bf16[1024,1,2,128]{0,3,2,1:T(8,128)(2,1)} %get-tuple-element.427, s32[]{:T(128)S(6)} %select_n.105, bf16[2,2048,1,128]{1,3,2,0:T(8,128)(2,1)} %get-tuple-element.431, s32[]{:T(128)S(6)} %select_n.104), kind=kOutput, calls=%fused_computation.7.clone.1 | convolution fusion | flops 405797888 | bytes 7737352 | tf_op jit(solution)/shard_map/while/body/eval_jaxpr/bhge,lhe->hgbl/dot_general | solution.py:59
  148.2 5.3 %fusion.81 = (f32[2,512]{1,0:T(2,128)S(1)}, f32[1536,512,2]{1,0,2:T(8,128)S(1)}) fusion(f32[2,512]{1,0:T(2,128)S(1)} %get-tuple-element.382, f32[1536,512,2]{1,0,2:T(8,128)} %get-tuple-element.383, pred[512,1536]{0,1:T(8,128)(4,1)} %copy-done.1, bf16[1024,1,2,128]{0,3,2,1:T(8,128)(2,1)} %get-tuple-element.432, s32[]{:T(128)S(6)} %select_n.105, ...), kind=kOutput, calls=%fused_computation.3.clone.1 | convolution fusion | flops 408943616 | bytes 14032908 | tf_op jit(solution)/shard_map/while/body/eval_jaxpr/bhge,lhe->hgbl/dot_general | solution.py:71
  153.5 2.0 fusion.82
  155.6 2.2 convolution_bitcast_fusion.3
  157.7 1.8 fusion.80
  159.9 2.7 fusion.85
  162.6 3.5 %fusion.84 = bf16[1,512,1,2,128]{1,4,3,2,0:T(8,128)(2,1)} fusion(bf16[2,2048,1,128]{1,3,2,0:T(8,128)(2,1)} %get-tuple-element.431, s32[]{:T(128)S(6)} %add.200, s32[]{:T(128)S(6)} %select_n.104, f32[2,512]{1,0:T(2,128)S(1)} %get-tuple-element.382, f32[1536,512,2]{1,0,2:T(8,128)S(1)} %bitcast.249, pred[512,1536]{0,1:T(8,128)(4,1)S(1)} %copy-done.2), kind=kOutput, calls=%fused_computation.22.clone.1 | convolution fusion | flops 407502848 | bytes 7737352 | tf_op jit(solution)/shard_map/while/body/eval_jaxpr/hgbl,lhe->bhge/dot_general | solution.py:68
  170.6 5.4 %fusion.79 = (f32[2,512]{1,0:T(2,128)S(1)}, f32[1536,512,2]{1,0,2:T(8,128)}) fusion(pred[512,1536]{0,1:T(8,128)(4,1)S(1)} %compare_and_fusion.2, bf16[1024,1,2,128]{0,3,2,1:T(8,128)(2,1)} %get-tuple-element.427, s32[]{:T(128)S(6)} %select_n.105, bf16[2,2048,1,128]{1,3,2,0:T(8,128)(2,1)} %get-tuple-element.431, s32[]{:T(128)S(6)} %select_n.104), kind=kOutput, calls=%fused_computation.7.clone.1 | convolution fusion | flops 405797888 | bytes 7737352 | tf_op jit(solution)/shard_map/while/body/eval_jaxpr/bhge,lhe->hgbl/dot_general | solution.py:59
  176.0 5.3 %fusion.81 = (f32[2,512]{1,0:T(2,128)S(1)}, f32[1536,512,2]{1,0,2:T(8,128)S(1)}) fusion(f32[2,512]{1,0:T(2,128)S(1)} %get-tuple-element.382, f32[1536,512,2]{1,0,2:T(8,128)} %get-tuple-element.383, pred[512,1536]{0,1:T(8,128)(4,1)} %copy-done.1, bf16[1024,1,2,128]{0,3,2,1:T(8,128)(2,1)} %get-tuple-element.432, s32[]{:T(128)S(6)} %select_n.105, ...), kind=kOutput, calls=%fused_computation.3.clone.1 | convolution fusion | flops 408943616 | bytes 14032908 | tf_op jit(solution)/shard_map/while/body/eval_jaxpr/bhge,lhe->hgbl/dot_general | solution.py:71
  181.3 2.0 fusion.82
  183.4 2.2 convolution_bitcast_fusion.3
  185.5 1.8 fusion.80
  187.7 2.7 fusion.85
  190.4 3.5 %fusion.84 = bf16[1,512,1,2,128]{1,4,3,2,0:T(8,128)(2,1)} fusion(bf16[2,2048,1,128]{1,3,2,0:T(8,128)(2,1)} %get-tuple-element.431, s32[]{:T(128)S(6)} %add.200, s32[]{:T(128)S(6)} %select_n.104, f32[2,512]{1,0:T(2,128)S(1)} %get-tuple-element.382, f32[1536,512,2]{1,0,2:T(8,128)S(1)} %bitcast.249, pred[512,1536]{0,1:T(8,128)(4,1)S(1)} %copy-done.2), kind=kOutput, calls=%fused_computation.22.clone.1 | convolution fusion | flops 407502848 | bytes 7737352 | tf_op jit(solution)/shard_map/while/body/eval_jaxpr/hgbl,lhe->bhge/dot_general | solution.py:68
  195.9 1.4 slice.116
  197.3 1.9 collective-permute-start.2
  199.2 6.7 %collective-permute-done.2 = bf16[2,1024,1,128]{1,3,2,0:T(8,128)(2,1)S(1)} collective-permute-done((bf16[2,1024,1,128]{1,3,2,0:T(8,128)(2,1)S(1)}, bf16[2,1024,1,128]{1,3,2,0:T(8,128)(2,1)S(1)}, u32[]{:S(2)}, u32[]{:S(2)}) %collective-permute-start.2) | collective-permute-done | bytes 524320 | tf_op jit(solution)/shard_map/ppermute | solution.py:17
  208.0 2.9 broadcast_in_dim.99
  210.9 4.8 %all-to-all-start.2 = ((bf16[8,1024,2,128]{3,1,2,0:T(8,128)(2,1)}), bf16[8,1024,2,128]{3,1,2,0:T(8,128)(2,1)}, u32[]{:S(2)}, u32[]{:S(2)}) async-start(bf16[8,1024,2,128]{3,1,2,0:T(8,128)(2,1)} %broadcast_in_dim.99), calls=%async_computation.2 | async-start | bytes 8388608 | tf_op jit(solution)/shard_map/all_to_all | solution.py:26
  215.7 50.6 %all-to-all-done.2 = bf16[8,1024,2,128]{3,1,2,0:T(8,128)(2,1)} async-done(((bf16[8,1024,2,128]{3,1,2,0:T(8,128)(2,1)}), bf16[8,1024,2,128]{3,1,2,0:T(8,128)(2,1)}, u32[]{:S(2)}, u32[]{:S(2)}) %all-to-all-start.2) | async-done | bytes 4194336 | tf_op jit(solution)/shard_map/all_to_all | solution.py:26
  266.3 6.5 %convert_bitcast_fusion.1 = bf16[672,2,8,128]{3,0,1,2:T(8,128)(2,1)} fusion(bf16[8,1024,2,128]{3,1,2,0:T(8,128)(2,1)} %all-to-all-done.2, bf16[1024,672]{0,1:T(8,128)(2,1)S(1)} %copy-done), kind=kOutput, calls=%fused_computation.53 | convolution fusion | flops 2819948544 | bytes 8323072 | tf_op jit(solution)/shard_map/tf,htkc->fkhc/dot_general | solution.py:167
  272.7 4.6 %copy.124 = bf16[672,2,8,128]{0,3,2,1:T(8,128)(2,1)} copy(bf16[672,2,8,128]{3,0,1,2:T(8,128)(2,1)} %convert_bitcast_fusion.1) | data formatting | bytes 5505024 | tf_op jit(solution)/shard_map/convert_element_type | solution.py:169
  277.3 2.2 copy.125
  280.9 3.5 %collective-permute-done.3 = bf16[16,672,2,32]{1,3,2,0:T(8,128)(2,1)S(1)} collective-permute-done((bf16[16,672,2,32]{1,3,2,0:T(8,128)(2,1)}, bf16[16,672,2,32]{1,3,2,0:T(8,128)(2,1)S(1)}, u32[]{:S(2)}, u32[]{:S(2)}) %collective-permute-start.3) | collective-permute-done | bytes 1376288 | tf_op jit(solution)/shard_map/ppermute | solution.py:52
  284.5 3.2 add_convert_fusion
  287.6 7.1 %all-to-all-start.3 = ((bf16[16,672,2,32]{1,3,2,0:T(8,128)(2,1)}), bf16[16,672,2,32]{1,3,2,0:T(8,128)(2,1)}, u32[]{:S(2)}, u32[]{:S(2)}) async-start(bf16[16,672,2,32]{1,3,2,0:T(8,128)(2,1)} %add_convert_fusion), calls=%async_computation.3 | async-start | bytes 3145728 | tf_op jit(solution)/shard_map/all_to_all | solution.py:26
  294.7 2.5 copy.122
  297.2 3.2 copy.121
  300.4 2.6 copy.123
  303.0 1.4 copy.153
  304.4 1.5 multiply_reduce_fusion
  308.1 7.3 %bitcast_convert_fusion = bf16[1024,672]{0,1:T(8,128)(2,1)} fusion(bf16[8,1024,2,128]{3,1,2,0:T(8,128)(2,1)} %all-to-all-done.2, bf16[672,2,8,128]{0,3,2,1:T(8,128)(2,1)} %bitcast.261), kind=kOutput, calls=%fused_computation.52 | convolution fusion | flops 2819260416 | bytes 8323072 | tf_op jit(solution)/shard_map/htkc,fkhc->tf/dot_general | solution.py:164
  315.4 20.1 %all-to-all-done.3 = bf16[16,672,2,32]{1,3,2,0:T(8,128)(2,1)} async-done(((bf16[16,672,2,32]{1,3,2,0:T(8,128)(2,1)}), bf16[16,672,2,32]{1,3,2,0:T(8,128)(2,1)}, u32[]{:S(2)}, u32[]{:S(2)}) %all-to-all-start.3) | async-done | bytes 1376288 | tf_op jit(solution)/shard_map/all_to_all | solution.py:26
  335.5 1.7 convert_reduce_fusion.1
  (132 shorter events, 20.1 us)
Async XLA Ops:
  0.6 57.2 %copy-start = (bf16[1024,672]{0,1:T(8,128)(2,1)S(1)}, bf16[1024,672]{0,1:T(8,128)(2,1)}, u32[]{:S(2)}) copy-start(bf16[1024,672]{0,1:T(8,128)(2,1)} %param.16) | copy-start | bytes 4128772
  50.1 3.5 %collective-permute-start = (bf16[16,672,2,32]{1,3,2,0:T(8,128)(2,1)S(1)}, bf16[16,672,2,32]{1,3,2,0:T(8,128)(2,1)}, u32[]{:S(2)}, u32[]{:S(2)}) collective-permute-start(bf16[16,672,2,32]{1,3,2,0:T(8,128)(2,1)S(1)} %all_to_all.20), channel_id=1, source_target_pairs={{0,8},{8,0},{1,9},{9,1},{2,10},{10,2},{3,11},{11,3},{4,12},{12,4},... | collective-permute-start | bytes 4128776 | tf_op jit(solution)/shard_map/ppermute | solution.py:40
  56.2 1.6 copy-start.11
  63.9 7.3 %copy-start.12 = (bf16[1024,256]{1,0:T(8,128)(2,1)S(1)}, bf16[1024,256]{1,0:T(8,128)(2,1)}, u32[]{:S(2)}) copy-start(bf16[1024,256]{1,0:T(8,128)(2,1)} %param.17) | copy-start | bytes 1572868
  63.9 57.2 %all-to-all-start.1 = ((bf16[8,1024,2,128]{1,3,2,0:T(8,128)(2,1)}), bf16[8,1024,2,128]{1,3,2,0:T(8,128)(2,1)}, u32[]{:S(2)}, u32[]{:S(2)}) async-start(bf16[8,1024,2,128]{1,3,2,0:T(8,128)(2,1)} %copy.113), calls=%async_computation.1 | async-start | bytes 8388608 | tf_op jit(solution)/shard_map/all_to_all | solution.py:26
  71.5 57.6 %copy-start.9 = (bf16[1024,256]{0,1:T(8,128)(2,1)}, bf16[1024,256]{0,1:T(8,128)(2,1)S(1)}, u32[]{:S(2)}) copy-start(bf16[1024,256]{0,1:T(8,128)(2,1)S(1)} %copy.110) | copy-start | bytes 1572868
  71.6 52.7 %copy-start.7 = (f32[1024,256]{0,1:T(8,128)}, f32[1024,256]{0,1:T(8,128)S(1)}, u32[]{:S(2)}) copy-start(f32[1024,256]{0,1:T(8,128)S(1)} %convert_element_type.100) | copy-start | bytes 3145732
  71.7 57.3 %copy-start.19 = (f32[1024,2]{0,1:T(2,128)}, f32[1024,2]{0,1:T(2,128)S(1)}, u32[]{:S(2)}) copy-start(f32[1024,2]{0,1:T(2,128)S(1)} %multiply_reduce_fusion.1) | copy-start | bytes 24580
  71.7 53.6 %copy-start.25 = (f32[128]{0:T(128)S(1)}, f32[128]{0:T(128)}, u32[]{:S(2)}) copy-start(f32[128]{0:T(128)} %param.21) | copy-start | bytes 1540
  71.8 56.3 %copy-start.13 = (bf16[1024,256]{1,0:T(8,128)(2,1)S(1)}, bf16[1024,256]{1,0:T(8,128)(2,1)}, u32[]{:S(2)}) copy-start(bf16[1024,256]{1,0:T(8,128)(2,1)} %param.23) | copy-start | bytes 1572868
  121.1 6.9 %copy-start.16 = (s32[32768]{0:T(1024)S(1)}, s32[32768]{0:T(1024)}, u32[]{:S(2)}) copy-start(s32[32768]{0:T(1024)} %param.22) | copy-start | bytes 393220
  124.3 1.0 copy-start.5
  124.3 4.8 %copy-start.27 = (f32[128]{0:T(128)S(1)}, f32[128]{0:T(128)}, u32[]{:S(2)}) copy-start(f32[128]{0:T(128)} %param.20) | copy-start | bytes 1540
  124.4 1.1 copy-start.23
  125.3 0.6 copy-start.21
  125.9 10.6 %collective-permute-start.1 = (bf16[2,1024,1,128]{1,3,2,0:T(8,128)(2,1)S(1)}, bf16[2,1024,1,128]{1,3,2,0:T(8,128)(2,1)}, u32[]{:S(2)}, u32[]{:S(2)}) collective-permute-start(bf16[2,1024,1,128]{1,3,2,0:T(8,128)(2,1)S(1)} %pad_maximum_fusion), channel_id=1, source_target_pairs={{0,8},{8,16},{16,24},{24,32},{32,40},{40,48},{48,56},{56,64},{64,7... | collective-permute-start | bytes 1572872 | tf_op jit(solution)/shard_map/ppermute | solution.py:17
  128.1 12.2 %dynamic-slice-start = ((s32[32768]{0:T(1024)}, s32[]{:T(128)}), s32[1024]{0:T(1024)S(1)}, s32[]{:S(2)}) async-start(s32[32768]{0:T(1024)} %param.22, s32[]{:T(128)} %select_n.53), calls=%async_computation.6 | async-start | bytes 8704 | tf_op jit(solution)/shard_map/dynamic_slice | solution.py:117
  129.1 11.2 %copy-start.17 = (f32[1024,2]{0,1:T(2,128)}, f32[1024,2]{0,1:T(2,128)S(1)}, u32[]{:S(2)}) copy-start(f32[1024,2]{0,1:T(2,128)S(1)} %fusion.53) | copy-start | bytes 24580
  142.8 5.4 %copy-start.1 = (pred[512,1536]{0,1:T(8,128)(4,1)}, pred[512,1536]{0,1:T(8,128)(4,1)S(1)}, u32[]{:S(2)}) copy-start(pred[512,1536]{0,1:T(8,128)(4,1)S(1)} %compare_and_fusion.2) | copy-start | bytes 2359300 | tf_op jit(solution)/shard_map/while
  148.2 5.3 %slice-start = ((s8[6291456]{0:T(1024)(128)(4,1)}), s8[2097152]{0:T(1024)(128)(4,1)S(1)}, s32[]{:S(2)}) async-start(s8[6291456]{0:T(1024)(128)(4,1)} %bitcast.248), calls=%async_computation.4 | async-start | bytes 4194304 | tf_op jit(solution)/shard_map/while
  148.2 5.3 %slice-start.1 = ((s8[6291456]{0:T(1024)(128)(4,1)}), s8[4194304]{0:T(1024)(128)(4,1)S(1)}, s32[]{:S(2)}) async-start(s8[6291456]{0:T(1024)(128)(4,1)} %bitcast.248), calls=%async_computation.5 | async-start | bytes 8388608 | tf_op jit(solution)/shard_map/while
  148.2 5.3 %copy-start.2 = (pred[512,1536]{0,1:T(8,128)(4,1)S(1)}, pred[512,1536]{0,1:T(8,128)(4,1)}, u32[]{:S(2)}) copy-start(pred[512,1536]{0,1:T(8,128)(4,1)} %copy-done.1) | copy-start | bytes 2359300 | tf_op jit(solution)/shard_map/while
  155.5 2.2 copy-start.14
  157.7 1.8 copy-start.3
  159.9 2.7 copy-start.4
  170.6 5.4 %copy-start.1 = (pred[512,1536]{0,1:T(8,128)(4,1)}, pred[512,1536]{0,1:T(8,128)(4,1)S(1)}, u32[]{:S(2)}) copy-start(pred[512,1536]{0,1:T(8,128)(4,1)S(1)} %compare_and_fusion.2) | copy-start | bytes 2359300 | tf_op jit(solution)/shard_map/while
  176.0 5.3 %slice-start = ((s8[6291456]{0:T(1024)(128)(4,1)}), s8[2097152]{0:T(1024)(128)(4,1)S(1)}, s32[]{:S(2)}) async-start(s8[6291456]{0:T(1024)(128)(4,1)} %bitcast.248), calls=%async_computation.4 | async-start | bytes 4194304 | tf_op jit(solution)/shard_map/while
  176.0 5.3 %slice-start.1 = ((s8[6291456]{0:T(1024)(128)(4,1)}), s8[4194304]{0:T(1024)(128)(4,1)S(1)}, s32[]{:S(2)}) async-start(s8[6291456]{0:T(1024)(128)(4,1)} %bitcast.248), calls=%async_computation.5 | async-start | bytes 8388608 | tf_op jit(solution)/shard_map/while
  176.0 5.3 %copy-start.2 = (pred[512,1536]{0,1:T(8,128)(4,1)S(1)}, pred[512,1536]{0,1:T(8,128)(4,1)}, u32[]{:S(2)}) copy-start(pred[512,1536]{0,1:T(8,128)(4,1)} %copy-done.1) | copy-start | bytes 2359300 | tf_op jit(solution)/shard_map/while
  183.3 2.2 copy-start.14
  185.5 1.8 copy-start.3
  187.7 2.7 copy-start.4
  195.9 11.4 %copy-start.6 = (f32[1024,2,128]{0,2,1:T(8,128)S(1)}, f32[1024,2,128]{0,2,1:T(8,128)}, u32[]{:S(2)}) copy-start(f32[1024,2,128]{0,2,1:T(8,128)} %copy-done.5) | copy-start | bytes 3145732
  195.9 11.4 %copy-start.26 = (f32[128]{0:T(128)S(1)}, f32[128]{0:T(128)}, u32[]{:S(2)}) copy-start(f32[128]{0:T(128)} %param.21) | copy-start | bytes 1540
  195.9 11.6 %copy-start.24 = (f32[1024]{0:T(1024)S(1)}, f32[1024]{0:T(1024)}, u32[]{:S(2)}) copy-start(f32[1024]{0:T(1024)} %copy-done.23) | copy-start | bytes 12292
  195.9 11.6 %copy-start.22 = (f32[1024]{0:T(1024)S(1)}, f32[1024]{0:T(1024)}, u32[]{:S(2)}) copy-start(f32[1024]{0:T(1024)} %copy-done.21) | copy-start | bytes 12292
  197.3 8.6 %collective-permute-start.2 = (bf16[2,1024,1,128]{1,3,2,0:T(8,128)(2,1)S(1)}, bf16[2,1024,1,128]{1,3,2,0:T(8,128)(2,1)S(1)}, u32[]{:S(2)}, u32[]{:S(2)}) collective-permute-start(bf16[2,1024,1,128]{1,3,2,0:T(8,128)(2,1)S(1)} %slice.116), channel_id=1, source_target_pairs={{8,0},{16,8},{24,16},{32,24},{40,32},{48,40},{56,48},{64,56},{72,6... | collective-permute-start | bytes 1572872 | tf_op jit(solution)/shard_map/ppermute | solution.py:17
  210.9 55.4 %all-to-all-start.2 = ((bf16[8,1024,2,128]{3,1,2,0:T(8,128)(2,1)}), bf16[8,1024,2,128]{3,1,2,0:T(8,128)(2,1)}, u32[]{:S(2)}, u32[]{:S(2)}) async-start(bf16[8,1024,2,128]{3,1,2,0:T(8,128)(2,1)} %broadcast_in_dim.99), calls=%async_computation.2 | async-start | bytes 8388608 | tf_op jit(solution)/shard_map/all_to_all | solution.py:26
  280.8 3.6 %collective-permute-start.3 = (bf16[16,672,2,32]{1,3,2,0:T(8,128)(2,1)}, bf16[16,672,2,32]{1,3,2,0:T(8,128)(2,1)S(1)}, u32[]{:S(2)}, u32[]{:S(2)}) collective-permute-start(bf16[16,672,2,32]{1,3,2,0:T(8,128)(2,1)} %select_bitcast_fusion), channel_id=1, source_target_pairs={{0,8},{8,0},{1,9},{9,1},{2,10},{10,2},{3,11},{11,3},{4,12},{12,4},... | collective-permute-start | bytes 4128776 | tf_op jit(solution)/shard_map/ppermute | solution.py:52
  284.5 10.2 %copy-start.28 = (f32[128]{0:T(128)S(1)}, f32[128]{0:T(128)}, u32[]{:S(2)}) copy-start(f32[128]{0:T(128)} %param.20) | copy-start | bytes 1540
  287.6 47.9 %all-to-all-start.3 = ((bf16[16,672,2,32]{1,3,2,0:T(8,128)(2,1)}), bf16[16,672,2,32]{1,3,2,0:T(8,128)(2,1)}, u32[]{:S(2)}, u32[]{:S(2)}) async-start(bf16[16,672,2,32]{1,3,2,0:T(8,128)(2,1)} %add_convert_fusion), calls=%async_computation.3 | async-start | bytes 3145728 | tf_op jit(solution)/shard_map/all_to_all | solution.py:26
  297.2 7.2 %copy-start.8 = (f32[1024,256]{0,1:T(8,128)S(1)}, f32[1024,256]{0,1:T(8,128)}, u32[]{:S(2)}) copy-start(f32[1024,256]{0,1:T(8,128)} %copy-done.7) | copy-start | bytes 3145732
  300.4 5.5 %copy-start.20 = (f32[1024,2]{0,1:T(2,128)S(1)}, f32[1024,2]{0,1:T(2,128)}, u32[]{:S(2)}) copy-start(f32[1024,2]{0,1:T(2,128)} %copy-done.19) | copy-start | bytes 24580
  300.4 5.6 %copy-start.10 = (bf16[1024,256]{0,1:T(8,128)(2,1)S(1)}, bf16[1024,256]{0,1:T(8,128)(2,1)}, u32[]{:S(2)}) copy-start(bf16[1024,256]{0,1:T(8,128)(2,1)} %copy-done.9) | copy-start | bytes 1572868
  300.4 5.6 %copy-start.18 = (f32[1024,2]{0,1:T(2,128)S(1)}, f32[1024,2]{0,1:T(2,128)}, u32[]{:S(2)}) copy-start(f32[1024,2]{0,1:T(2,128)} %copy-done.17) | copy-start | bytes 24580
  304.4 2.8 copy-start.15

commit v3 on v2

--- a/solution.py
+++ b/solution.py
@@ -1,6 +1,8 @@
 import jax
 import jax.numpy as jnp
 from jax import lax
+from jax.experimental import pallas as pl
+from jax.experimental.pallas import tpu as pltpu
 from jax.sharding import PartitionSpec as P
 
 HD = 128
@@ -77,6 +79,64 @@
     dkey = jnp.einsum("hgbl,bhge->lhe", dscore, queries, preferred_element_type=jnp.float32)
     dvalue = jnp.einsum("hgbl,bhge->lhe", weights, grad_block, preferred_element_type=jnp.float32)
     return (attended, dquery, dkey, dvalue)
+
+
+def attention_kernel(q_ref, do_ref, k_ref, v_ref, qseg_ref, kseg_ref, out_ref, dq_ref, dkv_ref):
+    rows = q_ref.shape[0]
+    block = 256
+    span = block + WINDOW
+    dkv_ref[...] = jnp.zeros(dkv_ref.shape, jnp.float32)
+    nt = (((1,), (1,)), ((), ()))
+    tn = (((0,), (0,)), ((), ()))
+    for b in range(rows // block):
+        r0 = b * block
+        k = k_ref[pl.ds(r0, span), :]
+        v = v_ref[pl.ds(r0, span), :]
+        row = lax.broadcasted_iota(jnp.int32, (block, span), 0)
+        col = lax.broadcasted_iota(jnp.int32, (block, span), 1)
+        allowed = (col <= row + WINDOW) & (col > row)
+        allowed = allowed & (qseg_ref[pl.ds(r0, block), :] == kseg_ref[:, pl.ds(r0, span)])
+        dk_acc = jnp.zeros((span, HD), jnp.float32)
+        dv_acc = jnp.zeros((span, HD), jnp.float32)
+        for g in range(2):
+            q = q_ref[pl.ds(r0, block), pl.ds(g * HD, HD)]
+            do = do_ref[pl.ds(r0, block), pl.ds(g * HD, HD)]
+            scores = lax.dot_general(q, k, nt, preferred_element_type=jnp.float32)
+            exp_scores = jnp.where(allowed, jnp.exp(scores), 0.0)
+            probs = exp_scores / jnp.sum(exp_scores, axis=1, keepdims=True)
+            weights = probs.astype(jnp.bfloat16)
+            out_ref[pl.ds(r0, block), pl.ds(g * HD, HD)] = jnp.dot(
+                weights, v, preferred_element_type=jnp.float32
+            ).astype(out_ref.dtype)
+            dprob = lax.dot_general(do, v, nt, preferred_element_type=jnp.float32)
+            delta_row = jnp.sum(probs * dprob, axis=1, keepdims=True)
+            dscore = (probs * (dprob - delta_row)).astype(jnp.bfloat16)
+            dq_ref[pl.ds(r0, block), pl.ds(g * HD, HD)] = jnp.dot(
+                dscore, k, preferred_element_type=jnp.float32
+            )
+            dk_acc = dk_acc + lax.dot_general(dscore, q, tn, preferred_element_type=jnp.float32)
+            dv_acc = dv_acc + lax.dot_general(weights, do, tn, preferred_element_type=jnp.float32)
+        dkv_ref[0, pl.ds(r0, span), :] += dk_acc
+        dkv_ref[1, pl.ds(r0, span), :] += dv_acc
+
+
+def attend(queries, grad_out, keys, values, query_seg, key_seg):
+    rows = queries.shape[0]
+    spec = pl.BlockSpec(memory_space=pltpu.VMEM)
+    return pl.pallas_call(
+        attention_kernel,
+        out_shape=(
+            jax.ShapeDtypeStruct((rows, 2 * HD), jnp.bfloat16),
+            jax.ShapeDtypeStruct((rows, 2 * HD), jnp.float32),
+            jax.ShapeDtypeStruct((2, keys.shape[0], HD), jnp.float32),
+        ),
+        in_specs=[spec] * 6,
+        out_specs=(spec, spec, spec),
+        cost_estimate=pl.CostEstimate(
+            flops=12 * rows * (rows + WINDOW) * HD * 2, transcendentals=2 * rows * (rows + WINDOW),
+            bytes_accessed=16 * rows * HD * 4,
+        ),
+    )(queries, grad_out, keys, values, query_seg, key_seg)
 
 
 def body(normed, q_raw, key_weight, value_weight, q_gain, k_gain, segment_ids, grad_out):
@@ -105,48 +165,21 @@
     queries = normalize(query_in, q_gain, query_scale).astype(jnp.bfloat16)
     grad_heads = grad_out.reshape(rows_here, heads_here, 2, HD)
     stacked = jnp.stack([keys_bf, values_bf])
-    pieces = []
-    distance = 1
-    pieces.append(from_behind(stacked, SEQ, distance))
-    pieces.append(stacked)
-    extended = jnp.concatenate(pieces, axis=1)
-    block_rows = min(512, rows_here)
-    span_rows = block_rows + WINDOW
-    count_blocks = rows_here // block_rows
+    behind = from_behind(stacked, SEQ, 1)
+    extended = jnp.concatenate([behind, stacked], axis=1).reshape(2, WINDOW + rows_here, HD)
     seg_pad = jnp.concatenate([jnp.full((WINDOW,), -1, jnp.int32), segment_ids])
-    query_seg_all = lax.dynamic_slice_in_dim(segment_ids, base_row, rows_here, 0)
-    key_seg_all = lax.dynamic_slice_in_dim(seg_pad, base_row, WINDOW + rows_here, 0)
-
-    def step(grad_acc, block_index):
-        begin_row = block_index * block_rows
-        query_pos = base_row + begin_row + jnp.arange(block_rows, dtype=jnp.int32)
-        key_pos = base_row + begin_row - WINDOW + jnp.arange(span_rows, dtype=jnp.int32)
-        key_block = lax.dynamic_slice_in_dim(extended, begin_row, span_rows, 1)
-        attended, dquery, dkey, dvalue = attend_block(
-            lax.dynamic_slice_in_dim(queries, begin_row, block_rows, 0),
-            key_block[0],
-            key_block[1],
-            lax.dynamic_slice_in_dim(grad_heads, begin_row, block_rows, 0),
-            query_pos,
-            key_pos,
-            lax.dynamic_slice_in_dim(query_seg_all, begin_row, block_rows, 0),
-            lax.dynamic_slice_in_dim(key_seg_all, begin_row, span_rows, 0),
-        )
-        update = jnp.stack([dkey, dvalue])
-        grad_acc = lax.dynamic_update_slice_in_dim(
-            grad_acc,
-            lax.dynamic_slice_in_dim(grad_acc, begin_row, span_rows, 1) + update,
-            begin_row,
-            1,
-        )
-        return (grad_acc, (attended, dquery))
-
-    zero_acc = jnp.zeros((2, WINDOW + rows_here, heads_here, HD), jnp.float32)
-    grad_acc, (attended, dquery) = lax.scan(
-        step, zero_acc, jnp.arange(count_blocks, dtype=jnp.int32)
-    )
-    attention = attended.reshape(rows_here, 2 * heads_here * HD)
+    query_seg = lax.dynamic_slice_in_dim(segment_ids, base_row, rows_here, 0)
+    key_seg = lax.dynamic_slice_in_dim(seg_pad, base_row, WINDOW + rows_here, 0)
+    attention, dquery, grad_acc = attend(
+        queries.reshape(rows_here, 2 * HD),
+        grad_out,
+        extended[0],
+        extended[1],
+        query_seg.reshape(rows_here, 1),
+        key_seg.reshape(1, WINDOW + rows_here),
+    )
     dquery = dquery.reshape(rows_here, heads_here, 2, HD)
+    grad_acc = grad_acc.reshape(2, WINDOW + rows_here, heads_here, HD)
     own_grads = grad_acc[:, WINDOW:]
     offset_row = 0
     distance = 1

time: 339 us -> 305 us (0.90)
  matrix products: 59 us -> 16.5 us
  Pallas kernels: 0 us -> 14.9 us
    dot_general x12 -> x0, matrix products: 41.7 us -> none  [the longest x2 10.9 us: attend_block(): jnp.einsum('bhge,lhe->hgbl', queries, key_block, preferred_element_type=j...]
    pallas_call x0 -> x1, Pallas kernels: none -> 14.9 us  [attend(): pl.pallas_call(attention_kernel, out_shape=(jax.ShapeDtypeStruct((rows, 2...]
    ppermute x2, waiting for transfers between devices: 13.1 us -> 6.91 us  [from_behind(): return lax.ppermute(array, axis, pairs)]
    while x30 -> x0, local copies, waits for them, and re-layouts: 5.75 us -> none  [the longest x2 5.7 us: body(): lax.scan(step, zero_acc, jnp.arange(count_blocks, dtype=jnp.int32))]
    dynamic_update_slice x4 -> x0, local copies, waits for them, and re-layouts: 4 us -> none  [body(): lax.scan(step, zero_acc, jnp.arange(count_blocks, dtype=jnp.int32))]
    another operation x2 -> x0, other arithmetic: 3.98 us -> none
    all_to_all x3, waiting for transfers between devices: 120 us -> 124 us  [exchange(): return lax.all_to_all(blocks, axis, 0, 0)]
    unnamed x53 -> x24, local copies, waits for them, and re-layouts: 7.49 us -> 6.49 us
  transfers between devices with their start and end apart: 7 -> 7, of which waited for: 7 -> 7; matrix products, arithmetic and copies ran while one was open for 7% -> 8% of each run, Pallas kernels for 0% -> 0%
where the time goes in v3:
time: 305 us; the launch traced here: 304 us
  waiting for transfers between devices  138 us (45%)
  blocking collectives  48.4 us (16%)
  local copies, waits for them, and re-layouts  35 us (11%)
  other arithmetic  26.4 us (9%)
  starting transfers between devices  23.4 us (8%)
  matrix products  16.5 us (5%)
  Pallas kernels  14.9 us (5%)
    all_to_all x3, waiting for transfers between devices, exchange(): return lax.all_to_all(blocks, axis, 0, 0)  124 us
    all_to_all x1, blocking collectives, exchange(): return lax.all_to_all(blocks, axis, 0, 0)  48.4 us
    all_to_all x3, starting transfers between devices, exchange(): return lax.all_to_all(blocks, axis, 0, 0)  17.9 us
    pallas_call x1, Pallas kernels, attend(): pl.pallas_call(attention_kernel, out_shape=(jax.ShapeDtypeStruct((rows, 2...  14.9 us
    ppermute x2, waiting for transfers between devices, from_behind(): return lax.ppermute(array, axis, pairs)  6.91 us
    dot_general x1, matrix products, body(): jnp.einsum('tf,htkc->fkhc', normed, grads_all, preferred_element_type=jnp...  6.55 us
    unnamed x24, local copies, waits for them, and re-layouts  6.49 us
    dot_general x1, matrix products, body(): jnp.einsum('htkc,fkhc->tf', grads_all, weight_all, preferred_element_type...  6.38 us
  transfers between devices with their start and end apart: 7, of which 7 were waited for; matrix products, arithmetic and copies ran while one was open for 8% of the time, Pallas kernels for 0%

profile of v3, /device:TPU:2, one launch (start us, length us, event | category | flops | bytes accessed | tf_op | source)
XLA Modules:
  0.0 303.7 jit_solution(7285790002500282351)
XLA Ops:
  0.6 0.9 pad_maximum_fusion.2
  1.8 48.4 %all_to_all.20 = bf16[16,672,2,32]{1,3,2,0:T(8,128)(2,1)} all-to-all(bf16[16,672,2,32]{1,3,2,0:T(8,128)(2,1)S(1)} %broadcast_in_dim.16), channel_id=1, replica_groups=mesh['chip'=16,'core'=2,'uly'=8] {'chip'}, dimensions={0} | all-to-all | bytes 2752512 | tf_op jit(solution)/shard_map/all_to_all | solution.py:28
  50.2 3.7 %collective-permute-done = bf16[16,672,2,32]{1,3,2,0:T(8,128)(2,1)} collective-permute-done((bf16[16,672,2,32]{1,3,2,0:T(8,128)(2,1)}, bf16[16,672,2,32]{1,3,2,0:T(8,128)(2,1)}, u32[]{:S(2)}, u32[]{:S(2)}) %collective-permute-start) | collective-permute-done | bytes 1376288 | tf_op jit(solution)/shard_map/ppermute | solution.py:42
  54.0 3.5 %maximum_select_fusion = bf16[16,2,672,2,32]{2,4,3,1,0:T(8,128)(2,1)S(1)} fusion(bf16[16,1,672,2,32]{2,4,3,1,0:T(8,128)(2,1)} %bitcast.4, bf16[16,1,672,2,32]{2,4,3,1,0:T(8,128)(2,1)} %bitcast.3, pred[]{:T(512)S(6)} %eq.3), kind=kLoop, calls=%fused_computation.2 | loop fusion | flops 4128768 | bytes 5505025 | tf_op jit(solution)/shard_map/jit(_where)/select_n | solution.py:44
  57.7 1.7 copy-done.4
  59.5 3.6 %convert_bitcast_fusion = bf16[8,1024,2,128]{1,3,0,2:T(8,128)(2,1)S(1)} fusion(bf16[672,2,8,128]{0,3,2,1:T(8,128)(2,1)S(1)} %bitcast.92, bf16[1024,672]{0,1:T(8,128)(2,1)S(1)} %copy-done), kind=kOutput, calls=%fused_computation.1 | convolution fusion | flops 2820669440 | bytes 8323072 | tf_op jit(solution)/shard_map/tf,fkhc->htkc/dot_general | solution.py:154
  63.1 2.4 copy.60
  65.5 7.3 %all-to-all-start.1 = ((bf16[8,1024,2,128]{1,3,2,0:T(8,128)(2,1)}), bf16[8,1024,2,128]{1,3,2,0:T(8,128)(2,1)}, u32[]{:S(2)}, u32[]{:S(2)}) async-start(bf16[8,1024,2,128]{1,3,2,0:T(8,128)(2,1)} %copy.60), calls=%async_computation.1 | async-start | bytes 8388608 | tf_op jit(solution)/shard_map/all_to_all | solution.py:28
  73.4 1.2 multiply_reduce_fusion.1
  74.7 48.0 %all-to-all-done.1 = bf16[8,1024,2,128]{1,3,2,0:T(8,128)(2,1)} async-done(((bf16[8,1024,2,128]{1,3,2,0:T(8,128)(2,1)}), bf16[8,1024,2,128]{1,3,2,0:T(8,128)(2,1)}, u32[]{:S(2)}, u32[]{:S(2)}) %all-to-all-start.1) | async-done | bytes 4194336 | tf_op jit(solution)/shard_map/all_to_all | solution.py:28
  122.7 3.2 %convert_reduce_fusion = f32[1024,2,128]{0,2,1:T(8,128)S(1)} fusion(bf16[8,1024,2,128]{1,3,2,0:T(8,128)(2,1)} %all-to-all-done.1), kind=kLoop, calls=%fused_computation | loop fusion | flops 3932160 | bytes 5242880 | tf_op jit(solution)/shard_map/reduce_sum | solution.py:158
  125.9 0.7 slice.83
  126.6 0.8 slice.82
  127.5 1.2 copy.79
  128.7 1.8 copy.80
  130.9 0.7 copy-done.7
  131.6 1.8 pad_maximum_fusion
  133.4 1.9 collective-permute-start.1
  135.4 1.3 pad_dynamic-slice_fusion
  137.4 1.0 copy.64.qseg_ref
  138.4 1.0 copy.57
  139.4 2.4 mul.204
  141.8 1.0 copy-done.1
  142.8 1.0 fusion.10.q_ref
  144.2 1.1 maximum_maximum_fusion
  145.4 1.1 slice_bitcast_fusion.1
  146.4 14.9 %shard_map.124 = (bf16[1024,256]{1,0:T(8,128)(2,1)}, f32[1024,256]{1,0:T(8,128)}, f32[2,2048,128]{2,1,0:T(8,128)}) custom-call(bf16[1024,256]{1,0:T(8,128)(2,1)} %fusion.10.q_ref, bf16[1024,256]{1,0:T(8,128)(2,1)} %do_ref.1, bf16[2048,128]{1,0:T(8,128)(2,1)} %get-tuple-element.44.k_ref, bf16[2048,128]{1,0:T(8,128)(2,1)} %get-tuple-element.43.v_ref, ...), custom_call_target="tpu_custom_call" | custom-call | flops 6442450944 | bytes 8388608 | tf_op jit(solution)/shard_map/pallas_call | solution.py:126
  161.3 1.3 slice.108
  162.6 3.4 %collective-permute-start.2 = (bf16[2,1024,1,128]{3,1,2,0:T(8,128)(2,1)S(1)}, bf16[2,1024,1,128]{3,1,2,0:T(8,128)(2,1)S(1)}, u32[]{:S(2)}, u32[]{:S(2)}) collective-permute-start(bf16[2,1024,1,128]{3,1,2,0:T(8,128)(2,1)S(1)} %slice.108), channel_id=1, source_target_pairs={{8,0},{16,8},{24,16},{32,24},{40,32},{48,40},{56,48},{64,56},{72,6... | collective-permute-start | bytes 1572872 | tf_op jit(solution)/shard_map/ppermute | solution.py:19
  166.1 6.5 %collective-permute-done.2 = bf16[2,1024,1,128]{3,1,2,0:T(8,128)(2,1)S(1)} collective-permute-done((bf16[2,1024,1,128]{3,1,2,0:T(8,128)(2,1)S(1)}, bf16[2,1024,1,128]{3,1,2,0:T(8,128)(2,1)S(1)}, u32[]{:S(2)}, u32[]{:S(2)}) %collective-permute-start.2) | collective-permute-done | bytes 524320 | tf_op jit(solution)/shard_map/ppermute | solution.py:19
  172.5 1.3 slice_add_fusion
  174.5 2.8 broadcast_in_dim.18
  177.3 4.5 %all-to-all-start.2 = ((bf16[8,1024,2,128]{3,1,2,0:T(8,128)(2,1)}), bf16[8,1024,2,128]{3,1,2,0:T(8,128)(2,1)}, u32[]{:S(2)}, u32[]{:S(2)}) async-start(bf16[8,1024,2,128]{3,1,2,0:T(8,128)(2,1)} %broadcast_in_dim.18), calls=%async_computation.2 | async-start | bytes 8388608 | tf_op jit(solution)/shard_map/all_to_all | solution.py:28
  181.9 50.6 %all-to-all-done.2 = bf16[8,1024,2,128]{3,1,2,0:T(8,128)(2,1)} async-done(((bf16[8,1024,2,128]{3,1,2,0:T(8,128)(2,1)}), bf16[8,1024,2,128]{3,1,2,0:T(8,128)(2,1)}, u32[]{:S(2)}, u32[]{:S(2)}) %all-to-all-start.2) | async-done | bytes 4194336 | tf_op jit(solution)/shard_map/all_to_all | solution.py:28
  232.5 6.6 %convert_bitcast_fusion.1 = bf16[672,2,8,128]{3,0,1,2:T(8,128)(2,1)} fusion(bf16[8,1024,2,128]{3,1,2,0:T(8,128)(2,1)} %all-to-all-done.2, bf16[1024,672]{0,1:T(8,128)(2,1)S(1)} %copy-done), kind=kOutput, calls=%fused_computation.8 | convolution fusion | flops 2819948544 | bytes 8323072 | tf_op jit(solution)/shard_map/tf,htkc->fkhc/dot_general | solution.py:200
  239.0 4.6 %copy.68 = bf16[672,2,8,128]{0,3,2,1:T(8,128)(2,1)} copy(bf16[672,2,8,128]{3,0,1,2:T(8,128)(2,1)} %convert_bitcast_fusion.1) | data formatting | bytes 5505024 | tf_op jit(solution)/shard_map/convert_element_type | solution.py:202
  243.6 2.2 copy.69
  245.8 1.3 select_bitcast_fusion
  247.2 3.6 %collective-permute-done.3 = bf16[16,672,2,32]{1,3,2,0:T(8,128)(2,1)} collective-permute-done((bf16[16,672,2,32]{1,3,2,0:T(8,128)(2,1)}, bf16[16,672,2,32]{1,3,2,0:T(8,128)(2,1)}, u32[]{:S(2)}, u32[]{:S(2)}) %collective-permute-start.3) | collective-permute-done | bytes 1376288 | tf_op jit(solution)/shard_map/ppermute | solution.py:54
  250.9 3.6 %add_convert_fusion = bf16[16,672,2,32]{1,3,2,0:T(8,128)(2,1)} fusion(bf16[16,672,2,32]{1,3,2,0:T(8,128)(2,1)} %collective-permute-done.3, pred[]{:T(512)S(6)} %and.14, bf16[16,2,672,2,32]{2,4,1,0,3:T(8,128)(2,1)} %bitcast.86, s32[]{:T(128)S(6)} %select_n.36), kind=kLoop, calls=%fused_computation.6 | loop fusion | flops 3440640 | bytes 4521989 | tf_op jit(solution)/shard_map/convert_element_type | solution.py:55
  254.5 6.0 %all-to-all-start.3 = ((bf16[16,672,2,32]{1,3,2,0:T(8,128)(2,1)}), bf16[16,672,2,32]{1,3,2,0:T(8,128)(2,1)}, u32[]{:S(2)}, u32[]{:S(2)}) async-start(bf16[16,672,2,32]{1,3,2,0:T(8,128)(2,1)} %add_convert_fusion), calls=%async_computation.3 | async-start | bytes 3145728 | tf_op jit(solution)/shard_map/all_to_all | solution.py:28
  260.6 2.7 reshape.294
  263.3 2.4 multiply_reduce_fusion
  266.2 1.2 broadcast_in_dim.19
  267.4 2.4 fusion.7
  269.8 6.4 %bitcast_convert_fusion = bf16[1024,672]{0,1:T(8,128)(2,1)} fusion(bf16[8,1024,2,128]{3,1,2,0:T(8,128)(2,1)} %all-to-all-done.2, bf16[672,2,8,128]{0,3,2,1:T(8,128)(2,1)S(1)} %bitcast.93), kind=kOutput, calls=%fused_computation.7 | convolution fusion | flops 2819260416 | bytes 8323072 | tf_op jit(solution)/shard_map/htkc,fkhc->tf/dot_general | solution.py:197
  276.2 25.2 %all-to-all-done.3 = bf16[16,672,2,32]{1,3,2,0:T(8,128)(2,1)} async-done(((bf16[16,672,2,32]{1,3,2,0:T(8,128)(2,1)}), bf16[16,672,2,32]{1,3,2,0:T(8,128)(2,1)}, u32[]{:S(2)}, u32[]{:S(2)}) %all-to-all-start.3) | async-done | bytes 1376288 | tf_op jit(solution)/shard_map/all_to_all | solution.py:28
  301.4 1.7 convert_reduce_fusion.1
  (43 shorter events, 4.6 us)
Async XLA Ops:
  0.6 58.8 %copy-start = (bf16[1024,672]{0,1:T(8,128)(2,1)S(1)}, bf16[1024,672]{0,1:T(8,128)(2,1)}, u32[]{:S(2)}) copy-start(bf16[1024,672]{0,1:T(8,128)(2,1)} %param.14) | copy-start | bytes 4128772
  50.2 3.8 %collective-permute-start = (bf16[16,672,2,32]{1,3,2,0:T(8,128)(2,1)}, bf16[16,672,2,32]{1,3,2,0:T(8,128)(2,1)}, u32[]{:S(2)}, u32[]{:S(2)}) collective-permute-start(bf16[16,672,2,32]{1,3,2,0:T(8,128)(2,1)} %all_to_all.20), channel_id=1, source_target_pairs={{0,8},{8,0},{1,9},{9,1},{2,10},{10,2},{3,11},{11,3},{4,12},{12,4},... | collective-permute-start | bytes 4128776 | tf_op jit(solution)/shard_map/ppermute | solution.py:42
  57.7 1.7 copy-start.4
  65.5 7.3 %copy-start.3 = (bf16[1024,256]{1,0:T(8,128)(2,1)S(1)}, bf16[1024,256]{1,0:T(8,128)(2,1)}, u32[]{:S(2)}) copy-start(bf16[1024,256]{1,0:T(8,128)(2,1)} %param.15) | copy-start | bytes 1572868
  65.5 57.2 %all-to-all-start.1 = ((bf16[8,1024,2,128]{1,3,2,0:T(8,128)(2,1)}), bf16[8,1024,2,128]{1,3,2,0:T(8,128)(2,1)}, u32[]{:S(2)}, u32[]{:S(2)}) async-start(bf16[8,1024,2,128]{1,3,2,0:T(8,128)(2,1)} %copy.60), calls=%async_computation.1 | async-start | bytes 8388608 | tf_op jit(solution)/shard_map/all_to_all | solution.py:28
  125.9 4.9 %copy-start.9 = (f32[128]{0:T(128)S(1)}, f32[128]{0:T(128)}, u32[]{:S(2)}) copy-start(f32[128]{0:T(128)} %param.19) | copy-start | bytes 1540
  126.6 12.8 %copy-start.10 = (f32[128]{0:T(128)S(1)}, f32[128]{0:T(128)}, u32[]{:S(2)}) copy-start(f32[128]{0:T(128)} %param.18) | copy-start | bytes 1540
  130.9 0.7 copy-start.7
  133.4 10.8 %collective-permute-start.1 = (bf16[2,1024,1,128]{3,1,2,0:T(8,128)(2,1)}, bf16[2,1024,1,128]{3,1,2,0:T(8,128)(2,1)}, u32[]{:S(2)}, u32[]{:S(2)}) collective-permute-start(bf16[2,1024,1,128]{3,1,2,0:T(8,128)(2,1)} %pad_maximum_fusion), channel_id=1, source_target_pairs={{0,8},{8,16},{16,24},{24,32},{32,40},{40,48},{48,56},{56,64},{64,7... | collective-permute-start | bytes 1572872 | tf_op jit(solution)/shard_map/ppermute | solution.py:19
  139.4 4.9 %copy-start.6 = (bf16[1024,1,128]{2,0,1:T(8,128)(2,1)S(1)}, bf16[1024,1,128]{2,0,1:T(8,128)(2,1)}, u32[]{:S(2)}) copy-start(bf16[1024,1,128]{2,0,1:T(8,128)(2,1)} %copy.80) | copy-start | bytes 786436
  139.4 4.9 %copy-start.8 = (bf16[1,1024,1,128]{3,1,2,0:T(8,128)(2,1)S(1)}, bf16[1,1024,1,128]{3,1,2,0:T(8,128)(2,1)}, u32[]{:S(2)}) copy-start(bf16[1,1024,1,128]{3,1,2,0:T(8,128)(2,1)} %copy-done.7) | copy-start | bytes 786436
  141.8 1.0 copy-start.1
  162.6 9.9 %collective-permute-start.2 = (bf16[2,1024,1,128]{3,1,2,0:T(8,128)(2,1)S(1)}, bf16[2,1024,1,128]{3,1,2,0:T(8,128)(2,1)S(1)}, u32[]{:S(2)}, u32[]{:S(2)}) collective-permute-start(bf16[2,1024,1,128]{3,1,2,0:T(8,128)(2,1)S(1)} %slice.108), channel_id=1, source_target_pairs={{8,0},{16,8},{24,16},{32,24},{40,32},{48,40},{56,48},{64,56},{72,6... | collective-permute-start | bytes 1572872 | tf_op jit(solution)/shard_map/ppermute | solution.py:19
  177.3 55.2 %all-to-all-start.2 = ((bf16[8,1024,2,128]{3,1,2,0:T(8,128)(2,1)}), bf16[8,1024,2,128]{3,1,2,0:T(8,128)(2,1)}, u32[]{:S(2)}, u32[]{:S(2)}) async-start(bf16[8,1024,2,128]{3,1,2,0:T(8,128)(2,1)} %broadcast_in_dim.18), calls=%async_computation.2 | async-start | bytes 8388608 | tf_op jit(solution)/shard_map/all_to_all | solution.py:28
  247.1 3.8 %collective-permute-start.3 = (bf16[16,672,2,32]{1,3,2,0:T(8,128)(2,1)}, bf16[16,672,2,32]{1,3,2,0:T(8,128)(2,1)}, u32[]{:S(2)}, u32[]{:S(2)}) collective-permute-start(bf16[16,672,2,32]{1,3,2,0:T(8,128)(2,1)} %select_bitcast_fusion), channel_id=1, source_target_pairs={{0,8},{8,0},{1,9},{9,1},{2,10},{10,2},{3,11},{11,3},{4,12},{12,4},... | collective-permute-start | bytes 4128776 | tf_op jit(solution)/shard_map/ppermute | solution.py:54
  254.5 46.9 %all-to-all-start.3 = ((bf16[16,672,2,32]{1,3,2,0:T(8,128)(2,1)}), bf16[16,672,2,32]{1,3,2,0:T(8,128)(2,1)}, u32[]{:S(2)}, u32[]{:S(2)}) async-start(bf16[16,672,2,32]{1,3,2,0:T(8,128)(2,1)} %add_convert_fusion), calls=%async_computation.3 | async-start | bytes 3145728 | tf_op jit(solution)/shard_map/all_to_all | solution.py:28
  265.7 1.7 copy-start.2
  266.1 3.6 %copy-start.5 = (bf16[672,2,32,32]{0,3,2,1:T(8,128)(2,1)S(1)}, bf16[672,2,32,32]{0,3,2,1:T(8,128)(2,1)}, u32[]{:S(2)}) copy-start(bf16[672,2,32,32]{0,3,2,1:T(8,128)(2,1)} %copy-done.4) | copy-start | bytes 8257540

commit v4 on v3

--- a/solution.py
+++ b/solution.py
@@ -1,3 +1,5 @@
+import functools
+
 import jax
 import jax.numpy as jnp
 from jax import lax
@@ -37,12 +39,82 @@
 SWAP = [(0, 1), (1, 0)]
 
 
+def gather_kernel(chips, x_ref, out_ref, local_sem, send_sem, recv_sem, fwd_send, fwd_recv):
+    chip = lax.axis_index("chip")
+    core = lax.axis_index("core")
+    uly = lax.axis_index("uly")
+    other = 1 - core
+    mesh_ids = pl.DeviceIdType.MESH
+    barrier = pltpu.get_barrier_semaphore()
+    for d in range(1, chips):
+        peer = (lax.rem(chip + d, chips), core, uly)
+        pl.semaphore_signal(barrier, 1, device_id=peer, device_id_type=mesh_ids)
+    pl.semaphore_signal(barrier, 1, device_id=(chip, other, uly), device_id_type=mesh_ids)
+    pl.semaphore_wait(barrier, chips)
+    mine = chip * 2 + core
+    local = pltpu.make_async_copy(x_ref, out_ref.at[mine], local_sem)
+    local.start()
+    sends = {}
+    for d in range(1, chips):
+        sends[d] = pltpu.make_async_remote_copy(
+            src_ref=x_ref,
+            dst_ref=out_ref.at[mine],
+            send_sem=send_sem.at[d],
+            recv_sem=recv_sem.at[d],
+            device_id=(lax.rem(chip + d, chips), core, uly),
+            device_id_type=mesh_ids,
+        )
+        sends[d].start()
+    forwards = [
+        pltpu.make_async_remote_copy(
+            src_ref=x_ref,
+            dst_ref=out_ref.at[mine],
+            send_sem=fwd_send.at[0],
+            recv_sem=fwd_recv.at[0],
+            device_id=(chip, other, uly),
+            device_id_type=mesh_ids,
+        )
+    ]
+    forwards[0].start()
+    for d in range(1, chips):
+        sends[d].wait_recv()
+        slot = lax.rem(chip + chips - d, chips) * 2 + core
+        forward = pltpu.make_async_remote_copy(
+            src_ref=out_ref.at[slot],
+            dst_ref=out_ref.at[slot],
+            send_sem=fwd_send.at[d],
+            recv_sem=fwd_recv.at[d],
+            device_id=(chip, other, uly),
+            device_id_type=mesh_ids,
+        )
+        forward.start()
+        forwards.append(forward)
+    for d in range(1, chips):
+        sends[d].wait_send()
+    for forward in forwards:
+        forward.wait()
+    local.wait()
+
+
 def gather_seq(block):
-    mine = gather_all(block, "chip")
-    other = lax.ppermute(mine, "core", SWAP)
-    first = lax.axis_index("core") == 0
-    pair = jnp.where(first, jnp.stack([mine, other], 1), jnp.stack([other, mine], 1))
-    return pair.reshape((-1,) + block.shape)
+    chips = lax.axis_size("chip")
+    flat = block.reshape(-1, 128)
+    spec = pl.BlockSpec(memory_space=pltpu.VMEM)
+    out = pl.pallas_call(
+        functools.partial(gather_kernel, chips),
+        out_shape=jax.ShapeDtypeStruct((2 * chips,) + flat.shape, flat.dtype),
+        in_specs=[spec],
+        out_specs=spec,
+        scratch_shapes=[
+            pltpu.SemaphoreType.DMA(()),
+            pltpu.SemaphoreType.DMA((chips,)),
+            pltpu.SemaphoreType.DMA((chips,)),
+            pltpu.SemaphoreType.DMA((chips,)),
+            pltpu.SemaphoreType.DMA((chips,)),
+        ],
+        compiler_params=pltpu.CompilerParams(collective_id=0, has_side_effects=True),
+    )(flat)
+    return out.reshape((2 * chips,) + block.shape)
 
 
 def reduce_seq(blocks):

time: 305 us -> 337 us (1.10)
  blocking collectives: 48.4 us -> 0 us
  local copies, waits for them, and re-layouts: 35 us -> 76.6 us
  Pallas kernels: 14.9 us -> 52.1 us
  starting transfers between devices: 23.4 us -> 32.9 us
  waiting for transfers between devices: 138 us -> 130 us
    all_to_all x1 -> x0, blocking collectives: 48.4 us -> none  [exchange(): return lax.all_to_all(blocks, axis, 0, 0)]
    pallas_call x0 -> x1, Pallas kernels: none -> 37.2 us  [gather_seq(): pl.pallas_call(functools.partial(gather_kernel, chips), out_shape=jax.Sha...]
    reshape x0 -> x2, local copies, waits for them, and re-layouts: none -> 23.4 us  [the longest x1 22.5 us: gather_seq(): return out.reshape((2 * chips,) + block.shape)]
    transpose x1, local copies, waits for them, and re-layouts: 0.24 us -> 20.7 us  [body(): gathered.transpose(1, 2, 0, 3).reshape(feats, 2, n_uly, heads_here * HD)]
    all_to_all x3, starting transfers between devices: 17.9 us -> 24.8 us  [exchange(): return lax.all_to_all(blocks, axis, 0, 0)]
    all_to_all x3, waiting for transfers between devices: 124 us -> 120 us  [exchange(): return lax.all_to_all(blocks, axis, 0, 0)]
    ppermute x1 -> x0, waiting for transfers between devices: 3.75 us -> none  [gather_seq(): other = lax.ppermute(mine, 'core', SWAP)]
    select_n x1 -> x0, other arithmetic: 3.51 us -> none  [gather_seq(): jnp.where(first, jnp.stack([mine, other], 1), jnp.stack([other, mine], 1))]
  transfers between devices with their start and end apart: 7 -> 6, of which waited for: 7 -> 6; matrix products, arithmetic and copies ran while one was open for 8% -> 8% of each run, Pallas kernels for 0% -> 0%
where the time goes in v4:
time: 337 us; the launch traced here: 335 us
  waiting for transfers between devices  130 us (39%)
  local copies, waits for them, and re-layouts  76.6 us (23%)
  Pallas kernels  52.1 us (15%)
  starting transfers between devices  32.9 us (10%)
  other arithmetic  23.8 us (7%)
  matrix products  18.4 us (5%)
    all_to_all x3, waiting for transfers between devices, exchange(): return lax.all_to_all(blocks, axis, 0, 0)  120 us
    pallas_call x1, Pallas kernels, gather_seq(): pl.pallas_call(functools.partial(gather_kernel, chips), out_shape=jax.Sha...  37.2 us
    all_to_all x3, starting transfers between devices, exchange(): return lax.all_to_all(blocks, axis, 0, 0)  24.8 us
    reshape x1, local copies, waits for them, and re-layouts, gather_seq(): return out.reshape((2 * chips,) + block.shape)  22.5 us
    transpose x1, local copies, waits for them, and re-layouts, body(): gathered.transpose(1, 2, 0, 3).reshape(feats, 2, n_uly, heads_here * HD)  20.7 us
    pallas_call x1, Pallas kernels, attend(): pl.pallas_call(attention_kernel, out_shape=(jax.ShapeDtypeStruct((rows, 2...  14.8 us
    ppermute x2, waiting for transfers between devices, from_behind(): return lax.ppermute(array, axis, pairs)  6.92 us
  transfers between devices with their start and end apart: 6, of which 6 were waited for; matrix products, arithmetic and copies ran while one was open for 8% of the time, Pallas kernels for 0%

profile of v4, /device:TPU:2, one launch (start us, length us, event | category | flops | bytes accessed | tf_op | source)
XLA Modules:
  0.0 334.8 jit_solution(2258479842111679636)
XLA Ops:
  0.6 0.9 pad_maximum_fusion.2
  1.8 0.8 reshape.290.x_ref
  2.6 37.2 %shard_map.124 = bf16[32,336,128]{2,1,0:T(8,128)(2,1)} custom-call(bf16[336,128]{1,0:T(8,128)(2,1)} %reshape.290.x_ref), custom_call_target="tpu_custom_call" | custom-call | tf_op jit(solution)/shard_map/pallas_call | solution.py:103
  39.9 22.5 %reshape.291 = bf16[32,672,2,32]{3,2,1,0:T(2,128)(2,1)} reshape(bf16[32,336,128]{2,1,0:T(8,128)(2,1)} %shard_map.124) | data formatting | bytes 5505024 | tf_op jit(solution)/shard_map/reshape | solution.py:117
  62.4 20.7 %copy.53 = bf16[672,2,32,32]{0,3,2,1:T(8,128)(2,1)} copy(bf16[672,2,32,32]{3,1,0,2:T(2,128)(2,1)} %bitcast.81) | data formatting | bytes 5505024 | tf_op jit(solution)/shard_map/transpose | solution.py:225
  83.2 5.5 %convert_bitcast_fusion = bf16[8,1024,2,128]{1,3,0,2:T(8,128)(2,1)S(1)} fusion(bf16[672,2,8,128]{0,3,2,1:T(8,128)(2,1)} %bitcast.88, bf16[1024,672]{0,1:T(8,128)(2,1)S(1)} %copy-done), kind=kOutput, calls=%fused_computation.1 | convolution fusion | flops 2820669440 | bytes 8323072 | tf_op jit(solution)/shard_map/tf,fkhc->htkc/dot_general | solution.py:226
  88.7 2.4 copy.55
  91.1 9.7 %all-to-all-start = ((bf16[8,1024,2,128]{1,3,2,0:T(8,128)(2,1)}), bf16[8,1024,2,128]{1,3,2,0:T(8,128)(2,1)}, u32[]{:S(2)}, u32[]{:S(2)}) async-start(bf16[8,1024,2,128]{1,3,2,0:T(8,128)(2,1)} %copy.55), calls=%async_computation | async-start | bytes 8388608 | tf_op jit(solution)/shard_map/all_to_all | solution.py:30
  101.3 1.2 multiply_reduce_fusion.1
  102.7 48.2 %all-to-all-done = bf16[8,1024,2,128]{1,3,2,0:T(8,128)(2,1)} async-done(((bf16[8,1024,2,128]{1,3,2,0:T(8,128)(2,1)}), bf16[8,1024,2,128]{1,3,2,0:T(8,128)(2,1)}, u32[]{:S(2)}, u32[]{:S(2)}) %all-to-all-start) | async-done | bytes 4194336 | tf_op jit(solution)/shard_map/all_to_all | solution.py:30
  150.9 3.2 convert_reduce_fusion
  154.1 0.8 slice.82
  155.0 0.8 copy.75
  155.8 1.2 copy.74
  158.2 1.8 pad_maximum_fusion
  160.0 1.9 collective-permute-start
  161.9 1.3 pad_dynamic-slice_fusion
  163.2 1.0 copy.51
  164.9 1.0 copy.59.qseg_ref
  165.9 2.4 mul.204
  168.4 1.0 copy-done.1
  169.4 1.0 fusion.10.q_ref
  170.8 1.1 maximum_maximum_fusion
  171.9 1.1 slice_bitcast_fusion.1
  173.0 14.8 %shard_map.125 = (bf16[1024,256]{1,0:T(8,128)(2,1)}, f32[1024,256]{1,0:T(8,128)}, f32[2,2048,128]{2,1,0:T(8,128)}) custom-call(bf16[1024,256]{1,0:T(8,128)(2,1)} %fusion.10.q_ref, bf16[1024,256]{1,0:T(8,128)(2,1)} %do_ref.1, bf16[2048,128]{1,0:T(8,128)(2,1)} %get-tuple-element.44.k_ref, bf16[2048,128]{1,0:T(8,128)(2,1)} %get-tuple-element.43.v_ref, ...), custom_call_target="tpu_custom_call" | custom-call | flops 6442450944 | bytes 8388608 | tf_op jit(solution)/shard_map/pallas_call | solution.py:198
  187.8 1.3 slice.108
  189.1 3.4 %collective-permute-start.1 = (bf16[2,1024,1,128]{3,1,2,0:T(8,128)(2,1)S(1)}, bf16[2,1024,1,128]{3,1,2,0:T(8,128)(2,1)S(1)}, u32[]{:S(2)}, u32[]{:S(2)}) collective-permute-start(bf16[2,1024,1,128]{3,1,2,0:T(8,128)(2,1)S(1)} %slice.108), channel_id=1, source_target_pairs={{8,0},{16,8},{24,16},{32,24},{40,32},{48,40},{56,48},{64,56},{72,6... | collective-permute-start | bytes 1572872 | tf_op jit(solution)/shard_map/ppermute | solution.py:21
  192.5 6.5 %collective-permute-done.1 = bf16[2,1024,1,128]{3,1,2,0:T(8,128)(2,1)S(1)} collective-permute-done((bf16[2,1024,1,128]{3,1,2,0:T(8,128)(2,1)S(1)}, bf16[2,1024,1,128]{3,1,2,0:T(8,128)(2,1)S(1)}, u32[]{:S(2)}, u32[]{:S(2)}) %collective-permute-start.1) | collective-permute-done | bytes 524320 | tf_op jit(solution)/shard_map/ppermute | solution.py:21
  199.0 1.3 slice_add_fusion
  201.0 2.8 broadcast_in_dim.15
  203.8 4.6 %all-to-all-start.1 = ((bf16[8,1024,2,128]{3,1,2,0:T(8,128)(2,1)}), bf16[8,1024,2,128]{3,1,2,0:T(8,128)(2,1)}, u32[]{:S(2)}, u32[]{:S(2)}) async-start(bf16[8,1024,2,128]{3,1,2,0:T(8,128)(2,1)} %broadcast_in_dim.15), calls=%async_computation.1 | async-start | bytes 8388608 | tf_op jit(solution)/shard_map/all_to_all | solution.py:30
  208.3 47.9 %all-to-all-done.1 = bf16[8,1024,2,128]{3,1,2,0:T(8,128)(2,1)} async-done(((bf16[8,1024,2,128]{3,1,2,0:T(8,128)(2,1)}), bf16[8,1024,2,128]{3,1,2,0:T(8,128)(2,1)}, u32[]{:S(2)}, u32[]{:S(2)}) %all-to-all-start.1) | async-done | bytes 4194336 | tf_op jit(solution)/shard_map/all_to_all | solution.py:30
  256.3 6.5 %convert_bitcast_fusion.1 = bf16[672,2,8,128]{3,0,1,2:T(8,128)(2,1)} fusion(bf16[8,1024,2,128]{3,1,2,0:T(8,128)(2,1)} %all-to-all-done.1, bf16[1024,672]{0,1:T(8,128)(2,1)S(1)} %copy-done), kind=kOutput, calls=%fused_computation.7 | convolution fusion | flops 2819948544 | bytes 8323072 | tf_op jit(solution)/shard_map/tf,htkc->fkhc/dot_general | solution.py:272
  262.8 4.6 %copy.63 = bf16[672,2,8,128]{0,3,2,1:T(8,128)(2,1)} copy(bf16[672,2,8,128]{3,0,1,2:T(8,128)(2,1)} %convert_bitcast_fusion.1) | data formatting | bytes 5505024 | tf_op jit(solution)/shard_map/convert_element_type | solution.py:274
  267.4 2.2 copy.64
  269.6 1.4 select_bitcast_fusion
  270.9 2.8 collective-permute-start.2
  273.7 3.4 %collective-permute-done.2 = bf16[16,672,2,32]{1,3,2,0:T(8,128)(2,1)} collective-permute-done((bf16[16,672,2,32]{1,3,2,0:T(8,128)(2,1)}, bf16[16,672,2,32]{1,3,2,0:T(8,128)(2,1)}, u32[]{:S(2)}, u32[]{:S(2)}) %collective-permute-start.2) | collective-permute-done | bytes 1376288 | tf_op jit(solution)/shard_map/ppermute | solution.py:126
  277.1 3.7 %add_convert_fusion = bf16[16,672,2,32]{1,3,2,0:T(8,128)(2,1)} fusion(bf16[16,672,2,32]{1,3,2,0:T(8,128)(2,1)} %collective-permute-done.2, pred[]{:T(512)S(6)} %and.14, bf16[16,2,672,2,32]{2,4,1,0,3:T(8,128)(2,1)} %bitcast.83, s32[]{:T(128)S(6)} %select_n.21), kind=kLoop, calls=%fused_computation.5 | loop fusion | flops 3440640 | bytes 4521989 | tf_op jit(solution)/shard_map/convert_element_type | solution.py:127
  280.8 10.5 %all-to-all-start.2 = ((bf16[16,672,2,32]{1,3,2,0:T(8,128)(2,1)}), bf16[16,672,2,32]{1,3,2,0:T(8,128)(2,1)}, u32[]{:S(2)}, u32[]{:S(2)}) async-start(bf16[16,672,2,32]{1,3,2,0:T(8,128)(2,1)} %add_convert_fusion), calls=%async_computation.2 | async-start | bytes 3145728 | tf_op jit(solution)/shard_map/all_to_all | solution.py:30
  291.3 2.7 reshape.296
  294.1 3.2 multiply_reduce_fusion
  297.3 1.3 copy.61
  298.9 1.2 broadcast_in_dim.16
  300.1 2.4 fusion.7
  302.5 6.4 %bitcast_convert_fusion = bf16[1024,672]{0,1:T(8,128)(2,1)} fusion(bf16[8,1024,2,128]{3,1,2,0:T(8,128)(2,1)} %all-to-all-done.1, bf16[672,2,8,128]{0,3,2,1:T(8,128)(2,1)S(1)} %bitcast.89), kind=kOutput, calls=%fused_computation.6 | convolution fusion | flops 2819260416 | bytes 8323072 | tf_op jit(solution)/shard_map/htkc,fkhc->tf/dot_general | solution.py:269
  308.9 23.6 %all-to-all-done.2 = bf16[16,672,2,32]{1,3,2,0:T(8,128)(2,1)} async-done(((bf16[16,672,2,32]{1,3,2,0:T(8,128)(2,1)}), bf16[16,672,2,32]{1,3,2,0:T(8,128)(2,1)}, u32[]{:S(2)}, u32[]{:S(2)}) %all-to-all-start.2) | async-done | bytes 1376288 | tf_op jit(solution)/shard_map/all_to_all | solution.py:30
  332.5 1.7 convert_reduce_fusion.1
  (40 shorter events, 4.8 us)
Async XLA Ops:
  0.6 82.6 %copy-start = (bf16[1024,672]{0,1:T(8,128)(2,1)S(1)}, bf16[1024,672]{0,1:T(8,128)(2,1)}, u32[]{:S(2)}) copy-start(bf16[1024,672]{0,1:T(8,128)(2,1)} %param.14) | copy-start | bytes 4128772
  91.1 9.7 %copy-start.3 = (bf16[1024,256]{1,0:T(8,128)(2,1)S(1)}, bf16[1024,256]{1,0:T(8,128)(2,1)}, u32[]{:S(2)}) copy-start(bf16[1024,256]{1,0:T(8,128)(2,1)} %param.15) | copy-start | bytes 1572868
  91.1 59.8 %all-to-all-start = ((bf16[8,1024,2,128]{1,3,2,0:T(8,128)(2,1)}), bf16[8,1024,2,128]{1,3,2,0:T(8,128)(2,1)}, u32[]{:S(2)}, u32[]{:S(2)}) async-start(bf16[8,1024,2,128]{1,3,2,0:T(8,128)(2,1)} %copy.55), calls=%async_computation | async-start | bytes 8388608 | tf_op jit(solution)/shard_map/all_to_all | solution.py:30
  154.1 3.2 copy-start.8
  155.0 11.0 %copy-start.9 = (f32[128]{0:T(128)S(1)}, f32[128]{0:T(128)}, u32[]{:S(2)}) copy-start(f32[128]{0:T(128)} %param.18) | copy-start | bytes 1540
  157.5 0.7 copy-start.6
  160.0 10.8 %collective-permute-start = (bf16[2,1024,1,128]{3,1,2,0:T(8,128)(2,1)}, bf16[2,1024,1,128]{3,1,2,0:T(8,128)(2,1)}, u32[]{:S(2)}, u32[]{:S(2)}) collective-permute-start(bf16[2,1024,1,128]{3,1,2,0:T(8,128)(2,1)} %pad_maximum_fusion), channel_id=1, source_target_pairs={{0,8},{8,16},{16,24},{24,32},{32,40},{40,48},{48,56},{56,64},{64,7... | collective-permute-start | bytes 1572872 | tf_op jit(solution)/shard_map/ppermute | solution.py:21
  165.9 4.8 %copy-start.5 = (bf16[1024,1,128]{2,0,1:T(8,128)(2,1)S(1)}, bf16[1024,1,128]{2,0,1:T(8,128)(2,1)}, u32[]{:S(2)}) copy-start(bf16[1024,1,128]{2,0,1:T(8,128)(2,1)} %copy.75) | copy-start | bytes 786436
  165.9 4.8 %copy-start.7 = (bf16[1,1024,1,128]{3,1,2,0:T(8,128)(2,1)S(1)}, bf16[1,1024,1,128]{3,1,2,0:T(8,128)(2,1)}, u32[]{:S(2)}) copy-start(bf16[1,1024,1,128]{3,1,2,0:T(8,128)(2,1)} %copy-done.6) | copy-start | bytes 786436
  168.4 1.0 copy-start.1
  189.1 9.9 %collective-permute-start.1 = (bf16[2,1024,1,128]{3,1,2,0:T(8,128)(2,1)S(1)}, bf16[2,1024,1,128]{3,1,2,0:T(8,128)(2,1)S(1)}, u32[]{:S(2)}, u32[]{:S(2)}) collective-permute-start(bf16[2,1024,1,128]{3,1,2,0:T(8,128)(2,1)S(1)} %slice.108), channel_id=1, source_target_pairs={{8,0},{16,8},{24,16},{32,24},{40,32},{48,40},{56,48},{64,56},{72,6... | collective-permute-start | bytes 1572872 | tf_op jit(solution)/shard_map/ppermute | solution.py:21
  203.8 52.5 %all-to-all-start.1 = ((bf16[8,1024,2,128]{3,1,2,0:T(8,128)(2,1)}), bf16[8,1024,2,128]{3,1,2,0:T(8,128)(2,1)}, u32[]{:S(2)}, u32[]{:S(2)}) async-start(bf16[8,1024,2,128]{3,1,2,0:T(8,128)(2,1)} %broadcast_in_dim.15), calls=%async_computation.1 | async-start | bytes 8388608 | tf_op jit(solution)/shard_map/all_to_all | solution.py:30
  270.9 6.2 %collective-permute-start.2 = (bf16[16,672,2,32]{1,3,2,0:T(8,128)(2,1)}, bf16[16,672,2,32]{1,3,2,0:T(8,128)(2,1)}, u32[]{:S(2)}, u32[]{:S(2)}) collective-permute-start(bf16[16,672,2,32]{1,3,2,0:T(8,128)(2,1)} %select_bitcast_fusion), channel_id=1, source_target_pairs={{0,8},{8,0},{1,9},{9,1},{2,10},{10,2},{3,11},{11,3},{4,12},{12,4},... | collective-permute-start | bytes 4128776 | tf_op jit(solution)/shard_map/ppermute | solution.py:126
  280.8 51.7 %all-to-all-start.2 = ((bf16[16,672,2,32]{1,3,2,0:T(8,128)(2,1)}), bf16[16,672,2,32]{1,3,2,0:T(8,128)(2,1)}, u32[]{:S(2)}, u32[]{:S(2)}) async-start(bf16[16,672,2,32]{1,3,2,0:T(8,128)(2,1)} %add_convert_fusion), calls=%async_computation.2 | async-start | bytes 3145728 | tf_op jit(solution)/shard_map/all_to_all | solution.py:30
  297.3 2.8 copy-start.2
  298.8 3.6 %copy-start.4 = (bf16[672,2,32,32]{0,3,2,1:T(8,128)(2,1)S(1)}, bf16[672,2,32,32]{0,3,2,1:T(8,128)(2,1)}, u32[]{:S(2)}) copy-start(bf16[672,2,32,32]{0,3,2,1:T(8,128)(2,1)} %copy.53) | copy-start | bytes 8257540

commit v5 on v4

--- a/solution.py
+++ b/solution.py
@@ -52,13 +52,13 @@
     pl.semaphore_signal(barrier, 1, device_id=(chip, other, uly), device_id_type=mesh_ids)
     pl.semaphore_wait(barrier, chips)
     mine = chip * 2 + core
-    local = pltpu.make_async_copy(x_ref, out_ref.at[mine], local_sem)
+    local = pltpu.make_async_copy(x_ref, out_ref.at[:, pl.ds(mine, 1)], local_sem)
     local.start()
     sends = {}
     for d in range(1, chips):
         sends[d] = pltpu.make_async_remote_copy(
             src_ref=x_ref,
-            dst_ref=out_ref.at[mine],
+            dst_ref=out_ref.at[:, pl.ds(mine, 1)],
             send_sem=send_sem.at[d],
             recv_sem=recv_sem.at[d],
             device_id=(lax.rem(chip + d, chips), core, uly),
@@ -68,7 +68,7 @@
     forwards = [
         pltpu.make_async_remote_copy(
             src_ref=x_ref,
-            dst_ref=out_ref.at[mine],
+            dst_ref=out_ref.at[:, pl.ds(mine, 1)],
             send_sem=fwd_send.at[0],
             recv_sem=fwd_recv.at[0],
             device_id=(chip, other, uly),
@@ -80,8 +80,8 @@
         sends[d].wait_recv()
         slot = lax.rem(chip + chips - d, chips) * 2 + core
         forward = pltpu.make_async_remote_copy(
-            src_ref=out_ref.at[slot],
-            dst_ref=out_ref.at[slot],
+            src_ref=out_ref.at[:, pl.ds(slot, 1)],
+            dst_ref=out_ref.at[:, pl.ds(slot, 1)],
             send_sem=fwd_send.at[d],
             recv_sem=fwd_recv.at[d],
             device_id=(chip, other, uly),
@@ -98,11 +98,10 @@
 
 def gather_seq(block):
     chips = lax.axis_size("chip")
-    flat = block.reshape(-1, 128)
     spec = pl.BlockSpec(memory_space=pltpu.VMEM)
-    out = pl.pallas_call(
+    return pl.pallas_call(
         functools.partial(gather_kernel, chips),
-        out_shape=jax.ShapeDtypeStruct((2 * chips,) + flat.shape, flat.dtype),
+        out_shape=jax.ShapeDtypeStruct((block.shape[0], 2 * chips) + block.shape[1:], block.dtype),
         in_specs=[spec],
         out_specs=spec,
         scratch_shapes=[
@@ -113,8 +112,7 @@
             pltpu.SemaphoreType.DMA((chips,)),
         ],
         compiler_params=pltpu.CompilerParams(collective_id=0, has_side_effects=True),
-    )(flat)
-    return out.reshape((2 * chips,) + block.shape)
+    )(block[:, None])
 
 
 def reduce_seq(blocks):
@@ -220,12 +218,12 @@
     col_block = key_weight.shape[1]
     seq_index = lax.axis_index(SEQ)
     base_row = seq_index * rows_here
-    pair_local = jnp.stack([key_weight, value_weight], axis=1)
-    gathered = gather_seq(pair_local)
-    weight_all = gathered.transpose(1, 2, 0, 3).reshape(feats, 2, n_uly, heads_here * HD)
-    terms = jnp.einsum(
-        "tf,fkhc->htkc", normed, weight_all, preferred_element_type=jnp.float32
+    pair_t = jnp.stack([key_weight.T, value_weight.T])
+    weight_t = gather_seq(pair_t).reshape(2, n_seq * col_block, feats)
+    terms = lax.dot_general(
+        normed, weight_t, (((1,), (2,)), ((), ())), preferred_element_type=jnp.float32
     ).astype(jnp.bfloat16)
+    terms = terms.reshape(rows_here, 2, n_uly, heads_here * HD).transpose(2, 0, 1, 3)
     received = exchange(terms, "uly")
     raw_pair = jnp.sum(received.astype(jnp.float32), axis=0)
     key_raw = raw_pair[:, 0]
@@ -266,8 +264,9 @@
     key_grad = pull_key(own_grads[0])[0].astype(jnp.bfloat16).reshape(rows_here, heads_here * HD)
     value_grad = own_grads[1].astype(jnp.bfloat16).reshape(rows_here, heads_here * HD)
     grads_all = gather_all(jnp.stack([key_grad, value_grad], axis=1), "uly")
+    weight_heads = weight_t.reshape(2, n_uly, heads_here * HD, feats)
     grad_normed = jnp.einsum(
-        "htkc,fkhc->tf", grads_all, weight_all, preferred_element_type=jnp.float32
+        "htkc,khcf->tf", grads_all, weight_heads, preferred_element_type=jnp.float32
     ).astype(jnp.bfloat16)
     weight_part = jnp.einsum(
         "tf,htkc->fkhc", normed, grads_all, preferred_element_type=jnp.float32

time: 337 us -> 299 us (0.89)
  local copies, waits for them, and re-layouts: 76.6 us -> 32.9 us
  Pallas kernels: 52.1 us -> 56.9 us
    reshape x2 -> x1, local copies, waits for them, and re-layouts: 23.4 us -> 2.4 us  [body(): terms.reshape(rows_here, 2, n_uly, heads_here * HD).transpose(2, 0, 1, 3)]
    transpose x1 -> x0, local copies, waits for them, and re-layouts: 20.7 us -> none  [body(): gathered.transpose(1, 2, 0, 3).reshape(feats, 2, n_uly, heads_here * HD)]
    pallas_call x1, Pallas kernels: 37.2 us -> 42 us  [gather_seq(): pl.pallas_call(functools.partial(gather_kernel, chips), out_shape=jax.Sha...]
where the time goes in v5:
time: 299 us; the launch traced here: 298 us
  waiting for transfers between devices  132 us (44%)
  Pallas kernels  56.9 us (19%)
  starting transfers between devices  33.2 us (11%)
  local copies, waits for them, and re-layouts  32.9 us (11%)
  other arithmetic  23.6 us (8%)
  matrix products  18.5 us (6%)
    all_to_all x3, waiting for transfers between devices, exchange(): return lax.all_to_all(blocks, axis, 0, 0)  121 us
    pallas_call x1, Pallas kernels, gather_seq(): pl.pallas_call(functools.partial(gather_kernel, chips), out_shape=jax.Sha...  42 us
    all_to_all x3, starting transfers between devices, exchange(): return lax.all_to_all(blocks, axis, 0, 0)  24.8 us
    pallas_call x1, Pallas kernels, attend(): pl.pallas_call(attention_kernel, out_shape=(jax.ShapeDtypeStruct((rows, 2...  14.9 us
    ppermute x2, waiting for transfers between devices, from_behind(): return lax.ppermute(array, axis, pairs)  6.91 us
    dot_general x1, matrix products, body(): jnp.einsum('tf,htkc->fkhc', normed, grads_all, preferred_element_type=jnp...  6.58 us
    dot_general x1, matrix products, body(): jnp.einsum('htkc,khcf->tf', grads_all, weight_heads, preferred_element_ty...  6.38 us
  transfers between devices with their start and end apart: 6, of which 6 were waited for; matrix products, arithmetic and copies ran while one was open for 8% of the time, Pallas kernels for 0%

profile of v5, /device:TPU:2, one launch (start us, length us, event | category | flops | bytes accessed | tf_op | source)
XLA Modules:
  0.0 297.6 jit_solution(9741429547271596513)
XLA Ops:
  0.6 1.6 maximum_bitcast_fusion.x_ref
  2.2 42.0 %shard_map.124 = bf16[2,32,32,672]{3,2,1,0:T(8,128)(2,1)} custom-call(bf16[2,1,32,672]{3,2,1,0:T(8,128)(2,1)} %maximum_bitcast_fusion.x_ref), custom_call_target="tpu_custom_call" | custom-call | tf_op jit(solution)/shard_map/pallas_call | solution.py:102
  44.3 5.5 %convolution_convert_fusion = bf16[2,1024,1024]{2,1,0:T(8,128)(2,1)S(1)} fusion(bf16[2,1024,672]{2,1,0:T(8,128)(2,1)} %bitcast.100, bf16[1024,672]{0,1:T(8,128)(2,1)S(1)} %copy-done), kind=kOutput, calls=%fused_computation.8 | convolution fusion | flops 2820669440 | bytes 8323072 | tf_op jit(solution)/shard_map/dot_general | solution.py:223
  49.8 2.4 copy.83
  52.2 9.0 %all-to-all-start = ((bf16[8,1024,2,128]{1,3,2,0:T(8,128)(2,1)}), bf16[8,1024,2,128]{1,3,2,0:T(8,128)(2,1)}, u32[]{:S(2)}, u32[]{:S(2)}) async-start(bf16[8,1024,2,128]{1,3,2,0:T(8,128)(2,1)} %bitcast.94), calls=%async_computation | async-start | bytes 8388608 | tf_op jit(solution)/shard_map/all_to_all | solution.py:30
  61.7 1.2 multiply_reduce_fusion.1
  63.1 48.2 %all-to-all-done = bf16[8,1024,2,128]{1,3,2,0:T(8,128)(2,1)} async-done(((bf16[8,1024,2,128]{1,3,2,0:T(8,128)(2,1)}), bf16[8,1024,2,128]{1,3,2,0:T(8,128)(2,1)}, u32[]{:S(2)}, u32[]{:S(2)}) %all-to-all-start) | async-done | bytes 4194336 | tf_op jit(solution)/shard_map/all_to_all | solution.py:30
  111.3 3.2 %convert_reduce_fusion = f32[1024,2,128]{0,2,1:T(8,128)S(1)} fusion(bf16[8,1024,2,128]{1,3,2,0:T(8,128)(2,1)} %all-to-all-done), kind=kLoop, calls=%fused_computation | loop fusion | flops 3932160 | bytes 5242880 | tf_op jit(solution)/shard_map/reduce_sum | solution.py:228
  114.4 0.7 slice.83
  115.2 0.8 slice.82
  116.0 1.2 copy.66
  117.3 1.8 copy.67
  119.5 0.7 copy-done.6
  120.2 1.8 pad_maximum_fusion
  122.0 1.9 collective-permute-start
  123.9 1.3 pad_dynamic-slice_fusion
  125.3 0.7 dynamic_slice.6
  125.9 1.0 copy.51.qseg_ref
  127.0 1.0 copy.45
  128.0 2.4 mul.204
  130.4 1.0 copy-done.1
  131.4 1.0 fusion.10.q_ref
  132.8 1.1 maximum_maximum_fusion
  134.0 1.1 slice_bitcast_fusion.1
  135.0 14.9 %shard_map.125 = (bf16[1024,256]{1,0:T(8,128)(2,1)}, f32[1024,256]{1,0:T(8,128)}, f32[2,2048,128]{2,1,0:T(8,128)}) custom-call(bf16[1024,256]{1,0:T(8,128)(2,1)} %fusion.10.q_ref, bf16[1024,256]{1,0:T(8,128)(2,1)} %do_ref.1, bf16[2048,128]{1,0:T(8,128)(2,1)} %get-tuple-element.44.k_ref, bf16[2048,128]{1,0:T(8,128)(2,1)} %get-tuple-element.43.v_ref, ...), custom_call_target="tpu_custom_call" | custom-call | flops 6442450944 | bytes 8388608 | tf_op jit(solution)/shard_map/pallas_call | solution.py:196
  149.9 1.3 slice.108
  151.2 3.4 %collective-permute-start.1 = (bf16[2,1024,1,128]{3,1,2,0:T(8,128)(2,1)S(1)}, bf16[2,1024,1,128]{3,1,2,0:T(8,128)(2,1)S(1)}, u32[]{:S(2)}, u32[]{:S(2)}) collective-permute-start(bf16[2,1024,1,128]{3,1,2,0:T(8,128)(2,1)S(1)} %slice.108), channel_id=1, source_target_pairs={{8,0},{16,8},{24,16},{32,24},{40,32},{48,40},{56,48},{64,56},{72,6... | collective-permute-start | bytes 1572872 | tf_op jit(solution)/shard_map/ppermute | solution.py:21
  154.6 6.5 %collective-permute-done.1 = bf16[2,1024,1,128]{3,1,2,0:T(8,128)(2,1)S(1)} collective-permute-done((bf16[2,1024,1,128]{3,1,2,0:T(8,128)(2,1)S(1)}, bf16[2,1024,1,128]{3,1,2,0:T(8,128)(2,1)S(1)}, u32[]{:S(2)}, u32[]{:S(2)}) %collective-permute-start.1) | collective-permute-done | bytes 524320 | tf_op jit(solution)/shard_map/ppermute | solution.py:21
  161.1 1.3 slice_add_fusion
  163.1 2.8 broadcast_in_dim.18
  165.8 4.6 %all-to-all-start.1 = ((bf16[8,1024,2,128]{3,1,2,0:T(8,128)(2,1)}), bf16[8,1024,2,128]{3,1,2,0:T(8,128)(2,1)}, u32[]{:S(2)}, u32[]{:S(2)}) async-start(bf16[8,1024,2,128]{3,1,2,0:T(8,128)(2,1)} %broadcast_in_dim.18), calls=%async_computation.1 | async-start | bytes 8388608 | tf_op jit(solution)/shard_map/all_to_all | solution.py:30
  170.4 47.7 %all-to-all-done.1 = bf16[8,1024,2,128]{3,1,2,0:T(8,128)(2,1)} async-done(((bf16[8,1024,2,128]{3,1,2,0:T(8,128)(2,1)}), bf16[8,1024,2,128]{3,1,2,0:T(8,128)(2,1)}, u32[]{:S(2)}, u32[]{:S(2)}) %all-to-all-start.1) | async-done | bytes 4194336 | tf_op jit(solution)/shard_map/all_to_all | solution.py:30
  218.1 6.6 %convert_bitcast_fusion = bf16[672,2,8,128]{3,0,1,2:T(8,128)(2,1)} fusion(bf16[8,1024,2,128]{3,1,2,0:T(8,128)(2,1)} %all-to-all-done.1, bf16[1024,672]{0,1:T(8,128)(2,1)S(1)} %copy-done), kind=kOutput, calls=%fused_computation.7 | convolution fusion | flops 2819948544 | bytes 8323072 | tf_op jit(solution)/shard_map/tf,htkc->fkhc/dot_general | solution.py:271
  224.7 4.6 %copy.55 = bf16[672,2,8,128]{0,3,2,1:T(8,128)(2,1)} copy(bf16[672,2,8,128]{3,0,1,2:T(8,128)(2,1)} %convert_bitcast_fusion) | data formatting | bytes 5505024 | tf_op jit(solution)/shard_map/convert_element_type | solution.py:273
  229.3 2.2 copy.56
  231.4 1.3 select_bitcast_fusion
  232.8 3.0 %collective-permute-start.2 = (bf16[16,672,2,32]{1,3,2,0:T(8,128)(2,1)}, bf16[16,672,2,32]{1,3,2,0:T(8,128)(2,1)}, u32[]{:S(2)}, u32[]{:S(2)}) collective-permute-start(bf16[16,672,2,32]{1,3,2,0:T(8,128)(2,1)} %select_bitcast_fusion), channel_id=1, source_target_pairs={{0,8},{8,0},{1,9},{9,1},{2,10},{10,2},{3,11},{11,3},{4,12},{12,4},... | collective-permute-start | bytes 4128776 | tf_op jit(solution)/shard_map/ppermute | solution.py:124
  235.8 3.4 %collective-permute-done.2 = bf16[16,672,2,32]{1,3,2,0:T(8,128)(2,1)} collective-permute-done((bf16[16,672,2,32]{1,3,2,0:T(8,128)(2,1)}, bf16[16,672,2,32]{1,3,2,0:T(8,128)(2,1)}, u32[]{:S(2)}, u32[]{:S(2)}) %collective-permute-start.2) | collective-permute-done | bytes 1376288 | tf_op jit(solution)/shard_map/ppermute | solution.py:124
  239.2 3.6 %add_convert_fusion = bf16[16,672,2,32]{1,3,2,0:T(8,128)(2,1)} fusion(bf16[16,672,2,32]{1,3,2,0:T(8,128)(2,1)} %collective-permute-done.2, pred[]{:T(512)S(6)} %and.14, bf16[16,2,672,2,32]{2,4,1,0,3:T(8,128)(2,1)} %bitcast.93, s32[]{:T(128)S(6)} %select_n.21), kind=kLoop, calls=%fused_computation.5 | loop fusion | flops 3440640 | bytes 4521989 | tf_op jit(solution)/shard_map/convert_element_type | solution.py:125
  242.8 11.3 %all-to-all-start.2 = ((bf16[16,672,2,32]{1,3,2,0:T(8,128)(2,1)}), bf16[16,672,2,32]{1,3,2,0:T(8,128)(2,1)}, u32[]{:S(2)}, u32[]{:S(2)}) async-start(bf16[16,672,2,32]{1,3,2,0:T(8,128)(2,1)} %add_convert_fusion), calls=%async_computation.2 | async-start | bytes 3145728 | tf_op jit(solution)/shard_map/all_to_all | solution.py:30
  254.2 2.7 reshape.292
  256.9 2.4 multiply_reduce_fusion
  259.8 1.2 broadcast_in_dim.19
  261.0 2.4 fusion.7
  263.4 6.4 %bitcast_convert_fusion = bf16[1024,672]{0,1:T(8,128)(2,1)} fusion(bf16[8,1024,2,128]{3,1,2,0:T(8,128)(2,1)} %all-to-all-done.1, bf16[2,8,128,672]{3,2,1,0:T(8,128)(2,1)S(1)} %bitcast.101), kind=kOutput, calls=%fused_computation.6 | convolution fusion | flops 2819260416 | bytes 8323072 | tf_op jit(solution)/shard_map/htkc,khcf->tf/dot_general | solution.py:268
  269.8 25.5 %all-to-all-done.2 = bf16[16,672,2,32]{1,3,2,0:T(8,128)(2,1)} async-done(((bf16[16,672,2,32]{1,3,2,0:T(8,128)(2,1)}), bf16[16,672,2,32]{1,3,2,0:T(8,128)(2,1)}, u32[]{:S(2)}, u32[]{:S(2)}) %all-to-all-start.2) | async-done | bytes 1376288 | tf_op jit(solution)/shard_map/all_to_all | solution.py:30
  295.3 1.7 convert_reduce_fusion.1
  297.0 0.7 slice_bitcast_fusion.3
  (36 shorter events, 2.7 us)
Async XLA Ops:
  0.6 43.6 %copy-start = (bf16[1024,672]{0,1:T(8,128)(2,1)S(1)}, bf16[1024,672]{0,1:T(8,128)(2,1)}, u32[]{:S(2)}) copy-start(bf16[1024,672]{0,1:T(8,128)(2,1)} %param.14) | copy-start | bytes 4128772
  52.2 9.0 %copy-start.3 = (bf16[1024,256]{1,0:T(8,128)(2,1)S(1)}, bf16[1024,256]{1,0:T(8,128)(2,1)}, u32[]{:S(2)}) copy-start(bf16[1024,256]{1,0:T(8,128)(2,1)} %param.15) | copy-start | bytes 1572868
  52.2 59.0 %all-to-all-start = ((bf16[8,1024,2,128]{1,3,2,0:T(8,128)(2,1)}), bf16[8,1024,2,128]{1,3,2,0:T(8,128)(2,1)}, u32[]{:S(2)}, u32[]{:S(2)}) async-start(bf16[8,1024,2,128]{1,3,2,0:T(8,128)(2,1)} %bitcast.94), calls=%async_computation | async-start | bytes 8388608 | tf_op jit(solution)/shard_map/all_to_all | solution.py:30
  114.4 4.9 %copy-start.8 = (f32[128]{0:T(128)S(1)}, f32[128]{0:T(128)}, u32[]{:S(2)}) copy-start(f32[128]{0:T(128)} %param.19) | copy-start | bytes 1540
  116.0 12.0 %copy-start.9 = (f32[128]{0:T(128)S(1)}, f32[128]{0:T(128)}, u32[]{:S(2)}) copy-start(f32[128]{0:T(128)} %param.18) | copy-start | bytes 1540
  119.5 0.7 copy-start.6
  122.0 10.8 %collective-permute-start = (bf16[2,1024,1,128]{3,1,2,0:T(8,128)(2,1)}, bf16[2,1024,1,128]{3,1,2,0:T(8,128)(2,1)}, u32[]{:S(2)}, u32[]{:S(2)}) collective-permute-start(bf16[2,1024,1,128]{3,1,2,0:T(8,128)(2,1)} %pad_maximum_fusion), channel_id=1, source_target_pairs={{0,8},{8,16},{16,24},{24,32},{32,40},{40,48},{48,56},{56,64},{64,7... | collective-permute-start | bytes 1572872 | tf_op jit(solution)/shard_map/ppermute | solution.py:21
  128.0 4.8 %copy-start.5 = (bf16[1024,1,128]{2,0,1:T(8,128)(2,1)S(1)}, bf16[1024,1,128]{2,0,1:T(8,128)(2,1)}, u32[]{:S(2)}) copy-start(bf16[1024,1,128]{2,0,1:T(8,128)(2,1)} %copy.67) | copy-start | bytes 786436
  128.0 4.8 %copy-start.7 = (bf16[1,1024,1,128]{3,1,2,0:T(8,128)(2,1)S(1)}, bf16[1,1024,1,128]{3,1,2,0:T(8,128)(2,1)}, u32[]{:S(2)}) copy-start(bf16[1,1024,1,128]{3,1,2,0:T(8,128)(2,1)} %copy-done.6) | copy-start | bytes 786436
  130.4 1.0 copy-start.1
  151.2 9.9 %collective-permute-start.1 = (bf16[2,1024,1,128]{3,1,2,0:T(8,128)(2,1)S(1)}, bf16[2,1024,1,128]{3,1,2,0:T(8,128)(2,1)S(1)}, u32[]{:S(2)}, u32[]{:S(2)}) collective-permute-start(bf16[2,1024,1,128]{3,1,2,0:T(8,128)(2,1)S(1)} %slice.108), channel_id=1, source_target_pairs={{8,0},{16,8},{24,16},{32,24},{40,32},{48,40},{56,48},{64,56},{72,6... | collective-permute-start | bytes 1572872 | tf_op jit(solution)/shard_map/ppermute | solution.py:21
  165.8 52.2 %all-to-all-start.1 = ((bf16[8,1024,2,128]{3,1,2,0:T(8,128)(2,1)}), bf16[8,1024,2,128]{3,1,2,0:T(8,128)(2,1)}, u32[]{:S(2)}, u32[]{:S(2)}) async-start(bf16[8,1024,2,128]{3,1,2,0:T(8,128)(2,1)} %broadcast_in_dim.18), calls=%async_computation.1 | async-start | bytes 8388608 | tf_op jit(solution)/shard_map/all_to_all | solution.py:30
  232.8 6.4 %collective-permute-start.2 = (bf16[16,672,2,32]{1,3,2,0:T(8,128)(2,1)}, bf16[16,672,2,32]{1,3,2,0:T(8,128)(2,1)}, u32[]{:S(2)}, u32[]{:S(2)}) collective-permute-start(bf16[16,672,2,32]{1,3,2,0:T(8,128)(2,1)} %select_bitcast_fusion), channel_id=1, source_target_pairs={{0,8},{8,0},{1,9},{9,1},{2,10},{10,2},{3,11},{11,3},{4,12},{12,4},... | collective-permute-start | bytes 4128776 | tf_op jit(solution)/shard_map/ppermute | solution.py:124
  242.8 52.5 %all-to-all-start.2 = ((bf16[16,672,2,32]{1,3,2,0:T(8,128)(2,1)}), bf16[16,672,2,32]{1,3,2,0:T(8,128)(2,1)}, u32[]{:S(2)}, u32[]{:S(2)}) async-start(bf16[16,672,2,32]{1,3,2,0:T(8,128)(2,1)} %add_convert_fusion), calls=%async_computation.2 | async-start | bytes 3145728 | tf_op jit(solution)/shard_map/all_to_all | solution.py:30
  259.3 1.7 copy-start.2
  259.8 3.6 %copy-start.4 = (bf16[2,32,32,672]{3,2,1,0:T(8,128)(2,1)S(1)}, bf16[2,32,32,672]{3,2,1,0:T(8,128)(2,1)}, u32[]{:S(2)}) copy-start(bf16[2,32,32,672]{3,2,1,0:T(8,128)(2,1)} %shard_map.124) | copy-start | bytes 8257540

commit v6 on v5

--- a/solution.py
+++ b/solution.py
@@ -116,13 +116,14 @@
 
 
 def reduce_seq(blocks):
-    chips = blocks.shape[0] // 2
-    split = blocks.reshape((chips, 2) + blocks.shape[1:])
+    chips = blocks.shape[1] // 2
+    split = blocks.reshape((blocks.shape[0], chips, 2) + blocks.shape[2:])
     core = lax.axis_index("core")
-    keep = jnp.take(split, core, axis=1)
-    send = jnp.take(split, 1 - core, axis=1)
+    keep = jnp.take(split, core, axis=2)
+    send = jnp.take(split, 1 - core, axis=2)
     pair = (keep.astype(jnp.float32) + lax.ppermute(send, "core", SWAP).astype(jnp.float32))
-    return jnp.sum(exchange(pair.astype(jnp.bfloat16), "chip").astype(jnp.float32), axis=0)
+    pair = pair.astype(jnp.bfloat16).transpose(1, 0, 2, 3)
+    return jnp.sum(exchange(pair, "chip").astype(jnp.float32), axis=0)
 
 
 def attend_block(
@@ -269,12 +270,11 @@
         "htkc,khcf->tf", grads_all, weight_heads, preferred_element_type=jnp.float32
     ).astype(jnp.bfloat16)
     weight_part = jnp.einsum(
-        "tf,htkc->fkhc", normed, grads_all, preferred_element_type=jnp.float32
+        "htkc,tf->khcf", grads_all, normed, preferred_element_type=jnp.float32
     ).astype(jnp.bfloat16)
-    to_owner = weight_part.reshape(feats, 2, n_seq, col_block).transpose(2, 0, 1, 3)
-    summed = reduce_seq(to_owner)
-    grad_key_weight = summed[:, 0]
-    grad_value_weight = summed[:, 1]
+    summed = reduce_seq(weight_part.reshape(2, n_seq, col_block, feats))
+    grad_key_weight = summed[0].T
+    grad_value_weight = summed[1].T
     return (attention, grad_normed, grad_q, grad_key_weight, grad_value_weight)
 
 

time: 299 us -> 298 us (level)
    convert_element_type x1 -> x0, other arithmetic: 3.65 us -> none  [reduce_seq(): pair.astype(jnp.bfloat16)]
where the time goes in v6:
time: 298 us; the launch traced here: 297 us
  waiting for transfers between devices  132 us (44%)
  Pallas kernels  56.9 us (19%)
  starting transfers between devices  33.2 us (11%)
  local copies, waits for them, and re-layouts  32 us (11%)
  other arithmetic  23.7 us (8%)
  matrix products  18.5 us (6%)
    all_to_all x3, waiting for transfers between devices, exchange(): return lax.all_to_all(blocks, axis, 0, 0)  121 us
    pallas_call x1, Pallas kernels, gather_seq(): pl.pallas_call(functools.partial(gather_kernel, chips), out_shape=jax.Sha...  41.9 us
    all_to_all x3, starting transfers between devices, exchange(): return lax.all_to_all(blocks, axis, 0, 0)  24.8 us
    pallas_call x1, Pallas kernels, attend(): pl.pallas_call(attention_kernel, out_shape=(jax.ShapeDtypeStruct((rows, 2...  14.9 us
    ppermute x2, waiting for transfers between devices, from_behind(): return lax.ppermute(array, axis, pairs)  6.88 us
    dot_general x1, matrix products, body(): jnp.einsum('htkc,tf->khcf', grads_all, normed, preferred_element_type=jnp...  6.58 us
    dot_general x1, matrix products, body(): jnp.einsum('htkc,khcf->tf', grads_all, weight_heads, preferred_element_ty...  6.38 us
  transfers between devices with their start and end apart: 6, of which 6 were waited for; matrix products, arithmetic and copies ran while one was open for 8% of the time, Pallas kernels for 0%

profile of v6, /device:TPU:2, one launch (start us, length us, event | category | flops | bytes accessed | tf_op | source)
XLA Modules:
  0.0 296.9 jit_solution(15633355317958436016)
XLA Ops:
  0.6 1.6 maximum_bitcast_fusion.x_ref
  2.2 41.9 %shard_map.124 = bf16[2,32,32,672]{3,2,1,0:T(8,128)(2,1)} custom-call(bf16[2,1,32,672]{3,2,1,0:T(8,128)(2,1)} %maximum_bitcast_fusion.x_ref), custom_call_target="tpu_custom_call" | custom-call | tf_op jit(solution)/shard_map/pallas_call | solution.py:102
  44.2 5.5 %convolution_convert_fusion = bf16[2,1024,1024]{2,1,0:T(8,128)(2,1)S(1)} fusion(bf16[2,1024,672]{2,1,0:T(8,128)(2,1)} %bitcast.106, bf16[1024,672]{0,1:T(8,128)(2,1)S(1)} %copy-done), kind=kOutput, calls=%fused_computation.8 | convolution fusion | flops 2820669440 | bytes 8323072 | tf_op jit(solution)/shard_map/dot_general | solution.py:224
  49.7 2.5 copy.76
  52.2 9.0 %all-to-all-start = ((bf16[8,1024,2,128]{1,3,2,0:T(8,128)(2,1)}), bf16[8,1024,2,128]{1,3,2,0:T(8,128)(2,1)}, u32[]{:S(2)}, u32[]{:S(2)}) async-start(bf16[8,1024,2,128]{1,3,2,0:T(8,128)(2,1)} %bitcast.99), calls=%async_computation | async-start | bytes 8388608 | tf_op jit(solution)/shard_map/all_to_all | solution.py:30
  61.7 1.2 multiply_reduce_fusion.1
  63.1 48.2 %all-to-all-done = bf16[8,1024,2,128]{1,3,2,0:T(8,128)(2,1)} async-done(((bf16[8,1024,2,128]{1,3,2,0:T(8,128)(2,1)}), bf16[8,1024,2,128]{1,3,2,0:T(8,128)(2,1)}, u32[]{:S(2)}, u32[]{:S(2)}) %all-to-all-start) | async-done | bytes 4194336 | tf_op jit(solution)/shard_map/all_to_all | solution.py:30
  111.3 3.2 %convert_reduce_fusion = f32[1024,2,128]{0,2,1:T(8,128)S(1)} fusion(bf16[8,1024,2,128]{1,3,2,0:T(8,128)(2,1)} %all-to-all-done), kind=kLoop, calls=%fused_computation | loop fusion | flops 3932160 | bytes 5242880 | tf_op jit(solution)/shard_map/reduce_sum | solution.py:229
  114.5 0.7 slice.83
  115.2 0.8 slice.82
  116.1 1.2 copy.64
  117.3 1.8 copy.65
  119.6 0.7 copy-done.6
  120.2 1.8 pad_maximum_fusion
  122.0 1.9 collective-permute-start
  123.9 1.3 pad_dynamic-slice_fusion
  125.3 0.7 dynamic_slice.6
  125.9 1.1 copy.50.qseg_ref
  127.0 1.0 copy.44
  128.0 2.4 mul.204
  130.5 1.0 copy-done.1
  131.5 1.0 fusion.11.q_ref
  132.8 1.1 maximum_maximum_fusion
  134.0 1.0 slice_bitcast_fusion.1
  135.0 14.9 %shard_map.125 = (bf16[1024,256]{1,0:T(8,128)(2,1)}, f32[1024,256]{1,0:T(8,128)}, f32[2,2048,128]{2,1,0:T(8,128)}) custom-call(bf16[1024,256]{1,0:T(8,128)(2,1)} %fusion.11.q_ref, bf16[1024,256]{1,0:T(8,128)(2,1)} %do_ref.1, bf16[2048,128]{1,0:T(8,128)(2,1)} %get-tuple-element.44.k_ref, bf16[2048,128]{1,0:T(8,128)(2,1)} %get-tuple-element.43.v_ref, ...), custom_call_target="tpu_custom_call" | custom-call | flops 6442450944 | bytes 8388608 | tf_op jit(solution)/shard_map/pallas_call | solution.py:197
  149.9 1.3 slice.108
  151.2 3.4 %collective-permute-start.1 = (bf16[2,1024,1,128]{3,1,2,0:T(8,128)(2,1)S(1)}, bf16[2,1024,1,128]{3,1,2,0:T(8,128)(2,1)S(1)}, u32[]{:S(2)}, u32[]{:S(2)}) collective-permute-start(bf16[2,1024,1,128]{3,1,2,0:T(8,128)(2,1)S(1)} %slice.108), channel_id=1, source_target_pairs={{8,0},{16,8},{24,16},{32,24},{40,32},{48,40},{56,48},{64,56},{72,6... | collective-permute-start | bytes 1572872 | tf_op jit(solution)/shard_map/ppermute | solution.py:21
  154.7 6.5 %collective-permute-done.1 = bf16[2,1024,1,128]{3,1,2,0:T(8,128)(2,1)S(1)} collective-permute-done((bf16[2,1024,1,128]{3,1,2,0:T(8,128)(2,1)S(1)}, bf16[2,1024,1,128]{3,1,2,0:T(8,128)(2,1)S(1)}, u32[]{:S(2)}, u32[]{:S(2)}) %collective-permute-start.1) | collective-permute-done | bytes 524320 | tf_op jit(solution)/shard_map/ppermute | solution.py:21
  161.1 1.3 slice_add_fusion
  163.1 2.8 broadcast_in_dim.18
  165.9 4.6 %all-to-all-start.1 = ((bf16[8,1024,2,128]{3,1,2,0:T(8,128)(2,1)}), bf16[8,1024,2,128]{3,1,2,0:T(8,128)(2,1)}, u32[]{:S(2)}, u32[]{:S(2)}) async-start(bf16[8,1024,2,128]{3,1,2,0:T(8,128)(2,1)} %broadcast_in_dim.18), calls=%async_computation.1 | async-start | bytes 8388608 | tf_op jit(solution)/shard_map/all_to_all | solution.py:30
  170.5 47.7 %all-to-all-done.1 = bf16[8,1024,2,128]{3,1,2,0:T(8,128)(2,1)} async-done(((bf16[8,1024,2,128]{3,1,2,0:T(8,128)(2,1)}), bf16[8,1024,2,128]{3,1,2,0:T(8,128)(2,1)}, u32[]{:S(2)}, u32[]{:S(2)}) %all-to-all-start.1) | async-done | bytes 4194336 | tf_op jit(solution)/shard_map/all_to_all | solution.py:30
  218.1 6.6 %convert_bitcast_fusion = bf16[2,8,128,672]{2,3,0,1:T(8,128)(2,1)} fusion(bf16[8,1024,2,128]{3,1,2,0:T(8,128)(2,1)} %all-to-all-done.1, bf16[1024,672]{0,1:T(8,128)(2,1)S(1)} %copy-done), kind=kOutput, calls=%fused_computation.7 | convolution fusion | flops 2819948544 | bytes 8323072 | tf_op jit(solution)/shard_map/htkc,tf->khcf/dot_general | solution.py:272
  224.7 4.6 %copy.54 = bf16[2,8,128,672]{3,2,1,0:T(8,128)(2,1)} copy(bf16[2,8,128,672]{2,3,0,1:T(8,128)(2,1)} %convert_bitcast_fusion) | data formatting | bytes 5505024 | tf_op jit(solution)/shard_map/convert_element_type | solution.py:274
  229.3 2.7 select_bitcast_fusion
  232.0 3.0 %collective-permute-start.2 = (bf16[2,16,32,672]{3,2,1,0:T(8,128)(2,1)}, bf16[2,16,32,672]{3,2,1,0:T(8,128)(2,1)}, u32[]{:S(2)}, u32[]{:S(2)}) collective-permute-start(bf16[2,16,32,672]{3,2,1,0:T(8,128)(2,1)} %select_bitcast_fusion), channel_id=1, source_target_pairs={{0,8},{8,0},{1,9},{9,1},{2,10},{10,2},{3,11},{11,3},{4,12},{12,4},... | collective-permute-start | bytes 4128776 | tf_op jit(solution)/shard_map/ppermute | solution.py:124
  235.1 3.4 %collective-permute-done.2 = bf16[2,16,32,672]{3,2,1,0:T(8,128)(2,1)} collective-permute-done((bf16[2,16,32,672]{3,2,1,0:T(8,128)(2,1)}, bf16[2,16,32,672]{3,2,1,0:T(8,128)(2,1)}, u32[]{:S(2)}, u32[]{:S(2)}) %collective-permute-start.2) | collective-permute-done | bytes 1376288 | tf_op jit(solution)/shard_map/ppermute | solution.py:124
  238.4 2.4 fusion.4
  240.9 1.2 copy.56
  242.1 11.3 %all-to-all-start.2 = ((bf16[16,2,32,672]{3,2,1,0:T(8,128)(2,1)}), bf16[16,2,32,672]{3,2,1,0:T(8,128)(2,1)}, u32[]{:S(2)}, u32[]{:S(2)}) async-start(bf16[16,2,32,672]{3,2,1,0:T(8,128)(2,1)} %copy.56), calls=%async_computation.2 | async-start | bytes 3145728 | tf_op jit(solution)/shard_map/all_to_all | solution.py:30
  253.4 2.7 reshape.286
  256.1 2.4 multiply_reduce_fusion
  259.0 1.2 broadcast_in_dim.19
  260.3 2.4 fusion.8
  262.7 6.4 %bitcast_convert_fusion = bf16[1024,672]{0,1:T(8,128)(2,1)} fusion(bf16[8,1024,2,128]{3,1,2,0:T(8,128)(2,1)} %all-to-all-done.1, bf16[2,8,128,672]{3,2,1,0:T(8,128)(2,1)S(1)} %bitcast.107), kind=kOutput, calls=%fused_computation.6 | convolution fusion | flops 2819260416 | bytes 8323072 | tf_op jit(solution)/shard_map/htkc,khcf->tf/dot_general | solution.py:269
  269.0 25.5 %all-to-all-done.2 = bf16[16,2,32,672]{3,2,1,0:T(8,128)(2,1)} async-done(((bf16[16,2,32,672]{3,2,1,0:T(8,128)(2,1)}), bf16[16,2,32,672]{3,2,1,0:T(8,128)(2,1)}, u32[]{:S(2)}, u32[]{:S(2)}) %all-to-all-start.2) | async-done | bytes 1376288 | tf_op jit(solution)/shard_map/all_to_all | solution.py:30
  294.6 1.7 convert_reduce_fusion.1
  296.2 0.7 slice_bitcast_fusion.3
  (36 shorter events, 2.7 us)
Async XLA Ops:
  0.6 43.5 %copy-start = (bf16[1024,672]{0,1:T(8,128)(2,1)S(1)}, bf16[1024,672]{0,1:T(8,128)(2,1)}, u32[]{:S(2)}) copy-start(bf16[1024,672]{0,1:T(8,128)(2,1)} %param.14) | copy-start | bytes 4128772
  52.2 9.0 %copy-start.3 = (bf16[1024,256]{1,0:T(8,128)(2,1)S(1)}, bf16[1024,256]{1,0:T(8,128)(2,1)}, u32[]{:S(2)}) copy-start(bf16[1024,256]{1,0:T(8,128)(2,1)} %param.15) | copy-start | bytes 1572868
  52.2 59.0 %all-to-all-start = ((bf16[8,1024,2,128]{1,3,2,0:T(8,128)(2,1)}), bf16[8,1024,2,128]{1,3,2,0:T(8,128)(2,1)}, u32[]{:S(2)}, u32[]{:S(2)}) async-start(bf16[8,1024,2,128]{1,3,2,0:T(8,128)(2,1)} %bitcast.99), calls=%async_computation | async-start | bytes 8388608 | tf_op jit(solution)/shard_map/all_to_all | solution.py:30
  114.5 4.9 %copy-start.8 = (f32[128]{0:T(128)S(1)}, f32[128]{0:T(128)}, u32[]{:S(2)}) copy-start(f32[128]{0:T(128)} %param.19) | copy-start | bytes 1540
  116.1 12.0 %copy-start.9 = (f32[128]{0:T(128)S(1)}, f32[128]{0:T(128)}, u32[]{:S(2)}) copy-start(f32[128]{0:T(128)} %param.18) | copy-start | bytes 1540
  119.5 0.7 copy-start.6
  122.0 10.8 %collective-permute-start = (bf16[2,1024,1,128]{3,1,2,0:T(8,128)(2,1)}, bf16[2,1024,1,128]{3,1,2,0:T(8,128)(2,1)}, u32[]{:S(2)}, u32[]{:S(2)}) collective-permute-start(bf16[2,1024,1,128]{3,1,2,0:T(8,128)(2,1)} %pad_maximum_fusion), channel_id=1, source_target_pairs={{0,8},{8,16},{16,24},{24,32},{32,40},{40,48},{48,56},{56,64},{64,7... | collective-permute-start | bytes 1572872 | tf_op jit(solution)/shard_map/ppermute | solution.py:21
  128.0 4.8 %copy-start.5 = (bf16[1024,1,128]{2,0,1:T(8,128)(2,1)S(1)}, bf16[1024,1,128]{2,0,1:T(8,128)(2,1)}, u32[]{:S(2)}) copy-start(bf16[1024,1,128]{2,0,1:T(8,128)(2,1)} %copy.65) | copy-start | bytes 786436
  128.0 4.8 %copy-start.7 = (bf16[1,1024,1,128]{3,1,2,0:T(8,128)(2,1)S(1)}, bf16[1,1024,1,128]{3,1,2,0:T(8,128)(2,1)}, u32[]{:S(2)}) copy-start(bf16[1,1024,1,128]{3,1,2,0:T(8,128)(2,1)} %copy-done.6) | copy-start | bytes 786436
  130.5 1.0 copy-start.1
  151.2 9.9 %collective-permute-start.1 = (bf16[2,1024,1,128]{3,1,2,0:T(8,128)(2,1)S(1)}, bf16[2,1024,1,128]{3,1,2,0:T(8,128)(2,1)S(1)}, u32[]{:S(2)}, u32[]{:S(2)}) collective-permute-start(bf16[2,1024,1,128]{3,1,2,0:T(8,128)(2,1)S(1)} %slice.108), channel_id=1, source_target_pairs={{8,0},{16,8},{24,16},{32,24},{40,32},{48,40},{56,48},{64,56},{72,6... | collective-permute-start | bytes 1572872 | tf_op jit(solution)/shard_map/ppermute | solution.py:21
  165.9 52.3 %all-to-all-start.1 = ((bf16[8,1024,2,128]{3,1,2,0:T(8,128)(2,1)}), bf16[8,1024,2,128]{3,1,2,0:T(8,128)(2,1)}, u32[]{:S(2)}, u32[]{:S(2)}) async-start(bf16[8,1024,2,128]{3,1,2,0:T(8,128)(2,1)} %broadcast_in_dim.18), calls=%async_computation.1 | async-start | bytes 8388608 | tf_op jit(solution)/shard_map/all_to_all | solution.py:30
  232.0 6.4 %collective-permute-start.2 = (bf16[2,16,32,672]{3,2,1,0:T(8,128)(2,1)}, bf16[2,16,32,672]{3,2,1,0:T(8,128)(2,1)}, u32[]{:S(2)}, u32[]{:S(2)}) collective-permute-start(bf16[2,16,32,672]{3,2,1,0:T(8,128)(2,1)} %select_bitcast_fusion), channel_id=1, source_target_pairs={{0,8},{8,0},{1,9},{9,1},{2,10},{10,2},{3,11},{11,3},{4,12},{12,4},... | collective-permute-start | bytes 4128776 | tf_op jit(solution)/shard_map/ppermute | solution.py:124
  242.1 52.4 %all-to-all-start.2 = ((bf16[16,2,32,672]{3,2,1,0:T(8,128)(2,1)}), bf16[16,2,32,672]{3,2,1,0:T(8,128)(2,1)}, u32[]{:S(2)}, u32[]{:S(2)}) async-start(bf16[16,2,32,672]{3,2,1,0:T(8,128)(2,1)} %copy.56), calls=%async_computation.2 | async-start | bytes 3145728 | tf_op jit(solution)/shard_map/all_to_all | solution.py:30
  258.6 1.7 copy-start.2
  259.0 3.6 %copy-start.4 = (bf16[2,32,32,672]{3,2,1,0:T(8,128)(2,1)S(1)}, bf16[2,32,32,672]{3,2,1,0:T(8,128)(2,1)}, u32[]{:S(2)}) copy-start(bf16[2,32,32,672]{3,2,1,0:T(8,128)(2,1)} %shard_map.124) | copy-start | bytes 8257540

commit v7 on v6

--- a/solution.py
+++ b/solution.py
@@ -115,6 +115,54 @@
     )(block[:, None])
 
 
+def uly_kernel(count, scatter, x_ref, out_ref, local_sem, send_sem, recv_sem):
+    chip = lax.axis_index("chip")
+    core = lax.axis_index("core")
+    me = lax.axis_index("uly")
+    mesh_ids = pl.DeviceIdType.MESH
+    barrier = pltpu.get_barrier_semaphore()
+    for d in range(1, count):
+        peer = (chip, core, lax.rem(me + d, count))
+        pl.semaphore_signal(barrier, 1, device_id=peer, device_id_type=mesh_ids)
+    pl.semaphore_wait(barrier, count - 1)
+    local = pltpu.make_async_copy(x_ref.at[me] if scatter else x_ref, out_ref.at[me], local_sem)
+    local.start()
+    sends = []
+    for d in range(1, count):
+        target = lax.rem(me + d, count)
+        send = pltpu.make_async_remote_copy(
+            src_ref=x_ref.at[target] if scatter else x_ref,
+            dst_ref=out_ref.at[me],
+            send_sem=send_sem.at[d],
+            recv_sem=recv_sem.at[d],
+            device_id=(chip, core, target),
+            device_id_type=mesh_ids,
+        )
+        send.start()
+        sends.append(send)
+    for send in sends:
+        send.wait()
+    local.wait()
+
+
+def exchange_uly(x, scatter, kernel_id):
+    count = lax.axis_size("uly")
+    block = x.shape[1:] if scatter else x.shape
+    spec = pl.BlockSpec(memory_space=pltpu.VMEM)
+    return pl.pallas_call(
+        functools.partial(uly_kernel, count, scatter),
+        out_shape=jax.ShapeDtypeStruct((count,) + block, x.dtype),
+        in_specs=[spec],
+        out_specs=spec,
+        scratch_shapes=[
+            pltpu.SemaphoreType.DMA(()),
+            pltpu.SemaphoreType.DMA((count,)),
+            pltpu.SemaphoreType.DMA((count,)),
+        ],
+        compiler_params=pltpu.CompilerParams(collective_id=kernel_id, has_side_effects=True),
+    )(x)
+
+
 def reduce_seq(blocks):
     chips = blocks.shape[1] // 2
     split = blocks.reshape((blocks.shape[0], chips, 2) + blocks.shape[2:])
@@ -225,7 +273,8 @@
         normed, weight_t, (((1,), (2,)), ((), ())), preferred_element_type=jnp.float32
     ).astype(jnp.bfloat16)
     terms = terms.reshape(rows_here, 2, n_uly, heads_here * HD).transpose(2, 0, 1, 3)
-    received = exchange(terms, "uly")
+    received = exchange_uly(terms.reshape(n_uly, rows_here, 2 * HD), True, 1)
+    received = received.reshape(n_uly, rows_here, 2, HD)
     raw_pair = jnp.sum(received.astype(jnp.float32), axis=0)
     key_raw = raw_pair[:, 0]
     value_raw = raw_pair[:, 1]
@@ -264,7 +313,8 @@
     _, pull_key = jax.vjp(lambda raw_vals: normalize(raw_vals, k_gain, 1.0), key_in)
     key_grad = pull_key(own_grads[0])[0].astype(jnp.bfloat16).reshape(rows_here, heads_here * HD)
     value_grad = own_grads[1].astype(jnp.bfloat16).reshape(rows_here, heads_here * HD)
-    grads_all = gather_all(jnp.stack([key_grad, value_grad], axis=1), "uly")
+    grads_all = exchange_uly(jnp.concatenate([key_grad, value_grad], axis=1), False, 2)
+    grads_all = grads_all.reshape(n_uly, rows_here, 2, heads_here * HD)
     weight_heads = weight_t.reshape(2, n_uly, heads_here * HD, feats)
     grad_normed = jnp.einsum(
         "htkc,khcf->tf", grads_all, weight_heads, preferred_element_type=jnp.float32

time: 298 us -> 316 us (1.060)
  the two profiles are of different devices: /device:TPU:2 before, /device:TPU:32 now
where the time goes in v7:
time: 316 us; the launch traced here: 314 us
  Pallas kernels  167 us (53%)
  local copies, waits for them, and re-layouts  46 us (15%)
  waiting for transfers between devices  35.1 us (11%)
  other arithmetic  24.2 us (8%)
  starting transfers between devices  22 us (7%)
  matrix products  19.5 us (6%)
    pallas_call x2, Pallas kernels, exchange_uly(): pl.pallas_call(functools.partial(uly_kernel, count, scatter), out_shape=j...  106 us
    pallas_call x1, Pallas kernels, gather_seq(): pl.pallas_call(functools.partial(gather_kernel, chips), out_shape=jax.Sha...  45.8 us
    all_to_all x1, waiting for transfers between devices, exchange(): return lax.all_to_all(blocks, axis, 0, 0)  27.8 us
    pallas_call x1, Pallas kernels, attend(): pl.pallas_call(attention_kernel, out_shape=(jax.ShapeDtypeStruct((rows, 2...  14.9 us
    all_to_all x1, starting transfers between devices, exchange(): return lax.all_to_all(blocks, axis, 0, 0)  13.2 us
    reshape x1, local copies, waits for them, and re-layouts, body(): terms.reshape(rows_here, 2, n_uly, heads_here * HD).transpose(2, 0, 1, 3)  11.2 us
    reshape x1, local copies, waits for them, and re-layouts, body(): received = exchange_uly(terms.reshape(n_uly, rows_here, 2 * HD), True, 1)  7.61 us
    dot_general x1, matrix products, body(): lax.dot_general(normed, weight_t, (((1,), (2,)), ((), ())), preferred_ele...  6.97 us
  transfers between devices with their start and end apart: 4, of which 3 were waited for; matrix products, arithmetic and copies ran while one was open for 8% of the time, Pallas kernels for 0%

profile of v7, /device:TPU:32, one launch (start us, length us, event | category | flops | bytes accessed | tf_op | source)
XLA Modules:
  0.0 314.4 jit_solution(17249593872106696392)
XLA Ops:
  0.6 1.6 maximum_bitcast_fusion.x_ref
  2.2 45.8 %shard_map.124 = bf16[2,32,32,672]{3,2,1,0:T(8,128)(2,1)} custom-call(bf16[2,1,32,672]{3,2,1,0:T(8,128)(2,1)} %maximum_bitcast_fusion.x_ref), custom_call_target="tpu_custom_call" | custom-call | tf_op jit(solution)/shard_map/pallas_call | solution.py:102
  48.0 7.0 %convolution_convert_fusion = bf16[2,1024,1024]{2,1,0:T(8,128)(2,1)} fusion(bf16[2,1024,672]{2,1,0:T(8,128)(2,1)} %bitcast.125, bf16[1024,672]{0,1:T(8,128)(2,1)S(1)} %copy-done), kind=kOutput, calls=%fused_computation.12 | convolution fusion | flops 2820669440 | bytes 8323072 | tf_op jit(solution)/shard_map/dot_general | solution.py:272
  55.0 11.2 %copy.58 = bf16[1024,2,8,128]{3,1,0,2:T(2,128)(2,1)} copy(bf16[1024,2,8,128]{0,3,2,1:T(8,128)(2,1)} %bitcast.122) | data formatting | bytes 8388608 | tf_op jit(solution)/shard_map/reshape | solution.py:275
  66.2 7.6 %reshape.286.x_ref = bf16[8,1024,256]{2,1,0:T(8,128)(2,1)} reshape(bf16[8,1024,2,128]{3,2,1,0:T(2,128)(2,1)} %bitcast.116) | data formatting | bytes 8388608 | tf_op jit(solution)/shard_map/reshape | solution.py:276
  73.8 54.3 %shard_map.125 = bf16[8,1024,256]{2,1,0:T(8,128)(2,1)} custom-call(bf16[8,1024,256]{2,1,0:T(8,128)(2,1)} %reshape.286.x_ref), custom_call_target="tpu_custom_call" | custom-call | tf_op jit(solution)/shard_map/pallas_call | solution.py:152
  128.1 2.9 convert_reduce_fusion
  131.0 1.3 copy.59
  132.3 1.1 slice.83
  133.4 1.1 slice.82
  135.4 0.9 pad_maximum_fusion
  136.2 2.1 collective-permute-start
  138.3 0.5 reshape.283
  138.8 2.0 multiply_reduce_fusion.1
  140.8 1.2 copy.55
  142.0 1.3 pad_dynamic-slice_fusion
  143.3 1.0 copy.56
  144.4 0.7 dynamic_slice.6
  145.0 1.0 copy.62.qseg_ref
  146.1 2.4 mul.204
  148.5 1.0 copy-done.1
  149.5 1.0 fusion.20.q_ref
  150.5 1.1 maximum_maximum_fusion
  151.6 1.1 slice_bitcast_fusion.1
  152.6 14.9 %shard_map.126 = (bf16[1024,256]{1,0:T(8,128)(2,1)}, f32[1024,256]{1,0:T(8,128)}, f32[2,2048,128]{2,1,0:T(8,128)}) custom-call(bf16[1024,256]{1,0:T(8,128)(2,1)} %fusion.20.q_ref, bf16[1024,256]{1,0:T(8,128)(2,1)} %do_ref.1, bf16[2048,128]{1,0:T(8,128)(2,1)} %get-tuple-element.44.k_ref, bf16[2048,128]{1,0:T(8,128)(2,1)} %get-tuple-element.43.v_ref, ...), custom_call_target="tpu_custom_call" | custom-call | flops 6442450944 | bytes 8388608 | tf_op jit(solution)/shard_map/pallas_call | solution.py:245
  167.5 2.1 slice.110
  169.6 1.5 collective-permute-start.1
  171.1 4.0 %collective-permute-done.1 = bf16[2,1024,1,128]{3,1,2,0:T(8,128)(2,1)} collective-permute-done((bf16[2,1024,1,128]{3,1,2,0:T(8,128)(2,1)}, bf16[2,1024,1,128]{3,1,2,0:T(8,128)(2,1)}, u32[]{:S(2)}, u32[]{:S(2)}) %collective-permute-start.1) | collective-permute-done | bytes 524320 | tf_op jit(solution)/shard_map/ppermute | solution.py:21
  175.1 1.4 slice_add_fusion
  176.8 0.3 fusion.25
  177.1 0.9 pad_maximum_fusion.1.x_ref
  178.0 51.6 %shard_map.127 = bf16[8,1024,256]{2,1,0:T(8,128)(2,1)} custom-call(bf16[1024,256]{1,0:T(8,128)(2,1)} %pad_maximum_fusion.1.x_ref), custom_call_target="tpu_custom_call" | custom-call | tf_op jit(solution)/shard_map/pallas_call | solution.py:152
  229.6 6.5 %convert_bitcast_fusion = bf16[2,8,128,672]{2,3,0,1:T(8,128)(2,1)} fusion(bf16[1024,672]{0,1:T(8,128)(2,1)S(1)} %copy-done, bf16[8,1024,256]{2,1,0:T(8,128)(2,1)} %shard_map.127), kind=kOutput, calls=%fused_computation.11 | convolution fusion | flops 2819948544 | bytes 8323072 | tf_op jit(solution)/shard_map/htkc,tf->khcf/dot_general | solution.py:322
  236.1 4.6 %copy.68 = bf16[2,8,128,672]{3,2,1,0:T(8,128)(2,1)} copy(bf16[2,8,128,672]{2,3,0,1:T(8,128)(2,1)} %convert_bitcast_fusion) | data formatting | bytes 5505024 | tf_op jit(solution)/shard_map/convert_element_type | solution.py:324
  240.7 2.7 select_bitcast_fusion
  243.4 5.2 %collective-permute-start.2 = (bf16[2,16,32,672]{3,2,1,0:T(8,128)(2,1)}, bf16[2,16,32,672]{3,2,1,0:T(8,128)(2,1)}, u32[]{:S(2)}, u32[]{:S(2)}) collective-permute-start(bf16[2,16,32,672]{3,2,1,0:T(8,128)(2,1)} %select_bitcast_fusion), channel_id=1, source_target_pairs={{0,8},{8,0},{1,9},{9,1},{2,10},{10,2},{3,11},{11,3},{4,12},{12,4},... | collective-permute-start | bytes 4128776 | tf_op jit(solution)/shard_map/ppermute | solution.py:172
  248.6 3.4 %collective-permute-done.2 = bf16[2,16,32,672]{3,2,1,0:T(8,128)(2,1)} collective-permute-done((bf16[2,16,32,672]{3,2,1,0:T(8,128)(2,1)}, bf16[2,16,32,672]{3,2,1,0:T(8,128)(2,1)}, u32[]{:S(2)}, u32[]{:S(2)}) %collective-permute-start.2) | collective-permute-done | bytes 1376288 | tf_op jit(solution)/shard_map/ppermute | solution.py:172
  252.0 2.4 fusion.13
  254.4 1.3 copy.70
  255.7 13.2 %all-to-all-start = ((bf16[16,2,32,672]{3,2,1,0:T(8,128)(2,1)}), bf16[16,2,32,672]{3,2,1,0:T(8,128)(2,1)}, u32[]{:S(2)}, u32[]{:S(2)}) async-start(bf16[16,2,32,672]{3,2,1,0:T(8,128)(2,1)} %copy.70), calls=%async_computation | async-start | bytes 3145728 | tf_op jit(solution)/shard_map/all_to_all | solution.py:30
  269.0 2.7 reshape.292
  271.7 2.4 multiply_reduce_fusion
  274.6 1.2 broadcast_in_dim.16
  275.8 2.4 fusion.17
  278.2 6.1 %bitcast_convert_fusion = bf16[1024,672]{0,1:T(8,128)(2,1)} fusion(bf16[2,8,128,672]{3,2,1,0:T(8,128)(2,1)} %bitcast.126, bf16[8,1024,256]{2,1,0:T(8,128)(2,1)S(1)} %copy-done.4), kind=kOutput, calls=%fused_computation.10 | convolution fusion | flops 2819260416 | bytes 8323072 | tf_op jit(solution)/shard_map/htkc,khcf->tf/dot_general | solution.py:319
  284.3 27.8 %all-to-all-done = bf16[16,2,32,672]{3,2,1,0:T(8,128)(2,1)} async-done(((bf16[16,2,32,672]{3,2,1,0:T(8,128)(2,1)}), bf16[16,2,32,672]{3,2,1,0:T(8,128)(2,1)}, u32[]{:S(2)}, u32[]{:S(2)}) %all-to-all-start) | async-done | bytes 1376288 | tf_op jit(solution)/shard_map/all_to_all | solution.py:30
  312.1 1.7 convert_reduce_fusion.1
  313.7 0.7 slice_bitcast_fusion.3
  (37 shorter events, 1.6 us)
Async XLA Ops:
  0.6 47.4 %copy-start = (bf16[1024,672]{0,1:T(8,128)(2,1)S(1)}, bf16[1024,672]{0,1:T(8,128)(2,1)}, u32[]{:S(2)}) copy-start(bf16[1024,672]{0,1:T(8,128)(2,1)} %param.14) | copy-start | bytes 4128772
  131.0 4.2 %copy-start.9 = (f32[128]{0:T(128)S(1)}, f32[128]{0:T(128)}, u32[]{:S(2)}) copy-start(f32[128]{0:T(128)} %param.19) | copy-start | bytes 1540
  132.3 6.0 %copy-start.3 = (bf16[1024,256]{1,0:T(8,128)(2,1)S(1)}, bf16[1024,256]{1,0:T(8,128)(2,1)}, u32[]{:S(2)}) copy-start(bf16[1024,256]{1,0:T(8,128)(2,1)} %param.15) | copy-start | bytes 1572868
  134.7 3.6 %copy-start.5 = (bf16[1024,1,128]{2,0,1:T(8,128)(2,1)}, bf16[1024,1,128]{2,0,1:T(8,128)(2,1)S(1)}, u32[]{:S(2)}) copy-start(bf16[1024,1,128]{2,0,1:T(8,128)(2,1)S(1)} %copy.78) | copy-start | bytes 786436
  135.4 3.0 copy-start.7
  135.4 10.7 %copy-start.10 = (f32[128]{0:T(128)S(1)}, f32[128]{0:T(128)}, u32[]{:S(2)}) copy-start(f32[128]{0:T(128)} %param.18) | copy-start | bytes 1540
  136.2 14.2 %collective-permute-start = (bf16[2,1024,1,128]{3,1,2,0:T(8,128)(2,1)}, bf16[2,1024,1,128]{3,1,2,0:T(8,128)(2,1)}, u32[]{:S(2)}, u32[]{:S(2)}) collective-permute-start(bf16[2,1024,1,128]{3,1,2,0:T(8,128)(2,1)} %pad_maximum_fusion), channel_id=1, source_target_pairs={{0,8},{8,16},{16,24},{24,32},{32,40},{40,48},{48,56},{56,64},{64,7... | collective-permute-start | bytes 1572872 | tf_op jit(solution)/shard_map/ppermute | solution.py:21
  146.1 4.4 %copy-start.6 = (bf16[1024,1,128]{2,0,1:T(8,128)(2,1)S(1)}, bf16[1024,1,128]{2,0,1:T(8,128)(2,1)}, u32[]{:S(2)}) copy-start(bf16[1024,1,128]{2,0,1:T(8,128)(2,1)} %copy-done.5) | copy-start | bytes 786436
  146.1 4.4 %copy-start.8 = (bf16[1,1024,1,128]{3,1,2,0:T(8,128)(2,1)S(1)}, bf16[1,1024,1,128]{3,1,2,0:T(8,128)(2,1)}, u32[]{:S(2)}) copy-start(bf16[1,1024,1,128]{3,1,2,0:T(8,128)(2,1)} %copy-done.7) | copy-start | bytes 786436
  148.5 1.0 copy-start.1
  169.6 5.5 %collective-permute-start.1 = (bf16[2,1024,1,128]{3,1,2,0:T(8,128)(2,1)}, bf16[2,1024,1,128]{3,1,2,0:T(8,128)(2,1)}, u32[]{:S(2)}, u32[]{:S(2)}) collective-permute-start(bf16[2,1024,1,128]{3,1,2,0:T(8,128)(2,1)} %slice.110), channel_id=1, source_target_pairs={{8,0},{16,8},{24,16},{32,24},{40,32},{48,40},{56,48},{64,56},{72,6... | collective-permute-start | bytes 1572872 | tf_op jit(solution)/shard_map/ppermute | solution.py:21
  243.4 8.6 %collective-permute-start.2 = (bf16[2,16,32,672]{3,2,1,0:T(8,128)(2,1)}, bf16[2,16,32,672]{3,2,1,0:T(8,128)(2,1)}, u32[]{:S(2)}, u32[]{:S(2)}) collective-permute-start(bf16[2,16,32,672]{3,2,1,0:T(8,128)(2,1)} %select_bitcast_fusion), channel_id=1, source_target_pairs={{0,8},{8,0},{1,9},{9,1},{2,10},{10,2},{3,11},{11,3},{4,12},{12,4},... | collective-permute-start | bytes 4128776 | tf_op jit(solution)/shard_map/ppermute | solution.py:172
  255.7 56.4 %all-to-all-start = ((bf16[16,2,32,672]{3,2,1,0:T(8,128)(2,1)}), bf16[16,2,32,672]{3,2,1,0:T(8,128)(2,1)}, u32[]{:S(2)}, u32[]{:S(2)}) async-start(bf16[16,2,32,672]{3,2,1,0:T(8,128)(2,1)} %copy.70), calls=%async_computation | async-start | bytes 3145728 | tf_op jit(solution)/shard_map/all_to_all | solution.py:30
  274.1 1.7 copy-start.2
  274.6 3.6 %copy-start.4 = (bf16[8,1024,256]{2,1,0:T(8,128)(2,1)S(1)}, bf16[8,1024,256]{2,1,0:T(8,128)(2,1)}, u32[]{:S(2)}) copy-start(bf16[8,1024,256]{2,1,0:T(8,128)(2,1)} %shard_map.127) | copy-start | bytes 12582916

commit v8 on v6

--- a/solution.py
+++ b/solution.py
@@ -96,7 +96,7 @@
     local.wait()
 
 
-def gather_seq(block):
+def gather_seq(block, kernel_id):
     chips = lax.axis_size("chip")
     spec = pl.BlockSpec(memory_space=pltpu.VMEM)
     return pl.pallas_call(
@@ -111,7 +111,7 @@
             pltpu.SemaphoreType.DMA((chips,)),
             pltpu.SemaphoreType.DMA((chips,)),
         ],
-        compiler_params=pltpu.CompilerParams(collective_id=0, has_side_effects=True),
+        compiler_params=pltpu.CompilerParams(collective_id=kernel_id, has_side_effects=True),
     )(block[:, None])
 
 
@@ -219,16 +219,17 @@
     col_block = key_weight.shape[1]
     seq_index = lax.axis_index(SEQ)
     base_row = seq_index * rows_here
-    pair_t = jnp.stack([key_weight.T, value_weight.T])
-    weight_t = gather_seq(pair_t).reshape(2, n_seq * col_block, feats)
-    terms = lax.dot_general(
-        normed, weight_t, (((1,), (2,)), ((), ())), preferred_element_type=jnp.float32
-    ).astype(jnp.bfloat16)
-    terms = terms.reshape(rows_here, 2, n_uly, heads_here * HD).transpose(2, 0, 1, 3)
-    received = exchange(terms, "uly")
-    raw_pair = jnp.sum(received.astype(jnp.float32), axis=0)
-    key_raw = raw_pair[:, 0]
-    value_raw = raw_pair[:, 1]
+    weight_ts = []
+    raws = []
+    for index, weight in enumerate((key_weight, value_weight)):
+        weight_t = gather_seq(weight.T[None], index).reshape(n_seq * col_block, feats)
+        weight_ts.append(weight_t)
+        terms = lax.dot_general(
+            normed, weight_t, (((1,), (1,)), ((), ())), preferred_element_type=jnp.float32
+        ).astype(jnp.bfloat16)
+        terms = terms.reshape(rows_here, n_uly, heads_here * HD).transpose(1, 0, 2)
+        raws.append(jnp.sum(exchange(terms, "uly").astype(jnp.float32), axis=0))
+    key_raw, value_raw = raws
     key_in = key_raw.reshape(rows_here, heads_here, HD)
     keys_bf = normalize(key_in, k_gain, 1.0).astype(jnp.bfloat16)
     values_bf = value_raw.reshape(rows_here, heads_here, HD).astype(jnp.bfloat16)
@@ -265,7 +266,7 @@
     key_grad = pull_key(own_grads[0])[0].astype(jnp.bfloat16).reshape(rows_here, heads_here * HD)
     value_grad = own_grads[1].astype(jnp.bfloat16).reshape(rows_here, heads_here * HD)
     grads_all = gather_all(jnp.stack([key_grad, value_grad], axis=1), "uly")
-    weight_heads = weight_t.reshape(2, n_uly, heads_here * HD, feats)
+    weight_heads = jnp.stack(weight_ts).reshape(2, n_uly, heads_here * HD, feats)
     grad_normed = jnp.einsum(
         "htkc,khcf->tf", grads_all, weight_heads, preferred_element_type=jnp.float32
     ).astype(jnp.bfloat16)

time: 298 us -> 304 us (1.020)
  Pallas kernels: 56.9 us -> 87.2 us
  waiting for transfers between devices: 132 us -> 103 us
  matrix products: 18.5 us -> 21.9 us
    pallas_call x1 -> x2, Pallas kernels: 41.9 us -> 72.3 us  [gather_seq(): pl.pallas_call(functools.partial(gather_kernel, chips), out_shape=jax.Sha...]
    all_to_all x3 -> x4, waiting for transfers between devices: 121 us -> 92.5 us  [exchange(): return lax.all_to_all(blocks, axis, 0, 0)]
    another operation x0 -> x2, local copies, waits for them, and re-layouts: none -> 5.1 us  [body(): jnp.stack(weight_ts).reshape(2, n_uly, heads_here * HD, feats)]
    all_to_all x3 -> x4, starting transfers between devices: 24.8 us -> 29.8 us  [exchange(): return lax.all_to_all(blocks, axis, 0, 0)]
    dot_general x1 -> x2, matrix products: 5.54 us -> 9.15 us  [body(): lax.dot_general(normed, weight_t, (((1,), (1,)), ((), ())), preferred_ele...]
    unnamed x22 -> x28, local copies, waits for them, and re-layouts: 4.73 us -> 1.54 us
  transfers between devices with their start and end apart: 6 -> 7, of which waited for: 6 -> 6; matrix products, arithmetic and copies ran while one was open for 8% -> 13% of each run, Pallas kernels for 0% -> 15%
where the time goes in v8:
time: 304 us; the launch traced here: 302 us
  waiting for transfers between devices  103 us (34%)
  Pallas kernels  87.2 us (29%)
  starting transfers between devices  35.6 us (12%)
  local copies, waits for them, and re-layouts  31.4 us (10%)
  other arithmetic  22.5 us (7%)
  matrix products  21.9 us (7%)
    all_to_all x4, waiting for transfers between devices, exchange(): return lax.all_to_all(blocks, axis, 0, 0)  92.5 us
    pallas_call x2, Pallas kernels, gather_seq(): pl.pallas_call(functools.partial(gather_kernel, chips), out_shape=jax.Sha...  72.3 us
    all_to_all x4, starting transfers between devices, exchange(): return lax.all_to_all(blocks, axis, 0, 0)  29.8 us
    pallas_call x1, Pallas kernels, attend(): pl.pallas_call(attention_kernel, out_shape=(jax.ShapeDtypeStruct((rows, 2...  14.9 us
    dot_general x2, matrix products, body(): lax.dot_general(normed, weight_t, (((1,), (1,)), ((), ())), preferred_ele...  9.15 us
    ppermute x2, waiting for transfers between devices, from_behind(): return lax.ppermute(array, axis, pairs)  6.83 us
    dot_general x1, matrix products, body(): jnp.einsum('htkc,tf->khcf', grads_all, normed, preferred_element_type=jnp...  6.51 us
    dot_general x1, matrix products, body(): jnp.einsum('htkc,khcf->tf', grads_all, weight_heads, preferred_element_ty...  6.28 us
  transfers between devices with their start and end apart: 7, of which 6 were waited for; matrix products, arithmetic and copies ran while one was open for 13% of the time, Pallas kernels for 15%

profile of v8, /device:TPU:2, one launch (start us, length us, event | category | flops | bytes accessed | tf_op | source)
XLA Modules:
  0.0 302.2 jit_solution(2218177489876018838)
XLA Ops:
  0.6 26.7 %shard_map.124 = bf16[1,32,32,672]{3,2,1,0:T(8,128)(2,1)} custom-call(bf16[1,1,32,672]{3,2,1,0:T(8,128)(2,1)} %bitcast.127), custom_call_target="tpu_custom_call" | custom-call | tf_op jit(solution)/shard_map/pallas_call | solution.py:102
  27.4 4.6 %convolution_convert_fusion.1 = bf16[1024,1024]{0,1:T(8,128)(2,1)} fusion(bf16[1024,672]{1,0:T(8,128)(2,1)} %bitcast.114, bf16[1024,672]{0,1:T(8,128)(2,1)S(1)} %copy-done), kind=kOutput, calls=%fused_computation.10 | convolution fusion | flops 1410334720 | bytes 4849664 | tf_op jit(solution)/shard_map/dot_general | solution.py:227
  32.0 8.1 %all-to-all-start = ((bf16[8,1024,128]{1,2,0:T(8,128)(2,1)}), bf16[8,1024,128]{1,2,0:T(8,128)(2,1)}, u32[]{:S(2)}, u32[]{:S(2)}) async-start(bf16[8,1024,128]{1,2,0:T(8,128)(2,1)} %bitcast.124), calls=%async_computation | async-start | bytes 4194304 | tf_op jit(solution)/shard_map/all_to_all | solution.py:30
  40.1 45.5 %shard_map.125 = bf16[1,32,32,672]{3,2,1,0:T(8,128)(2,1)} custom-call(bf16[1,1,32,672]{3,2,1,0:T(8,128)(2,1)} %bitcast.128), custom_call_target="tpu_custom_call" | custom-call | tf_op jit(solution)/shard_map/pallas_call | solution.py:102
  85.6 4.6 %convolution_convert_fusion = bf16[1024,1024]{0,1:T(8,128)(2,1)} fusion(bf16[1024,672]{1,0:T(8,128)(2,1)} %bitcast.116, bf16[1024,672]{0,1:T(8,128)(2,1)S(1)} %copy-done), kind=kOutput, calls=%fused_computation.9 | convolution fusion | flops 1410334720 | bytes 4849664 | tf_op jit(solution)/shard_map/dot_general | solution.py:227
  90.2 8.4 %all-to-all-start.1 = ((bf16[8,1024,128]{1,2,0:T(8,128)(2,1)}), bf16[8,1024,128]{1,2,0:T(8,128)(2,1)}, u32[]{:S(2)}, u32[]{:S(2)}) async-start(bf16[8,1024,128]{1,2,0:T(8,128)(2,1)} %bitcast.123), calls=%async_computation.1 | async-start | bytes 4194304 | tf_op jit(solution)/shard_map/all_to_all | solution.py:30
  99.1 1.2 multiply_reduce_fusion.1
  100.4 2.0 convert_reduce_fusion
  102.7 23.4 %all-to-all-done.1 = bf16[8,1024,128]{1,2,0:T(8,128)(2,1)} async-done(((bf16[8,1024,128]{1,2,0:T(8,128)(2,1)}), bf16[8,1024,128]{1,2,0:T(8,128)(2,1)}, u32[]{:S(2)}, u32[]{:S(2)}) %all-to-all-start.1) | async-done | bytes 2097184 | tf_op jit(solution)/shard_map/all_to_all | solution.py:30
  126.1 2.0 reduce_sum.90
  128.6 0.7 copy-done.8
  129.2 0.8 pad_maximum_fusion
  130.1 1.9 collective-permute-start
  132.0 1.3 pad_dynamic-slice_fusion
  133.3 0.7 dynamic_slice.6
  134.0 1.0 copy.49.qseg_ref
  135.0 1.0 copy.46
  136.1 2.4 mul.242
  138.5 2.0 fusion.12.q_ref
  140.9 1.1 maximum_maximum_fusion
  142.0 1.0 slice_bitcast_fusion
  143.0 14.9 %shard_map.126 = (bf16[1024,256]{1,0:T(8,128)(2,1)}, f32[1024,256]{1,0:T(8,128)}, f32[2,2048,128]{2,1,0:T(8,128)}) custom-call(bf16[1024,256]{1,0:T(8,128)(2,1)} %fusion.12.q_ref, bf16[1024,256]{1,0:T(8,128)(2,1)} %do_ref.1, bf16[2048,128]{1,0:T(8,128)(2,1)} %get-tuple-element.44.k_ref, bf16[2048,128]{1,0:T(8,128)(2,1)} %get-tuple-element.43.v_ref, ...), custom_call_target="tpu_custom_call" | custom-call | flops 6442450944 | bytes 8388608 | tf_op jit(solution)/shard_map/pallas_call | solution.py:197
  157.9 1.4 slice.92
  159.3 3.5 %collective-permute-start.1 = (bf16[2,1024,1,128]{3,1,0,2:T(8,128)(2,1)S(1)}, bf16[2,1024,1,128]{3,1,0,2:T(8,128)(2,1)S(1)}, u32[]{:S(2)}, u32[]{:S(2)}) collective-permute-start(bf16[2,1024,1,128]{3,1,0,2:T(8,128)(2,1)S(1)} %slice.92), channel_id=1, source_target_pairs={{8,0},{16,8},{24,16},{32,24},{40,32},{48,40},{56,48},{64,56},{72,6... | collective-permute-start | bytes 1572872 | tf_op jit(solution)/shard_map/ppermute | solution.py:21
  162.8 6.5 %collective-permute-done.1 = bf16[2,1024,1,128]{3,1,0,2:T(8,128)(2,1)S(1)} collective-permute-done((bf16[2,1024,1,128]{3,1,0,2:T(8,128)(2,1)S(1)}, bf16[2,1024,1,128]{3,1,0,2:T(8,128)(2,1)S(1)}, u32[]{:S(2)}, u32[]{:S(2)}) %collective-permute-start.1) | collective-permute-done | bytes 524320 | tf_op jit(solution)/shard_map/ppermute | solution.py:21
  169.2 1.3 slice_add_fusion
  171.2 2.8 broadcast_in_dim.15
  174.0 4.6 %all-to-all-start.2 = ((bf16[8,1024,2,128]{3,1,2,0:T(8,128)(2,1)}), bf16[8,1024,2,128]{3,1,2,0:T(8,128)(2,1)}, u32[]{:S(2)}, u32[]{:S(2)}) async-start(bf16[8,1024,2,128]{3,1,2,0:T(8,128)(2,1)} %broadcast_in_dim.15), calls=%async_computation.2 | async-start | bytes 8388608 | tf_op jit(solution)/shard_map/all_to_all | solution.py:30
  178.6 50.3 %all-to-all-done.2 = bf16[8,1024,2,128]{3,1,2,0:T(8,128)(2,1)} async-done(((bf16[8,1024,2,128]{3,1,2,0:T(8,128)(2,1)}), bf16[8,1024,2,128]{3,1,2,0:T(8,128)(2,1)}, u32[]{:S(2)}, u32[]{:S(2)}) %all-to-all-start.2) | async-done | bytes 4194336 | tf_op jit(solution)/shard_map/all_to_all | solution.py:30
  228.9 6.5 %convert_bitcast_fusion = bf16[2,8,128,672]{2,3,0,1:T(8,128)(2,1)} fusion(bf16[8,1024,2,128]{3,1,2,0:T(8,128)(2,1)} %all-to-all-done.2, bf16[1024,672]{0,1:T(8,128)(2,1)S(1)} %copy-done), kind=kOutput, calls=%fused_computation.8 | convolution fusion | flops 2819948544 | bytes 8323072 | tf_op jit(solution)/shard_map/htkc,tf->khcf/dot_general | solution.py:273
  235.4 4.6 %copy.57 = bf16[2,8,128,672]{3,2,1,0:T(8,128)(2,1)} copy(bf16[2,8,128,672]{2,3,0,1:T(8,128)(2,1)} %convert_bitcast_fusion) | data formatting | bytes 5505024 | tf_op jit(solution)/shard_map/convert_element_type | solution.py:275
  240.0 2.7 select_bitcast_fusion
  243.1 3.4 %collective-permute-done.2 = bf16[2,16,32,672]{3,2,1,0:T(8,128)(2,1)} collective-permute-done((bf16[2,16,32,672]{3,2,1,0:T(8,128)(2,1)}, bf16[2,16,32,672]{3,2,1,0:T(8,128)(2,1)}, u32[]{:S(2)}, u32[]{:S(2)}) %collective-permute-start.2) | collective-permute-done | bytes 1376288 | tf_op jit(solution)/shard_map/ppermute | solution.py:124
  246.5 2.4 fusion.6
  249.0 1.2 copy.59
  250.2 8.8 %all-to-all-start.3 = ((bf16[16,2,32,672]{3,2,1,0:T(8,128)(2,1)}), bf16[16,2,32,672]{3,2,1,0:T(8,128)(2,1)}, u32[]{:S(2)}, u32[]{:S(2)}) async-start(bf16[16,2,32,672]{3,2,1,0:T(8,128)(2,1)} %copy.59), calls=%async_computation.3 | async-start | bytes 3145728 | tf_op jit(solution)/shard_map/all_to_all | solution.py:30
  259.1 2.6 copy.53
  261.6 2.5 copy.54
  264.2 2.7 reshape.396
  266.9 3.2 %multiply_reduce_fusion = f32[1024,2]{1,0:T(8,128)} fusion(f32[1024,1,2,128]{3,2,0,1:T(2,128)S(1)} %reshape.388, f32[1024,1,2,128]{3,2,0,1:T(2,128)} %reshape.396, f32[128]{0:T(128)S(1)} %broadcast_multiply_fusion), kind=kLoop, calls=%fused_computation.27 | loop fusion | flops 784384 | bytes 2105856 | tf_op jit(solution)/shard_map/transpose(jvp())/reduce_sum | solution.py:26
  270.1 1.3 copy.55
  271.6 1.2 broadcast_in_dim.16
  272.9 1.1 fusion.9
  274.3 0.5 copy-done.11
  274.8 6.3 %bitcast_convert_fusion = bf16[1024,672]{0,1:T(8,128)(2,1)} fusion(bf16[8,1024,2,128]{3,1,2,0:T(8,128)(2,1)} %all-to-all-done.2, bf16[1,8,128,672]{2,3,0,1:T(8,128)(2,1)S(1)} %copy-done.11, bf16[1,8,128,672]{2,3,0,1:T(8,128)(2,1)S(1)} %copy-done.10), kind=kOutput, calls=%fused_computation.7 | convolution fusion | flops 2820636672 | bytes 8323072 | tf_op jit(solution)/shard_map/htkc,khcf->tf/dot_general | solution.py:270
  281.1 18.8 %all-to-all-done.3 = bf16[16,2,32,672]{3,2,1,0:T(8,128)(2,1)} async-done(((bf16[16,2,32,672]{3,2,1,0:T(8,128)(2,1)}), bf16[16,2,32,672]{3,2,1,0:T(8,128)(2,1)}, u32[]{:S(2)}, u32[]{:S(2)}) %all-to-all-start.3) | async-done | bytes 1376288 | tf_op jit(solution)/shard_map/all_to_all | solution.py:30
  299.9 1.7 convert_reduce_fusion.1
  301.5 0.7 slice_bitcast_fusion.2
  (47 shorter events, 3.4 us)
Async XLA Ops:
  0.6 26.8 %copy-start = (bf16[1024,672]{0,1:T(8,128)(2,1)S(1)}, bf16[1024,672]{0,1:T(8,128)(2,1)}, u32[]{:S(2)}) copy-start(bf16[1024,672]{0,1:T(8,128)(2,1)} %param.14) | copy-start | bytes 4128772
  32.0 58.2 %all-to-all-start = ((bf16[8,1024,128]{1,2,0:T(8,128)(2,1)}), bf16[8,1024,128]{1,2,0:T(8,128)(2,1)}, u32[]{:S(2)}, u32[]{:S(2)}) async-start(bf16[8,1024,128]{1,2,0:T(8,128)(2,1)} %bitcast.124), calls=%async_computation | async-start | bytes 4194304 | tf_op jit(solution)/shard_map/all_to_all | solution.py:30
  90.2 8.4 %copy-start.3 = (bf16[1024,256]{1,0:T(8,128)(2,1)S(1)}, bf16[1024,256]{1,0:T(8,128)(2,1)}, u32[]{:S(2)}) copy-start(bf16[1024,256]{1,0:T(8,128)(2,1)} %param.15) | copy-start | bytes 1572868
  90.2 36.0 %all-to-all-start.1 = ((bf16[8,1024,128]{1,2,0:T(8,128)(2,1)}), bf16[8,1024,128]{1,2,0:T(8,128)(2,1)}, u32[]{:S(2)}, u32[]{:S(2)}) async-start(bf16[8,1024,128]{1,2,0:T(8,128)(2,1)} %bitcast.123), calls=%async_computation.1 | async-start | bytes 4194304 | tf_op jit(solution)/shard_map/all_to_all | solution.py:30
  102.4 25.9 %copy-start.12 = (f32[128]{0:T(128)S(1)}, f32[128]{0:T(128)}, u32[]{:S(2)}) copy-start(f32[128]{0:T(128)} %param.19) | copy-start | bytes 1540
  102.6 25.9 %copy-start.1 = (f32[1024,128]{1,0:T(8,128)}, f32[1024,128]{1,0:T(8,128)S(1)}, u32[]{:S(2)}) copy-start(f32[1024,128]{1,0:T(8,128)S(1)} %copy.47) | copy-start | bytes 1572868
  128.1 8.0 %copy-start.13 = (f32[128]{0:T(128)S(1)}, f32[128]{0:T(128)}, u32[]{:S(2)}) copy-start(f32[128]{0:T(128)} %param.18) | copy-start | bytes 1540
  128.3 7.8 %copy-start.6 = (bf16[1024,128]{1,0:T(8,128)(2,1)}, bf16[1024,128]{1,0:T(8,128)(2,1)S(1)}, u32[]{:S(2)}) copy-start(bf16[1024,128]{1,0:T(8,128)(2,1)S(1)} %copy.48) | copy-start | bytes 786436
  128.6 0.7 copy-start.8
  130.1 10.8 %collective-permute-start = (bf16[2,1024,1,128]{3,1,2,0:T(8,128)(2,1)}, bf16[2,1024,1,128]{3,1,2,0:T(8,128)(2,1)}, u32[]{:S(2)}, u32[]{:S(2)}) collective-permute-start(bf16[2,1024,1,128]{3,1,2,0:T(8,128)(2,1)} %pad_maximum_fusion), channel_id=1, source_target_pairs={{0,8},{8,16},{16,24},{24,32},{32,40},{40,48},{48,56},{56,64},{64,7... | collective-permute-start | bytes 1572872 | tf_op jit(solution)/shard_map/ppermute | solution.py:21
  136.1 4.8 %copy-start.9 = (bf16[1,1024,1,128]{3,1,2,0:T(8,128)(2,1)S(1)}, bf16[1,1024,1,128]{3,1,2,0:T(8,128)(2,1)}, u32[]{:S(2)}) copy-start(bf16[1,1024,1,128]{3,1,2,0:T(8,128)(2,1)} %copy-done.8) | copy-start | bytes 786436
  136.1 4.8 %copy-start.7 = (bf16[1024,128]{1,0:T(8,128)(2,1)S(1)}, bf16[1024,128]{1,0:T(8,128)(2,1)}, u32[]{:S(2)}) copy-start(bf16[1024,128]{1,0:T(8,128)(2,1)} %copy-done.6) | copy-start | bytes 786436
  157.9 12.6 %copy-start.2 = (f32[1024,128]{1,0:T(8,128)S(1)}, f32[1024,128]{1,0:T(8,128)}, u32[]{:S(2)}) copy-start(f32[1024,128]{1,0:T(8,128)} %copy-done.1) | copy-start | bytes 1572868
  159.3 9.9 %collective-permute-start.1 = (bf16[2,1024,1,128]{3,1,0,2:T(8,128)(2,1)S(1)}, bf16[2,1024,1,128]{3,1,0,2:T(8,128)(2,1)S(1)}, u32[]{:S(2)}, u32[]{:S(2)}) collective-permute-start(bf16[2,1024,1,128]{3,1,0,2:T(8,128)(2,1)S(1)} %slice.92), channel_id=1, source_target_pairs={{8,0},{16,8},{24,16},{32,24},{40,32},{48,40},{56,48},{64,56},{72,6... | collective-permute-start | bytes 1572872 | tf_op jit(solution)/shard_map/ppermute | solution.py:21
  174.0 54.9 %all-to-all-start.2 = ((bf16[8,1024,2,128]{3,1,2,0:T(8,128)(2,1)}), bf16[8,1024,2,128]{3,1,2,0:T(8,128)(2,1)}, u32[]{:S(2)}, u32[]{:S(2)}) async-start(bf16[8,1024,2,128]{3,1,2,0:T(8,128)(2,1)} %broadcast_in_dim.15), calls=%async_computation.2 | async-start | bytes 8388608 | tf_op jit(solution)/shard_map/all_to_all | solution.py:30
  242.7 3.8 %collective-permute-start.2 = (bf16[2,16,32,672]{3,2,1,0:T(8,128)(2,1)}, bf16[2,16,32,672]{3,2,1,0:T(8,128)(2,1)}, u32[]{:S(2)}, u32[]{:S(2)}) collective-permute-start(bf16[2,16,32,672]{3,2,1,0:T(8,128)(2,1)} %select_bitcast_fusion), channel_id=1, source_target_pairs={{0,8},{8,0},{1,9},{9,1},{2,10},{10,2},{3,11},{11,3},{4,12},{12,4},... | collective-permute-start | bytes 4128776 | tf_op jit(solution)/shard_map/ppermute | solution.py:124
  250.2 49.7 %all-to-all-start.3 = ((bf16[16,2,32,672]{3,2,1,0:T(8,128)(2,1)}), bf16[16,2,32,672]{3,2,1,0:T(8,128)(2,1)}, u32[]{:S(2)}, u32[]{:S(2)}) async-start(bf16[16,2,32,672]{3,2,1,0:T(8,128)(2,1)} %copy.59), calls=%async_computation.3 | async-start | bytes 3145728 | tf_op jit(solution)/shard_map/all_to_all | solution.py:30
  270.1 2.8 copy-start.4
  271.6 1.3 copy-start.5
  272.9 1.4 copy-start.10
  272.9 1.9 copy-start.11

commit v9 on v6

--- a/solution.py
+++ b/solution.py
@@ -35,81 +35,113 @@
     return exchange(jnp.broadcast_to(block[None], (count,) + block.shape), axis)
 
 
-SEQ = ("chip", "core")
+SEQ = ("level", "row", "core")
+CHIP = ("level", "row")
 SWAP = [(0, 1), (1, 0)]
 
 
-def gather_kernel(chips, x_ref, out_ref, local_sem, send_sem, recv_sem, fwd_send, fwd_recv):
-    chip = lax.axis_index("chip")
+def gather_kernel(levels, rows, x_ref, out_ref, local_sem, z_send, z_recv, x_send, x_recv, f_send, f_recv):
+    level = lax.axis_index("level")
+    row = lax.axis_index("row")
     core = lax.axis_index("core")
     uly = lax.axis_index("uly")
     other = 1 - core
     mesh_ids = pl.DeviceIdType.MESH
-    barrier = pltpu.get_barrier_semaphore()
-    for d in range(1, chips):
-        peer = (lax.rem(chip + d, chips), core, uly)
-        pl.semaphore_signal(barrier, 1, device_id=peer, device_id_type=mesh_ids)
-    pl.semaphore_signal(barrier, 1, device_id=(chip, other, uly), device_id_type=mesh_ids)
-    pl.semaphore_wait(barrier, chips)
-    mine = chip * 2 + core
-    local = pltpu.make_async_copy(x_ref, out_ref.at[:, pl.ds(mine, 1)], local_sem)
-    local.start()
-    sends = {}
-    for d in range(1, chips):
-        sends[d] = pltpu.make_async_remote_copy(
-            src_ref=x_ref,
-            dst_ref=out_ref.at[:, pl.ds(mine, 1)],
-            send_sem=send_sem.at[d],
-            recv_sem=recv_sem.at[d],
-            device_id=(lax.rem(chip + d, chips), core, uly),
+
+    def slot(at_level, at_row):
+        return (lax.rem(at_level, levels) * rows + lax.rem(at_row, rows)) * 2 + core
+
+    def window(index):
+        return out_ref.at[:, pl.ds(index, 1)]
+
+    def to_partner(index, dx, dz):
+        return pltpu.make_async_remote_copy(
+            src_ref=window(index),
+            dst_ref=window(index),
+            send_sem=f_send.at[dx, dz],
+            recv_sem=f_recv.at[dx, dz],
+            device_id=(level, row, other, uly),
             device_id_type=mesh_ids,
         )
-        sends[d].start()
-    forwards = [
-        pltpu.make_async_remote_copy(
+
+    barrier = pltpu.get_barrier_semaphore()
+    for dz in range(1, levels):
+        peer = (lax.rem(level + dz, levels), row, core, uly)
+        pl.semaphore_signal(barrier, 1, device_id=peer, device_id_type=mesh_ids)
+    for dx in range(1, rows):
+        peer = (level, lax.rem(row + dx, rows), core, uly)
+        pl.semaphore_signal(barrier, 1, device_id=peer, device_id_type=mesh_ids)
+    pl.semaphore_signal(barrier, 1, device_id=(level, row, other, uly), device_id_type=mesh_ids)
+    pl.semaphore_wait(barrier, levels + rows - 1)
+    mine = slot(level, row)
+    local = pltpu.make_async_copy(x_ref, window(mine), local_sem)
+    local.start()
+    z_copies = {}
+    for dz in range(1, levels):
+        z_copies[dz] = pltpu.make_async_remote_copy(
             src_ref=x_ref,
-            dst_ref=out_ref.at[:, pl.ds(mine, 1)],
-            send_sem=fwd_send.at[0],
-            recv_sem=fwd_recv.at[0],
-            device_id=(chip, other, uly),
+            dst_ref=window(mine),
+            send_sem=z_send.at[dz],
+            recv_sem=z_recv.at[dz],
+            device_id=(lax.rem(level + dz, levels), row, core, uly),
             device_id_type=mesh_ids,
         )
-    ]
-    forwards[0].start()
-    for d in range(1, chips):
-        sends[d].wait_recv()
-        slot = lax.rem(chip + chips - d, chips) * 2 + core
-        forward = pltpu.make_async_remote_copy(
-            src_ref=out_ref.at[:, pl.ds(slot, 1)],
-            dst_ref=out_ref.at[:, pl.ds(slot, 1)],
-            send_sem=fwd_send.at[d],
-            recv_sem=fwd_recv.at[d],
-            device_id=(chip, other, uly),
-            device_id_type=mesh_ids,
-        )
+        z_copies[dz].start()
+    local.wait()
+    x_moves = {}
+    forwards = []
+
+    def spread(dz, index):
+        for dx in range(1, rows):
+            move = pltpu.make_async_remote_copy(
+                src_ref=window(index),
+                dst_ref=window(index),
+                send_sem=x_send.at[dx, dz],
+                recv_sem=x_recv.at[dx, dz],
+                device_id=(level, lax.rem(row + dx, rows), core, uly),
+                device_id_type=mesh_ids,
+            )
+            move.start()
+            x_moves[dx, dz] = move
+        forward = to_partner(index, 0, dz)
         forward.start()
         forwards.append(forward)
-    for d in range(1, chips):
-        sends[d].wait_send()
+
+    spread(0, mine)
+    for dz in range(1, levels):
+        z_copies[dz].wait_recv()
+        spread(dz, slot(level + levels - dz, row))
+    for dx in range(1, rows):
+        for dz in range(levels):
+            x_moves[dx, dz].wait_recv()
+            forward = to_partner(slot(level + levels - dz, row + rows - dx), dx, dz)
+            forward.start()
+            forwards.append(forward)
+    for dz in range(1, levels):
+        z_copies[dz].wait_send()
+    for move in x_moves.values():
+        move.wait_send()
     for forward in forwards:
         forward.wait()
-    local.wait()
 
 
 def gather_seq(block):
-    chips = lax.axis_size("chip")
+    levels = lax.axis_size("level")
+    rows = lax.axis_size("row")
     spec = pl.BlockSpec(memory_space=pltpu.VMEM)
     return pl.pallas_call(
-        functools.partial(gather_kernel, chips),
-        out_shape=jax.ShapeDtypeStruct((block.shape[0], 2 * chips) + block.shape[1:], block.dtype),
+        functools.partial(gather_kernel, levels, rows),
+        out_shape=jax.ShapeDtypeStruct((block.shape[0], 2 * levels * rows) + block.shape[1:], block.dtype),
         in_specs=[spec],
         out_specs=spec,
         scratch_shapes=[
             pltpu.SemaphoreType.DMA(()),
-            pltpu.SemaphoreType.DMA((chips,)),
-            pltpu.SemaphoreType.DMA((chips,)),
-            pltpu.SemaphoreType.DMA((chips,)),
-            pltpu.SemaphoreType.DMA((chips,)),
+            pltpu.SemaphoreType.DMA((levels,)),
+            pltpu.SemaphoreType.DMA((levels,)),
+            pltpu.SemaphoreType.DMA((rows, levels)),
+            pltpu.SemaphoreType.DMA((rows, levels)),
+            pltpu.SemaphoreType.DMA((rows, levels)),
+            pltpu.SemaphoreType.DMA((rows, levels)),
         ],
         compiler_params=pltpu.CompilerParams(collective_id=0, has_side_effects=True),
     )(block[:, None])
@@ -123,7 +155,7 @@
     send = jnp.take(split, 1 - core, axis=2)
     pair = (keep.astype(jnp.float32) + lax.ppermute(send, "core", SWAP).astype(jnp.float32))
     pair = pair.astype(jnp.bfloat16).transpose(1, 0, 2, 3)
-    return jnp.sum(exchange(pair, "chip").astype(jnp.float32), axis=0)
+    return jnp.sum(exchange(pair, CHIP).astype(jnp.float32), axis=0)
 
 
 def attend_block(
@@ -280,7 +312,10 @@
 
 def solution(mesh):
     n_seq, n_uly = mesh.shape["seq"], mesh.shape["uly"]
-    fine = jax.sharding.Mesh(mesh.devices.reshape(n_seq // 2, 2, n_uly), ("chip", "core", "uly"))
+    rows = 4
+    fine = jax.sharding.Mesh(
+        mesh.devices.reshape(n_seq // (2 * rows), rows, 2, n_uly), ("level", "row", "core", "uly")
+    )
     return jax.shard_map(
         body,
         mesh=fine,

time: 298 us -> 284 us (0.953)
  Pallas kernels: 56.9 us -> 46.9 us
  starting transfers between devices: 33.2 us -> 27.2 us
    pallas_call x1, Pallas kernels: 41.9 us -> 31.9 us  [gather_seq(): pl.pallas_call(functools.partial(gather_kernel, levels, rows), out_shape=...]
    all_to_all x3, starting transfers between devices: 24.8 us -> 21.5 us  [exchange(): return lax.all_to_all(blocks, axis, 0, 0)]
  transfers between devices with their start and end apart: 6 -> 6, of which waited for: 6 -> 6; matrix products, arithmetic and copies ran while one was open for 8% -> 9% of each run, Pallas kernels for 0% -> 0%
where the time goes in v9:
time: 284 us; the launch traced here: 283 us
  waiting for transfers between devices  134 us (47%)
  Pallas kernels  46.9 us (17%)
  local copies, waits for them, and re-layouts  32 us (11%)
  starting transfers between devices  27.2 us (10%)
  other arithmetic  23.7 us (8%)
  matrix products  18.5 us (7%)
    all_to_all x3, waiting for transfers between devices, exchange(): return lax.all_to_all(blocks, axis, 0, 0)  124 us
    pallas_call x1, Pallas kernels, gather_seq(): pl.pallas_call(functools.partial(gather_kernel, levels, rows), out_shape=...  31.9 us
    all_to_all x3, starting transfers between devices, exchange(): return lax.all_to_all(blocks, axis, 0, 0)  21.5 us
    pallas_call x1, Pallas kernels, attend(): pl.pallas_call(attention_kernel, out_shape=(jax.ShapeDtypeStruct((rows, 2...  14.9 us
    ppermute x2, waiting for transfers between devices, from_behind(): return lax.ppermute(array, axis, pairs)  6.88 us
    dot_general x1, matrix products, body(): jnp.einsum('htkc,tf->khcf', grads_all, normed, preferred_element_type=jnp...  6.58 us
    dot_general x1, matrix products, body(): jnp.einsum('htkc,khcf->tf', grads_all, weight_heads, preferred_element_ty...  6.38 us
  transfers between devices with their start and end apart: 6, of which 6 were waited for; matrix products, arithmetic and copies ran while one was open for 9% of the time, Pallas kernels for 0%

profile of v9, /device:TPU:2, one launch (start us, length us, event | category | flops | bytes accessed | tf_op | source)
XLA Modules:
  0.0 283.3 jit_solution(3145324524758707791)
XLA Ops:
  0.6 1.6 maximum_bitcast_fusion.x_ref
  2.2 31.9 %shard_map.124 = bf16[2,32,32,672]{3,2,1,0:T(8,128)(2,1)} custom-call(bf16[2,1,32,672]{3,2,1,0:T(8,128)(2,1)} %maximum_bitcast_fusion.x_ref), custom_call_target="tpu_custom_call" | custom-call | tf_op jit(solution)/shard_map/pallas_call | solution.py:132
  34.2 5.5 %convolution_convert_fusion = bf16[2,1024,1024]{2,1,0:T(8,128)(2,1)S(1)} fusion(bf16[2,1024,672]{2,1,0:T(8,128)(2,1)} %bitcast.106, bf16[1024,672]{0,1:T(8,128)(2,1)S(1)} %copy-done), kind=kOutput, calls=%fused_computation.8 | convolution fusion | flops 2820669440 | bytes 8323072 | tf_op jit(solution)/shard_map/dot_general | solution.py:256
  39.7 2.5 copy.76
  42.2 5.6 %all-to-all-start = ((bf16[8,1024,2,128]{1,3,2,0:T(8,128)(2,1)}), bf16[8,1024,2,128]{1,3,2,0:T(8,128)(2,1)}, u32[]{:S(2)}, u32[]{:S(2)}) async-start(bf16[8,1024,2,128]{1,3,2,0:T(8,128)(2,1)} %bitcast.99), calls=%async_computation | async-start | bytes 8388608 | tf_op jit(solution)/shard_map/all_to_all | solution.py:30
  47.8 0.5 reshape.280
  48.3 1.2 multiply_reduce_fusion.1
  49.7 48.2 %all-to-all-done = bf16[8,1024,2,128]{1,3,2,0:T(8,128)(2,1)} async-done(((bf16[8,1024,2,128]{1,3,2,0:T(8,128)(2,1)}), bf16[8,1024,2,128]{1,3,2,0:T(8,128)(2,1)}, u32[]{:S(2)}, u32[]{:S(2)}) %all-to-all-start) | async-done | bytes 4194336 | tf_op jit(solution)/shard_map/all_to_all | solution.py:30
  97.9 3.2 %convert_reduce_fusion = f32[1024,2,128]{0,2,1:T(8,128)S(1)} fusion(bf16[8,1024,2,128]{1,3,2,0:T(8,128)(2,1)} %all-to-all-done), kind=kLoop, calls=%fused_computation | loop fusion | flops 3932160 | bytes 5242880 | tf_op jit(solution)/shard_map/reduce_sum | solution.py:261
  101.1 0.7 slice.83
  101.8 0.8 slice.82
  102.6 1.2 copy.64
  103.9 1.8 copy.65
  106.1 0.7 copy-done.6
  106.8 1.8 pad_maximum_fusion
  108.6 1.9 collective-permute-start
  110.5 1.3 pad_dynamic-slice_fusion
  111.8 0.7 dynamic_slice.6
  112.5 1.1 copy.50.qseg_ref
  113.6 1.0 copy.44
  114.6 2.4 mul.207
  117.1 1.0 copy-done.1
  118.0 1.0 fusion.11.q_ref
  119.4 1.1 maximum_maximum_fusion
  120.5 1.0 slice_bitcast_fusion.1
  121.6 14.9 %shard_map.125 = (bf16[1024,256]{1,0:T(8,128)(2,1)}, f32[1024,256]{1,0:T(8,128)}, f32[2,2048,128]{2,1,0:T(8,128)}) custom-call(bf16[1024,256]{1,0:T(8,128)(2,1)} %fusion.11.q_ref, bf16[1024,256]{1,0:T(8,128)(2,1)} %do_ref.1, bf16[2048,128]{1,0:T(8,128)(2,1)} %get-tuple-element.44.k_ref, bf16[2048,128]{1,0:T(8,128)(2,1)} %get-tuple-element.43.v_ref, ...), custom_call_target="tpu_custom_call" | custom-call | flops 6442450944 | bytes 8388608 | tf_op jit(solution)/shard_map/pallas_call | solution.py:229
  136.5 1.3 slice.108
  137.8 3.4 %collective-permute-start.1 = (bf16[2,1024,1,128]{3,1,2,0:T(8,128)(2,1)S(1)}, bf16[2,1024,1,128]{3,1,2,0:T(8,128)(2,1)S(1)}, u32[]{:S(2)}, u32[]{:S(2)}) collective-permute-start(bf16[2,1024,1,128]{3,1,2,0:T(8,128)(2,1)S(1)} %slice.108), channel_id=1, source_target_pairs={{8,0},{16,8},{24,16},{32,24},{40,32},{48,40},{56,48},{64,56},{72,6... | collective-permute-start | bytes 1572872 | tf_op jit(solution)/shard_map/ppermute | solution.py:21
  141.3 6.5 %collective-permute-done.1 = bf16[2,1024,1,128]{3,1,2,0:T(8,128)(2,1)S(1)} collective-permute-done((bf16[2,1024,1,128]{3,1,2,0:T(8,128)(2,1)S(1)}, bf16[2,1024,1,128]{3,1,2,0:T(8,128)(2,1)S(1)}, u32[]{:S(2)}, u32[]{:S(2)}) %collective-permute-start.1) | collective-permute-done | bytes 524320 | tf_op jit(solution)/shard_map/ppermute | solution.py:21
  147.7 1.3 slice_add_fusion
  149.7 2.8 broadcast_in_dim.18
  152.5 4.6 %all-to-all-start.1 = ((bf16[8,1024,2,128]{3,1,2,0:T(8,128)(2,1)}), bf16[8,1024,2,128]{3,1,2,0:T(8,128)(2,1)}, u32[]{:S(2)}, u32[]{:S(2)}) async-start(bf16[8,1024,2,128]{3,1,2,0:T(8,128)(2,1)} %broadcast_in_dim.18), calls=%async_computation.1 | async-start | bytes 8388608 | tf_op jit(solution)/shard_map/all_to_all | solution.py:30
  157.0 50.4 %all-to-all-done.1 = bf16[8,1024,2,128]{3,1,2,0:T(8,128)(2,1)} async-done(((bf16[8,1024,2,128]{3,1,2,0:T(8,128)(2,1)}), bf16[8,1024,2,128]{3,1,2,0:T(8,128)(2,1)}, u32[]{:S(2)}, u32[]{:S(2)}) %all-to-all-start.1) | async-done | bytes 4194336 | tf_op jit(solution)/shard_map/all_to_all | solution.py:30
  207.4 6.6 %convert_bitcast_fusion = bf16[2,8,128,672]{2,3,0,1:T(8,128)(2,1)} fusion(bf16[8,1024,2,128]{3,1,2,0:T(8,128)(2,1)} %all-to-all-done.1, bf16[1024,672]{0,1:T(8,128)(2,1)S(1)} %copy-done), kind=kOutput, calls=%fused_computation.7 | convolution fusion | flops 2819948544 | bytes 8323072 | tf_op jit(solution)/shard_map/htkc,tf->khcf/dot_general | solution.py:304
  214.0 4.6 %copy.54 = bf16[2,8,128,672]{3,2,1,0:T(8,128)(2,1)} copy(bf16[2,8,128,672]{2,3,0,1:T(8,128)(2,1)} %convert_bitcast_fusion) | data formatting | bytes 5505024 | tf_op jit(solution)/shard_map/convert_element_type | solution.py:306
  218.6 2.7 select_bitcast_fusion
  221.6 3.4 %collective-permute-done.2 = bf16[2,16,32,672]{3,2,1,0:T(8,128)(2,1)} collective-permute-done((bf16[2,16,32,672]{3,2,1,0:T(8,128)(2,1)}, bf16[2,16,32,672]{3,2,1,0:T(8,128)(2,1)}, u32[]{:S(2)}, u32[]{:S(2)}) %collective-permute-start.2) | collective-permute-done | bytes 1376288 | tf_op jit(solution)/shard_map/ppermute | solution.py:156
  225.0 2.4 fusion.4
  227.5 1.2 copy.56
  228.7 11.3 %all-to-all-start.2 = ((bf16[16,2,32,672]{3,2,1,0:T(8,128)(2,1)}), bf16[16,2,32,672]{3,2,1,0:T(8,128)(2,1)}, u32[]{:S(2)}, u32[]{:S(2)}) async-start(bf16[16,2,32,672]{3,2,1,0:T(8,128)(2,1)} %copy.56), calls=%async_computation.2 | async-start | bytes 3145728 | tf_op jit(solution)/shard_map/all_to_all | solution.py:30
  240.1 2.7 reshape.286
  242.8 2.4 multiply_reduce_fusion
  245.7 1.2 broadcast_in_dim.19
  247.0 2.4 fusion.8
  249.3 6.4 %bitcast_convert_fusion = bf16[1024,672]{0,1:T(8,128)(2,1)} fusion(bf16[8,1024,2,128]{3,1,2,0:T(8,128)(2,1)} %all-to-all-done.1, bf16[2,8,128,672]{3,2,1,0:T(8,128)(2,1)S(1)} %bitcast.107), kind=kOutput, calls=%fused_computation.6 | convolution fusion | flops 2819260416 | bytes 8323072 | tf_op jit(solution)/shard_map/htkc,khcf->tf/dot_general | solution.py:301
  255.7 25.2 %all-to-all-done.2 = bf16[16,2,32,672]{3,2,1,0:T(8,128)(2,1)} async-done(((bf16[16,2,32,672]{3,2,1,0:T(8,128)(2,1)}), bf16[16,2,32,672]{3,2,1,0:T(8,128)(2,1)}, u32[]{:S(2)}, u32[]{:S(2)}) %all-to-all-start.2) | async-done | bytes 1376288 | tf_op jit(solution)/shard_map/all_to_all | solution.py:30
  280.9 1.7 convert_reduce_fusion.1
  282.6 0.7 slice_bitcast_fusion.3
  (36 shorter events, 2.5 us)
Async XLA Ops:
  0.6 33.5 %copy-start = (bf16[1024,672]{0,1:T(8,128)(2,1)S(1)}, bf16[1024,672]{0,1:T(8,128)(2,1)}, u32[]{:S(2)}) copy-start(bf16[1024,672]{0,1:T(8,128)(2,1)} %param.14) | copy-start | bytes 4128772
  42.2 5.6 %copy-start.3 = (bf16[1024,256]{1,0:T(8,128)(2,1)S(1)}, bf16[1024,256]{1,0:T(8,128)(2,1)}, u32[]{:S(2)}) copy-start(bf16[1024,256]{1,0:T(8,128)(2,1)} %param.15) | copy-start | bytes 1572868
  42.2 55.6 %all-to-all-start = ((bf16[8,1024,2,128]{1,3,2,0:T(8,128)(2,1)}), bf16[8,1024,2,128]{1,3,2,0:T(8,128)(2,1)}, u32[]{:S(2)}, u32[]{:S(2)}) async-start(bf16[8,1024,2,128]{1,3,2,0:T(8,128)(2,1)} %bitcast.99), calls=%async_computation | async-start | bytes 8388608 | tf_op jit(solution)/shard_map/all_to_all | solution.py:30
  101.0 4.9 %copy-start.8 = (f32[128]{0:T(128)S(1)}, f32[128]{0:T(128)}, u32[]{:S(2)}) copy-start(f32[128]{0:T(128)} %param.19) | copy-start | bytes 1540
  102.6 12.0 %copy-start.9 = (f32[128]{0:T(128)S(1)}, f32[128]{0:T(128)}, u32[]{:S(2)}) copy-start(f32[128]{0:T(128)} %param.18) | copy-start | bytes 1540
  106.1 0.7 copy-start.6
  108.6 10.8 %collective-permute-start = (bf16[2,1024,1,128]{3,1,2,0:T(8,128)(2,1)}, bf16[2,1024,1,128]{3,1,2,0:T(8,128)(2,1)}, u32[]{:S(2)}, u32[]{:S(2)}) collective-permute-start(bf16[2,1024,1,128]{3,1,2,0:T(8,128)(2,1)} %pad_maximum_fusion), channel_id=1, source_target_pairs={{0,8},{8,16},{16,24},{24,32},{32,40},{40,48},{48,56},{56,64},{64,7... | collective-permute-start | bytes 1572872 | tf_op jit(solution)/shard_map/ppermute | solution.py:21
  114.6 4.8 %copy-start.5 = (bf16[1024,1,128]{2,0,1:T(8,128)(2,1)S(1)}, bf16[1024,1,128]{2,0,1:T(8,128)(2,1)}, u32[]{:S(2)}) copy-start(bf16[1024,1,128]{2,0,1:T(8,128)(2,1)} %copy.65) | copy-start | bytes 786436
  114.6 4.8 %copy-start.7 = (bf16[1,1024,1,128]{3,1,2,0:T(8,128)(2,1)S(1)}, bf16[1,1024,1,128]{3,1,2,0:T(8,128)(2,1)}, u32[]{:S(2)}) copy-start(bf16[1,1024,1,128]{3,1,2,0:T(8,128)(2,1)} %copy-done.6) | copy-start | bytes 786436
  117.1 1.0 copy-start.1
  137.8 9.9 %collective-permute-start.1 = (bf16[2,1024,1,128]{3,1,2,0:T(8,128)(2,1)S(1)}, bf16[2,1024,1,128]{3,1,2,0:T(8,128)(2,1)S(1)}, u32[]{:S(2)}, u32[]{:S(2)}) collective-permute-start(bf16[2,1024,1,128]{3,1,2,0:T(8,128)(2,1)S(1)} %slice.108), channel_id=1, source_target_pairs={{8,0},{16,8},{24,16},{32,24},{40,32},{48,40},{56,48},{64,56},{72,6... | collective-permute-start | bytes 1572872 | tf_op jit(solution)/shard_map/ppermute | solution.py:21
  152.5 54.9 %all-to-all-start.1 = ((bf16[8,1024,2,128]{3,1,2,0:T(8,128)(2,1)}), bf16[8,1024,2,128]{3,1,2,0:T(8,128)(2,1)}, u32[]{:S(2)}, u32[]{:S(2)}) async-start(bf16[8,1024,2,128]{3,1,2,0:T(8,128)(2,1)} %broadcast_in_dim.18), calls=%async_computation.1 | async-start | bytes 8388608 | tf_op jit(solution)/shard_map/all_to_all | solution.py:30
  221.3 3.8 %collective-permute-start.2 = (bf16[2,16,32,672]{3,2,1,0:T(8,128)(2,1)}, bf16[2,16,32,672]{3,2,1,0:T(8,128)(2,1)}, u32[]{:S(2)}, u32[]{:S(2)}) collective-permute-start(bf16[2,16,32,672]{3,2,1,0:T(8,128)(2,1)} %select_bitcast_fusion), channel_id=1, source_target_pairs={{0,8},{8,0},{1,9},{9,1},{2,10},{10,2},{3,11},{11,3},{4,12},{12,4},... | collective-permute-start | bytes 4128776 | tf_op jit(solution)/shard_map/ppermute | solution.py:156
  228.7 52.2 %all-to-all-start.2 = ((bf16[16,2,32,672]{3,2,1,0:T(8,128)(2,1)}), bf16[16,2,32,672]{3,2,1,0:T(8,128)(2,1)}, u32[]{:S(2)}, u32[]{:S(2)}) async-start(bf16[16,2,32,672]{3,2,1,0:T(8,128)(2,1)} %copy.56), calls=%async_computation.2 | async-start | bytes 3145728 | tf_op jit(solution)/shard_map/all_to_all | solution.py:30
  245.2 1.7 copy-start.2
  245.7 3.6 %copy-start.4 = (bf16[2,32,32,672]{3,2,1,0:T(8,128)(2,1)S(1)}, bf16[2,32,32,672]{3,2,1,0:T(8,128)(2,1)}, u32[]{:S(2)}) copy-start(bf16[2,32,32,672]{3,2,1,0:T(8,128)(2,1)} %shard_map.124) | copy-start | bytes 8257540

commit v10 on v9

--- a/solution.py
+++ b/solution.py
@@ -155,7 +155,10 @@
     send = jnp.take(split, 1 - core, axis=2)
     pair = (keep.astype(jnp.float32) + lax.ppermute(send, "core", SWAP).astype(jnp.float32))
     pair = pair.astype(jnp.bfloat16).transpose(1, 0, 2, 3)
-    return jnp.sum(exchange(pair, CHIP).astype(jnp.float32), axis=0)
+    levels = lax.axis_size("level")
+    by_row = pair.reshape((levels, chips // levels) + pair.shape[1:]).transpose(1, 0, 2, 3, 4)
+    part = jnp.sum(exchange(by_row, "row").astype(jnp.float32), axis=0)
+    return jnp.sum(exchange(part.astype(jnp.bfloat16), "level").astype(jnp.float32), axis=0)
 
 
 def attend_block(

time: 284 us -> 281 us (0.989)
  waiting for transfers between devices: 134 us -> 124 us
  starting transfers between devices: 27.2 us -> 31.8 us
    all_to_all x3 -> x4, waiting for transfers between devices: 124 us -> 114 us  [exchange(): return lax.all_to_all(blocks, axis, 0, 0)]
    all_to_all x3 -> x4, starting transfers between devices: 21.5 us -> 26.1 us  [exchange(): return lax.all_to_all(blocks, axis, 0, 0)]
  transfers between devices with their start and end apart: 6 -> 7, of which waited for: 6 -> 7; matrix products, arithmetic and copies ran while one was open for 9% -> 9% of each run, Pallas kernels for 0% -> 0%
where the time goes in v10:
time: 281 us; the launch traced here: 280 us
  waiting for transfers between devices  124 us (44%)
  Pallas kernels  46.9 us (17%)
  local copies, waits for them, and re-layouts  32.8 us (12%)
  starting transfers between devices  31.8 us (11%)
  other arithmetic  23.9 us (9%)
  matrix products  19.4 us (7%)
    all_to_all x4, waiting for transfers between devices, exchange(): return lax.all_to_all(blocks, axis, 0, 0)  114 us
    pallas_call x1, Pallas kernels, gather_seq(): pl.pallas_call(functools.partial(gather_kernel, levels, rows), out_shape=...  31.9 us
    all_to_all x4, starting transfers between devices, exchange(): return lax.all_to_all(blocks, axis, 0, 0)  26.1 us
    pallas_call x1, Pallas kernels, attend(): pl.pallas_call(attention_kernel, out_shape=(jax.ShapeDtypeStruct((rows, 2...  14.9 us
    dot_general x1, matrix products, body(): jnp.einsum('htkc,khcf->tf', grads_all, weight_heads, preferred_element_ty...  7.3 us
    ppermute x2, waiting for transfers between devices, from_behind(): return lax.ppermute(array, axis, pairs)  6.92 us
    dot_general x1, matrix products, body(): jnp.einsum('htkc,tf->khcf', grads_all, normed, preferred_element_type=jnp...  6.51 us
  transfers between devices with their start and end apart: 7, of which 7 were waited for; matrix products, arithmetic and copies ran while one was open for 9% of the time, Pallas kernels for 0%

profile of v10, /device:TPU:2, one launch (start us, length us, event | category | flops | bytes accessed | tf_op | source)
XLA Modules:
  0.0 280.0 jit_solution(5225561893576883884)
XLA Ops:
  0.6 1.6 maximum_bitcast_fusion.x_ref
  2.2 31.9 %shard_map.124 = bf16[2,32,32,672]{3,2,1,0:T(8,128)(2,1)} custom-call(bf16[2,1,32,672]{3,2,1,0:T(8,128)(2,1)} %maximum_bitcast_fusion.x_ref), custom_call_target="tpu_custom_call" | custom-call | tf_op jit(solution)/shard_map/pallas_call | solution.py:132
  34.2 5.5 %convolution_convert_fusion = bf16[2,1024,1024]{2,1,0:T(8,128)(2,1)S(1)} fusion(bf16[2,1024,672]{2,1,0:T(8,128)(2,1)} %bitcast.112, bf16[1024,672]{0,1:T(8,128)(2,1)S(1)} %copy-done), kind=kOutput, calls=%fused_computation.7 | convolution fusion | flops 2820669440 | bytes 8323072 | tf_op jit(solution)/shard_map/dot_general | solution.py:259
  39.7 2.5 copy.95
  42.3 5.6 %all-to-all-start = ((bf16[8,1024,2,128]{1,3,2,0:T(8,128)(2,1)}), bf16[8,1024,2,128]{1,3,2,0:T(8,128)(2,1)}, u32[]{:S(2)}, u32[]{:S(2)}) async-start(bf16[8,1024,2,128]{1,3,2,0:T(8,128)(2,1)} %bitcast.103), calls=%async_computation | async-start | bytes 8388608 | tf_op jit(solution)/shard_map/all_to_all | solution.py:30
  48.3 1.2 multiply_reduce_fusion.1
  49.7 48.2 %all-to-all-done = bf16[8,1024,2,128]{1,3,2,0:T(8,128)(2,1)} async-done(((bf16[8,1024,2,128]{1,3,2,0:T(8,128)(2,1)}), bf16[8,1024,2,128]{1,3,2,0:T(8,128)(2,1)}, u32[]{:S(2)}, u32[]{:S(2)}) %all-to-all-start) | async-done | bytes 4194336 | tf_op jit(solution)/shard_map/all_to_all | solution.py:30
  97.9 3.2 %convert_reduce_fusion = f32[1024,2,128]{0,2,1:T(8,128)S(1)} fusion(bf16[8,1024,2,128]{1,3,2,0:T(8,128)(2,1)} %all-to-all-done), kind=kLoop, calls=%fused_computation | loop fusion | flops 3932160 | bytes 5242880 | tf_op jit(solution)/shard_map/reduce_sum | solution.py:264
  101.1 0.7 slice.83
  101.8 0.8 slice.82
  102.7 1.2 copy.82
  103.9 1.8 copy.83
  106.2 0.7 copy-done.5
  106.9 1.8 pad_maximum_fusion
  108.7 1.9 collective-permute-start
  110.6 1.3 pad_dynamic-slice_fusion
  112.6 1.0 copy.65.qseg_ref
  113.6 1.0 copy.59
  114.6 2.4 mul.207
  117.1 1.0 copy-done.1
  118.0 1.0 fusion.10.q_ref
  119.5 1.1 maximum_maximum_fusion
  120.6 1.0 slice_bitcast_fusion.1
  121.6 14.9 %shard_map.125 = (bf16[1024,256]{1,0:T(8,128)(2,1)}, f32[1024,256]{1,0:T(8,128)}, f32[2,2048,128]{2,1,0:T(8,128)}) custom-call(bf16[1024,256]{1,0:T(8,128)(2,1)} %fusion.10.q_ref, bf16[1024,256]{1,0:T(8,128)(2,1)} %do_ref.1, bf16[2048,128]{1,0:T(8,128)(2,1)} %get-tuple-element.44.k_ref, bf16[2048,128]{1,0:T(8,128)(2,1)} %get-tuple-element.43.v_ref, ...), custom_call_target="tpu_custom_call" | custom-call | flops 6442450944 | bytes 8388608 | tf_op jit(solution)/shard_map/pallas_call | solution.py:232
  136.5 1.3 slice.108
  137.8 3.4 %collective-permute-start.1 = (bf16[2,1024,1,128]{3,1,2,0:T(8,128)(2,1)S(1)}, bf16[2,1024,1,128]{3,1,2,0:T(8,128)(2,1)S(1)}, u32[]{:S(2)}, u32[]{:S(2)}) collective-permute-start(bf16[2,1024,1,128]{3,1,2,0:T(8,128)(2,1)S(1)} %slice.108), channel_id=1, source_target_pairs={{8,0},{16,8},{24,16},{32,24},{40,32},{48,40},{56,48},{64,56},{72,6... | collective-permute-start | bytes 1572872 | tf_op jit(solution)/shard_map/ppermute | solution.py:21
  141.2 6.5 %collective-permute-done.1 = bf16[2,1024,1,128]{3,1,2,0:T(8,128)(2,1)S(1)} collective-permute-done((bf16[2,1024,1,128]{3,1,2,0:T(8,128)(2,1)S(1)}, bf16[2,1024,1,128]{3,1,2,0:T(8,128)(2,1)S(1)}, u32[]{:S(2)}, u32[]{:S(2)}) %collective-permute-start.1) | collective-permute-done | bytes 524320 | tf_op jit(solution)/shard_map/ppermute | solution.py:21
  147.7 1.3 slice_add_fusion
  149.7 2.8 broadcast_in_dim.18
  152.4 4.5 %all-to-all-start.1 = ((bf16[8,1024,2,128]{3,1,2,0:T(8,128)(2,1)}), bf16[8,1024,2,128]{3,1,2,0:T(8,128)(2,1)}, u32[]{:S(2)}, u32[]{:S(2)}) async-start(bf16[8,1024,2,128]{3,1,2,0:T(8,128)(2,1)} %broadcast_in_dim.18), calls=%async_computation.1 | async-start | bytes 8388608 | tf_op jit(solution)/shard_map/all_to_all | solution.py:30
  157.0 50.3 %all-to-all-done.1 = bf16[8,1024,2,128]{3,1,2,0:T(8,128)(2,1)} async-done(((bf16[8,1024,2,128]{3,1,2,0:T(8,128)(2,1)}), bf16[8,1024,2,128]{3,1,2,0:T(8,128)(2,1)}, u32[]{:S(2)}, u32[]{:S(2)}) %all-to-all-start.1) | async-done | bytes 4194336 | tf_op jit(solution)/shard_map/all_to_all | solution.py:30
  207.4 6.5 %convert_bitcast_fusion = bf16[2,8,128,672]{2,3,0,1:T(8,128)(2,1)} fusion(bf16[8,1024,2,128]{3,1,2,0:T(8,128)(2,1)} %all-to-all-done.1, bf16[1024,672]{0,1:T(8,128)(2,1)S(1)} %copy-done), kind=kOutput, calls=%fused_computation.6 | convolution fusion | flops 2819948544 | bytes 8323072 | tf_op jit(solution)/shard_map/htkc,tf->khcf/dot_general | solution.py:307
  213.9 4.6 %copy.69 = bf16[2,8,128,672]{3,2,1,0:T(8,128)(2,1)} copy(bf16[2,8,128,672]{2,3,0,1:T(8,128)(2,1)} %convert_bitcast_fusion) | data formatting | bytes 5505024 | tf_op jit(solution)/shard_map/convert_element_type | solution.py:309
  218.5 2.7 select_bitcast_fusion
  221.6 3.4 %collective-permute-done.2 = bf16[2,16,32,672]{3,2,1,0:T(8,128)(2,1)} collective-permute-done((bf16[2,16,32,672]{3,2,1,0:T(8,128)(2,1)}, bf16[2,16,32,672]{3,2,1,0:T(8,128)(2,1)}, u32[]{:S(2)}, u32[]{:S(2)}) %collective-permute-start.2) | collective-permute-done | bytes 1376288 | tf_op jit(solution)/shard_map/ppermute | solution.py:156
  225.0 2.4 add_convert_fusion
  227.4 1.3 copy.96
  228.7 5.1 %all-to-all-start.2 = ((bf16[4,4,2,32,672]{4,3,1,2,0:T(8,128)(2,1)}), bf16[4,4,2,32,672]{4,3,1,2,0:T(8,128)(2,1)}, u32[]{:S(2)}, u32[]{:S(2)}) async-start(bf16[4,4,2,32,672]{4,3,1,2,0:T(8,128)(2,1)} %bitcast.108), calls=%async_computation.2 | async-start | bytes 3145728 | tf_op jit(solution)/shard_map/all_to_all | solution.py:30
  233.7 2.7 reshape.289
  236.5 2.4 multiply_reduce_fusion
  239.3 1.2 broadcast_in_dim.19
  240.6 2.4 fusion.7
  243.0 10.4 %all-to-all-done.2 = bf16[4,4,2,32,672]{4,3,1,2,0:T(8,128)(2,1)} async-done(((bf16[4,4,2,32,672]{4,3,1,2,0:T(8,128)(2,1)}), bf16[4,4,2,32,672]{4,3,1,2,0:T(8,128)(2,1)}, u32[]{:S(2)}, u32[]{:S(2)}) %all-to-all-start.2) | async-done | bytes 1376288 | tf_op jit(solution)/shard_map/all_to_all | solution.py:30
  253.4 1.7 reduce_sum.76
  255.1 0.8 copy.73
  255.9 10.9 %all-to-all-start.3 = ((bf16[4,2,32,672]{3,2,1,0:T(8,128)(2,1)}), bf16[4,2,32,672]{3,2,1,0:T(8,128)(2,1)S(1)}, u32[]{:S(2)}, u32[]{:S(2)}) async-start(bf16[4,2,32,672]{3,2,1,0:T(8,128)(2,1)} %copy.73), calls=%async_computation.3 | async-start | bytes 786432 | tf_op jit(solution)/shard_map/all_to_all | solution.py:30
  266.8 7.3 %bitcast_convert_fusion = bf16[1024,672]{0,1:T(8,128)(2,1)} fusion(bf16[8,1024,2,128]{3,1,2,0:T(8,128)(2,1)} %all-to-all-done.1, bf16[2,8,128,672]{3,2,1,0:T(8,128)(2,1)} %bitcast.113), kind=kOutput, calls=%fused_computation.5 | convolution fusion | flops 2819260416 | bytes 8323072 | tf_op jit(solution)/shard_map/htkc,khcf->tf/dot_general | solution.py:304
  274.1 5.1 %all-to-all-done.3 = bf16[4,2,32,672]{3,2,1,0:T(8,128)(2,1)S(1)} async-done(((bf16[4,2,32,672]{3,2,1,0:T(8,128)(2,1)}), bf16[4,2,32,672]{3,2,1,0:T(8,128)(2,1)S(1)}, u32[]{:S(2)}, u32[]{:S(2)}) %all-to-all-start.3) | async-done | bytes 344096 | tf_op jit(solution)/shard_map/all_to_all | solution.py:30
  (38 shorter events, 4.5 us)
Async XLA Ops:
  0.6 33.5 %copy-start = (bf16[1024,672]{0,1:T(8,128)(2,1)S(1)}, bf16[1024,672]{0,1:T(8,128)(2,1)}, u32[]{:S(2)}) copy-start(bf16[1024,672]{0,1:T(8,128)(2,1)} %param.14) | copy-start | bytes 4128772
  42.3 5.6 %copy-start.3 = (bf16[1024,256]{1,0:T(8,128)(2,1)S(1)}, bf16[1024,256]{1,0:T(8,128)(2,1)}, u32[]{:S(2)}) copy-start(bf16[1024,256]{1,0:T(8,128)(2,1)} %param.15) | copy-start | bytes 1572868
  42.3 55.6 %all-to-all-start = ((bf16[8,1024,2,128]{1,3,2,0:T(8,128)(2,1)}), bf16[8,1024,2,128]{1,3,2,0:T(8,128)(2,1)}, u32[]{:S(2)}, u32[]{:S(2)}) async-start(bf16[8,1024,2,128]{1,3,2,0:T(8,128)(2,1)} %bitcast.103), calls=%async_computation | async-start | bytes 8388608 | tf_op jit(solution)/shard_map/all_to_all | solution.py:30
  101.1 4.9 %copy-start.7 = (f32[128]{0:T(128)S(1)}, f32[128]{0:T(128)}, u32[]{:S(2)}) copy-start(f32[128]{0:T(128)} %param.19) | copy-start | bytes 1540
  102.7 12.0 %copy-start.8 = (f32[128]{0:T(128)S(1)}, f32[128]{0:T(128)}, u32[]{:S(2)}) copy-start(f32[128]{0:T(128)} %param.18) | copy-start | bytes 1540
  106.2 0.7 copy-start.5
  108.7 10.8 %collective-permute-start = (bf16[2,1024,1,128]{3,1,2,0:T(8,128)(2,1)}, bf16[2,1024,1,128]{3,1,2,0:T(8,128)(2,1)}, u32[]{:S(2)}, u32[]{:S(2)}) collective-permute-start(bf16[2,1024,1,128]{3,1,2,0:T(8,128)(2,1)} %pad_maximum_fusion), channel_id=1, source_target_pairs={{0,8},{8,16},{16,24},{24,32},{32,40},{40,48},{48,56},{56,64},{64,7... | collective-permute-start | bytes 1572872 | tf_op jit(solution)/shard_map/ppermute | solution.py:21
  114.6 4.8 %copy-start.4 = (bf16[1024,1,128]{2,0,1:T(8,128)(2,1)S(1)}, bf16[1024,1,128]{2,0,1:T(8,128)(2,1)}, u32[]{:S(2)}) copy-start(bf16[1024,1,128]{2,0,1:T(8,128)(2,1)} %copy.83) | copy-start | bytes 786436
  114.6 4.8 %copy-start.6 = (bf16[1,1024,1,128]{3,1,2,0:T(8,128)(2,1)S(1)}, bf16[1,1024,1,128]{3,1,2,0:T(8,128)(2,1)}, u32[]{:S(2)}) copy-start(bf16[1,1024,1,128]{3,1,2,0:T(8,128)(2,1)} %copy-done.5) | copy-start | bytes 786436
  117.1 1.0 copy-start.1
  137.8 9.9 %collective-permute-start.1 = (bf16[2,1024,1,128]{3,1,2,0:T(8,128)(2,1)S(1)}, bf16[2,1024,1,128]{3,1,2,0:T(8,128)(2,1)S(1)}, u32[]{:S(2)}, u32[]{:S(2)}) collective-permute-start(bf16[2,1024,1,128]{3,1,2,0:T(8,128)(2,1)S(1)} %slice.108), channel_id=1, source_target_pairs={{8,0},{16,8},{24,16},{32,24},{40,32},{48,40},{56,48},{64,56},{72,6... | collective-permute-start | bytes 1572872 | tf_op jit(solution)/shard_map/ppermute | solution.py:21
  152.4 54.9 %all-to-all-start.1 = ((bf16[8,1024,2,128]{3,1,2,0:T(8,128)(2,1)}), bf16[8,1024,2,128]{3,1,2,0:T(8,128)(2,1)}, u32[]{:S(2)}, u32[]{:S(2)}) async-start(bf16[8,1024,2,128]{3,1,2,0:T(8,128)(2,1)} %broadcast_in_dim.18), calls=%async_computation.1 | async-start | bytes 8388608 | tf_op jit(solution)/shard_map/all_to_all | solution.py:30
  221.2 3.8 %collective-permute-start.2 = (bf16[2,16,32,672]{3,2,1,0:T(8,128)(2,1)}, bf16[2,16,32,672]{3,2,1,0:T(8,128)(2,1)}, u32[]{:S(2)}, u32[]{:S(2)}) collective-permute-start(bf16[2,16,32,672]{3,2,1,0:T(8,128)(2,1)} %select_bitcast_fusion), channel_id=1, source_target_pairs={{0,8},{8,0},{1,9},{9,1},{2,10},{10,2},{3,11},{11,3},{4,12},{12,4},... | collective-permute-start | bytes 4128776 | tf_op jit(solution)/shard_map/ppermute | solution.py:156
  228.7 24.7 %all-to-all-start.2 = ((bf16[4,4,2,32,672]{4,3,1,2,0:T(8,128)(2,1)}), bf16[4,4,2,32,672]{4,3,1,2,0:T(8,128)(2,1)}, u32[]{:S(2)}, u32[]{:S(2)}) async-start(bf16[4,4,2,32,672]{4,3,1,2,0:T(8,128)(2,1)} %bitcast.108), calls=%async_computation.2 | async-start | bytes 3145728 | tf_op jit(solution)/shard_map/all_to_all | solution.py:30
  238.9 1.7 copy-start.2
  255.9 23.3 %all-to-all-start.3 = ((bf16[4,2,32,672]{3,2,1,0:T(8,128)(2,1)}), bf16[4,2,32,672]{3,2,1,0:T(8,128)(2,1)S(1)}, u32[]{:S(2)}, u32[]{:S(2)}) async-start(bf16[4,2,32,672]{3,2,1,0:T(8,128)(2,1)} %copy.73), calls=%async_computation.3 | async-start | bytes 786432 | tf_op jit(solution)/shard_map/all_to_all | solution.py:30

commit v11 on v10

--- a/solution.py
+++ b/solution.py
@@ -148,16 +148,10 @@
 
 
 def reduce_seq(blocks):
-    chips = blocks.shape[1] // 2
-    split = blocks.reshape((blocks.shape[0], chips, 2) + blocks.shape[2:])
-    core = lax.axis_index("core")
-    keep = jnp.take(split, core, axis=2)
-    send = jnp.take(split, 1 - core, axis=2)
-    pair = (keep.astype(jnp.float32) + lax.ppermute(send, "core", SWAP).astype(jnp.float32))
-    pair = pair.astype(jnp.bfloat16).transpose(1, 0, 2, 3)
     levels = lax.axis_size("level")
-    by_row = pair.reshape((levels, chips // levels) + pair.shape[1:]).transpose(1, 0, 2, 3, 4)
-    part = jnp.sum(exchange(by_row, "row").astype(jnp.float32), axis=0)
+    split = blocks.reshape((blocks.shape[0], levels, -1) + blocks.shape[2:])
+    by_ring = split.transpose(2, 1, 0, 3, 4)
+    part = jnp.sum(exchange(by_ring, ("row", "core")).astype(jnp.float32), axis=0)
     return jnp.sum(exchange(part.astype(jnp.bfloat16), "level").astype(jnp.float32), axis=0)
 
 

time: 281 us -> 290 us (1.032)
  blocking collectives: 0 us -> 53.3 us
  waiting for transfers between devices: 124 us -> 88.1 us
  other arithmetic: 23.9 us -> 19.5 us
  starting transfers between devices: 31.8 us -> 27.7 us
    all_to_all x0 -> x1, blocking collectives: none -> 53.3 us  [exchange(): return lax.all_to_all(blocks, axis, 0, 0)]
    all_to_all x4 -> x3, waiting for transfers between devices: 114 us -> 81.2 us  [exchange(): return lax.all_to_all(blocks, axis, 0, 0)]
    transpose x0 -> x1, local copies, waits for them, and re-layouts: none -> 3.84 us  [reduce_seq(): by_ring = split.transpose(2, 1, 0, 3, 4)]
    all_to_all x4 -> x3, starting transfers between devices: 26.1 us -> 22.3 us  [exchange(): return lax.all_to_all(blocks, axis, 0, 0)]
    ppermute x1 -> x0, waiting for transfers between devices: 3.4 us -> none  [reduce_seq(): lax.ppermute(send, 'core', SWAP).astype(jnp.float32)]
    unnamed x20 -> x22, local copies, waits for them, and re-layouts: 4.74 us -> 6.67 us
  transfers between devices with their start and end apart: 7 -> 5, of which waited for: 7 -> 5; matrix products, arithmetic and copies ran while one was open for 9% -> 9% of each run, Pallas kernels for 0% -> 0%
where the time goes in v11:
time: 290 us; the launch traced here: 289 us
  waiting for transfers between devices  88.1 us (30%)
  blocking collectives  53.3 us (18%)
  Pallas kernels  47 us (16%)
  local copies, waits for them, and re-layouts  35.3 us (12%)
  starting transfers between devices  27.7 us (10%)
  other arithmetic  19.5 us (7%)
  matrix products  17.2 us (6%)
    all_to_all x3, waiting for transfers between devices, exchange(): return lax.all_to_all(blocks, axis, 0, 0)  81.2 us
    all_to_all x1, blocking collectives, exchange(): return lax.all_to_all(blocks, axis, 0, 0)  53.3 us
    pallas_call x1, Pallas kernels, gather_seq(): pl.pallas_call(functools.partial(gather_kernel, levels, rows), out_shape=...  32.1 us
    all_to_all x3, starting transfers between devices, exchange(): return lax.all_to_all(blocks, axis, 0, 0)  22.3 us
    pallas_call x1, Pallas kernels, attend(): pl.pallas_call(attention_kernel, out_shape=(jax.ShapeDtypeStruct((rows, 2...  14.9 us
    dot_general x1, matrix products, body(): jnp.einsum('htkc,khcf->tf', grads_all, weight_heads, preferred_element_ty...  7.3 us
    ppermute x2, waiting for transfers between devices, from_behind(): return lax.ppermute(array, axis, pairs)  6.9 us
    unnamed x22, local copies, waits for them, and re-layouts  6.67 us
  transfers between devices with their start and end apart: 5, of which 5 were waited for; matrix products, arithmetic and copies ran while one was open for 9% of the time, Pallas kernels for 0%

profile of v11, /device:TPU:2, one launch (start us, length us, event | category | flops | bytes accessed | tf_op | source)
XLA Modules:
  0.0 288.8 jit_solution(16530816655311014328)
XLA Ops:
  0.6 1.6 maximum_bitcast_fusion.x_ref
  2.2 32.1 %shard_map.124 = bf16[2,32,32,672]{3,2,1,0:T(8,128)(2,1)} custom-call(bf16[2,1,32,672]{3,2,1,0:T(8,128)(2,1)} %maximum_bitcast_fusion.x_ref), custom_call_target="tpu_custom_call" | custom-call | tf_op jit(solution)/shard_map/pallas_call | solution.py:132
  34.3 5.5 %convolution_convert_fusion = bf16[2,1024,1024]{2,1,0:T(8,128)(2,1)S(1)} fusion(bf16[2,1024,672]{2,1,0:T(8,128)(2,1)} %bitcast.93, bf16[1024,672]{0,1:T(8,128)(2,1)S(1)} %copy-done), kind=kOutput, calls=%fused_computation.6 | convolution fusion | flops 2820669440 | bytes 8323072 | tf_op jit(solution)/shard_map/dot_general | solution.py:253
  39.8 2.4 copy.87
  42.3 5.6 %all-to-all-start = ((bf16[8,1024,2,128]{1,3,2,0:T(8,128)(2,1)}), bf16[8,1024,2,128]{1,3,2,0:T(8,128)(2,1)}, u32[]{:S(2)}, u32[]{:S(2)}) async-start(bf16[8,1024,2,128]{1,3,2,0:T(8,128)(2,1)} %bitcast.87), calls=%async_computation | async-start | bytes 8388608 | tf_op jit(solution)/shard_map/all_to_all | solution.py:30
  47.8 0.5 reshape.279
  48.3 1.2 multiply_reduce_fusion.1
  49.7 48.2 %all-to-all-done = bf16[8,1024,2,128]{1,3,2,0:T(8,128)(2,1)} async-done(((bf16[8,1024,2,128]{1,3,2,0:T(8,128)(2,1)}), bf16[8,1024,2,128]{1,3,2,0:T(8,128)(2,1)}, u32[]{:S(2)}, u32[]{:S(2)}) %all-to-all-start) | async-done | bytes 4194336 | tf_op jit(solution)/shard_map/all_to_all | solution.py:30
  97.9 3.2 %convert_reduce_fusion = f32[1024,2,128]{0,2,1:T(8,128)S(1)} fusion(bf16[8,1024,2,128]{1,3,2,0:T(8,128)(2,1)} %all-to-all-done), kind=kLoop, calls=%fused_computation | loop fusion | flops 3932160 | bytes 5242880 | tf_op jit(solution)/shard_map/reduce_sum | solution.py:258
  101.1 0.7 slice.70
  101.8 0.8 slice.69
  102.7 1.2 copy.75
  103.9 1.8 copy.76
  106.1 0.7 copy-done.6
  106.8 1.8 pad_maximum_fusion
  108.6 1.9 collective-permute-start
  110.5 1.3 pad_dynamic-slice_fusion
  111.9 0.7 dynamic_slice.6
  112.5 1.0 copy.60.qseg_ref
  113.6 1.0 copy.54
  114.6 2.4 mul.207
  117.1 1.0 copy-done.1
  118.0 1.0 fusion.9.q_ref
  119.4 1.1 maximum_maximum_fusion
  120.6 1.1 slice_bitcast_fusion.1
  121.6 14.9 %shard_map.125 = (bf16[1024,256]{1,0:T(8,128)(2,1)}, f32[1024,256]{1,0:T(8,128)}, f32[2,2048,128]{2,1,0:T(8,128)}) custom-call(bf16[1024,256]{1,0:T(8,128)(2,1)} %fusion.9.q_ref, bf16[1024,256]{1,0:T(8,128)(2,1)} %do_ref.1, bf16[2048,128]{1,0:T(8,128)(2,1)} %get-tuple-element.32.k_ref, bf16[2048,128]{1,0:T(8,128)(2,1)} %get-tuple-element.31.v_ref, ...), custom_call_target="tpu_custom_call" | custom-call | flops 6442450944 | bytes 8388608 | tf_op jit(solution)/shard_map/pallas_call | solution.py:226
  136.5 1.3 slice.95
  137.8 3.4 %collective-permute-start.1 = (bf16[2,1024,1,128]{3,1,2,0:T(8,128)(2,1)S(1)}, bf16[2,1024,1,128]{3,1,2,0:T(8,128)(2,1)S(1)}, u32[]{:S(2)}, u32[]{:S(2)}) collective-permute-start(bf16[2,1024,1,128]{3,1,2,0:T(8,128)(2,1)S(1)} %slice.95), channel_id=1, source_target_pairs={{8,0},{16,8},{24,16},{32,24},{40,32},{48,40},{56,48},{64,56},{72,6... | collective-permute-start | bytes 1572872 | tf_op jit(solution)/shard_map/ppermute | solution.py:21
  141.2 6.5 %collective-permute-done.1 = bf16[2,1024,1,128]{3,1,2,0:T(8,128)(2,1)S(1)} collective-permute-done((bf16[2,1024,1,128]{3,1,2,0:T(8,128)(2,1)S(1)}, bf16[2,1024,1,128]{3,1,2,0:T(8,128)(2,1)S(1)}, u32[]{:S(2)}, u32[]{:S(2)}) %collective-permute-start.1) | collective-permute-done | bytes 524320 | tf_op jit(solution)/shard_map/ppermute | solution.py:21
  147.7 1.3 slice_add_fusion
  149.7 0.8 broadcast_in_dim.12
  150.5 53.3 %all_to_all.20 = bf16[8,1024,2,128]{3,1,2,0:T(8,128)(2,1)S(1)} all-to-all(bf16[8,1024,2,128]{3,1,2,0:T(8,128)(2,1)S(1)} %broadcast_in_dim.12), channel_id=1, replica_groups=mesh['level'=4,'row'=4,'core'=2,'uly'=8] {'uly'}, dimensions={0} | all-to-all | bytes 8388608 | tf_op jit(solution)/shard_map/all_to_all | solution.py:30
  203.8 1.9 copy-done.4
  205.7 4.3 %convert_bitcast_fusion = bf16[2,8,128,672]{2,3,0,1:T(8,128)(2,1)} fusion(bf16[8,1024,2,128]{3,1,2,0:T(8,128)(2,1)S(1)} %all_to_all.20, bf16[1024,672]{0,1:T(8,128)(2,1)S(1)} %copy-done), kind=kOutput, calls=%fused_computation.5 | convolution fusion | flops 2819948544 | bytes 8323072 | tf_op jit(solution)/shard_map/htkc,tf->khcf/dot_general | solution.py:301
  210.1 4.6 %copy.64 = bf16[2,8,128,672]{3,2,1,0:T(8,128)(2,1)} copy(bf16[2,8,128,672]{2,3,0,1:T(8,128)(2,1)} %convert_bitcast_fusion) | data formatting | bytes 5505024 | tf_op jit(solution)/shard_map/convert_element_type | solution.py:303
  214.6 3.8 %copy.65 = bf16[8,4,2,32,672]{4,3,1,2,0:T(8,128)(2,1)} copy(bf16[8,4,2,32,672]{4,3,0,1,2:T(8,128)(2,1)} %bitcast.88) | data formatting | bytes 5505024 | tf_op jit(solution)/shard_map/transpose | solution.py:153
  218.5 5.3 %all-to-all-start.2 = ((bf16[8,4,2,32,672]{4,3,1,2,0:T(8,128)(2,1)}), bf16[8,4,2,32,672]{4,3,1,2,0:T(8,128)(2,1)}, u32[]{:S(2)}, u32[]{:S(2)}) async-start(bf16[8,4,2,32,672]{4,3,1,2,0:T(8,128)(2,1)} %copy.65), calls=%async_computation.2 | async-start | bytes 6291456 | tf_op jit(solution)/shard_map/all_to_all | solution.py:30
  223.8 2.7 reshape.285
  226.5 2.4 multiply_reduce_fusion
  229.4 1.2 broadcast_in_dim.13
  230.6 2.4 fusion.6
  233.0 27.9 %all-to-all-done.2 = bf16[8,4,2,32,672]{4,3,1,2,0:T(8,128)(2,1)} async-done(((bf16[8,4,2,32,672]{4,3,1,2,0:T(8,128)(2,1)}), bf16[8,4,2,32,672]{4,3,1,2,0:T(8,128)(2,1)}, u32[]{:S(2)}, u32[]{:S(2)}) %all-to-all-start.2) | async-done | bytes 2752544 | tf_op jit(solution)/shard_map/all_to_all | solution.py:30
  260.9 2.5 reduce_sum.76
  263.4 0.8 copy.67
  264.2 11.5 %all-to-all-start.3 = ((bf16[4,2,32,672]{3,2,1,0:T(8,128)(2,1)}), bf16[4,2,32,672]{3,2,1,0:T(8,128)(2,1)S(1)}, u32[]{:S(2)}, u32[]{:S(2)}) async-start(bf16[4,2,32,672]{3,2,1,0:T(8,128)(2,1)} %copy.67), calls=%async_computation.3 | async-start | bytes 786432 | tf_op jit(solution)/shard_map/all_to_all | solution.py:30
  275.7 7.3 %bitcast_convert_fusion = bf16[1024,672]{0,1:T(8,128)(2,1)} fusion(bf16[8,1024,2,128]{3,1,2,0:T(8,128)(2,1)} %copy-done.4, bf16[2,8,128,672]{3,2,1,0:T(8,128)(2,1)} %bitcast.94), kind=kOutput, calls=%fused_computation.4 | convolution fusion | flops 2819260416 | bytes 8323072 | tf_op jit(solution)/shard_map/htkc,khcf->tf/dot_general | solution.py:298
  283.0 5.1 %all-to-all-done.3 = bf16[4,2,32,672]{3,2,1,0:T(8,128)(2,1)S(1)} async-done(((bf16[4,2,32,672]{3,2,1,0:T(8,128)(2,1)}), bf16[4,2,32,672]{3,2,1,0:T(8,128)(2,1)S(1)}, u32[]{:S(2)}, u32[]{:S(2)}) %all-to-all-start.3) | async-done | bytes 344096 | tf_op jit(solution)/shard_map/all_to_all | solution.py:30
  288.1 0.7 slice_bitcast_fusion.3
  (35 shorter events, 2.3 us)
Async XLA Ops:
  0.6 33.7 %copy-start = (bf16[1024,672]{0,1:T(8,128)(2,1)S(1)}, bf16[1024,672]{0,1:T(8,128)(2,1)}, u32[]{:S(2)}) copy-start(bf16[1024,672]{0,1:T(8,128)(2,1)} %param.12) | copy-start | bytes 4128772
  42.3 5.6 %copy-start.3 = (bf16[1024,256]{1,0:T(8,128)(2,1)S(1)}, bf16[1024,256]{1,0:T(8,128)(2,1)}, u32[]{:S(2)}) copy-start(bf16[1024,256]{1,0:T(8,128)(2,1)} %param.13) | copy-start | bytes 1572868
  42.3 55.6 %all-to-all-start = ((bf16[8,1024,2,128]{1,3,2,0:T(8,128)(2,1)}), bf16[8,1024,2,128]{1,3,2,0:T(8,128)(2,1)}, u32[]{:S(2)}, u32[]{:S(2)}) async-start(bf16[8,1024,2,128]{1,3,2,0:T(8,128)(2,1)} %bitcast.87), calls=%async_computation | async-start | bytes 8388608 | tf_op jit(solution)/shard_map/all_to_all | solution.py:30
  101.1 4.9 %copy-start.8 = (f32[128]{0:T(128)S(1)}, f32[128]{0:T(128)}, u32[]{:S(2)}) copy-start(f32[128]{0:T(128)} %param.17) | copy-start | bytes 1540
  101.8 12.8 %copy-start.9 = (f32[128]{0:T(128)S(1)}, f32[128]{0:T(128)}, u32[]{:S(2)}) copy-start(f32[128]{0:T(128)} %param.16) | copy-start | bytes 1540
  106.1 0.7 copy-start.6
  108.6 10.8 %collective-permute-start = (bf16[2,1024,1,128]{3,1,2,0:T(8,128)(2,1)}, bf16[2,1024,1,128]{3,1,2,0:T(8,128)(2,1)}, u32[]{:S(2)}, u32[]{:S(2)}) collective-permute-start(bf16[2,1024,1,128]{3,1,2,0:T(8,128)(2,1)} %pad_maximum_fusion), channel_id=1, source_target_pairs={{0,8},{8,16},{16,24},{24,32},{32,40},{40,48},{48,56},{56,64},{64,7... | collective-permute-start | bytes 1572872 | tf_op jit(solution)/shard_map/ppermute | solution.py:21
  114.6 4.8 %copy-start.5 = (bf16[1024,1,128]{2,0,1:T(8,128)(2,1)S(1)}, bf16[1024,1,128]{2,0,1:T(8,128)(2,1)}, u32[]{:S(2)}) copy-start(bf16[1024,1,128]{2,0,1:T(8,128)(2,1)} %copy.76) | copy-start | bytes 786436
  114.6 4.8 %copy-start.7 = (bf16[1,1024,1,128]{3,1,2,0:T(8,128)(2,1)S(1)}, bf16[1,1024,1,128]{3,1,2,0:T(8,128)(2,1)}, u32[]{:S(2)}) copy-start(bf16[1,1024,1,128]{3,1,2,0:T(8,128)(2,1)} %copy-done.6) | copy-start | bytes 786436
  117.0 1.0 copy-start.1
  137.8 9.9 %collective-permute-start.1 = (bf16[2,1024,1,128]{3,1,2,0:T(8,128)(2,1)S(1)}, bf16[2,1024,1,128]{3,1,2,0:T(8,128)(2,1)S(1)}, u32[]{:S(2)}, u32[]{:S(2)}) collective-permute-start(bf16[2,1024,1,128]{3,1,2,0:T(8,128)(2,1)S(1)} %slice.95), channel_id=1, source_target_pairs={{8,0},{16,8},{24,16},{32,24},{40,32},{48,40},{56,48},{64,56},{72,6... | collective-permute-start | bytes 1572872 | tf_op jit(solution)/shard_map/ppermute | solution.py:21
  203.8 1.9 copy-start.4
  218.5 42.5 %all-to-all-start.2 = ((bf16[8,4,2,32,672]{4,3,1,2,0:T(8,128)(2,1)}), bf16[8,4,2,32,672]{4,3,1,2,0:T(8,128)(2,1)}, u32[]{:S(2)}, u32[]{:S(2)}) async-start(bf16[8,4,2,32,672]{4,3,1,2,0:T(8,128)(2,1)} %copy.65), calls=%async_computation.2 | async-start | bytes 6291456 | tf_op jit(solution)/shard_map/all_to_all | solution.py:30
  228.9 1.7 copy-start.2
  264.2 23.8 %all-to-all-start.3 = ((bf16[4,2,32,672]{3,2,1,0:T(8,128)(2,1)}), bf16[4,2,32,672]{3,2,1,0:T(8,128)(2,1)S(1)}, u32[]{:S(2)}, u32[]{:S(2)}) async-start(bf16[4,2,32,672]{3,2,1,0:T(8,128)(2,1)} %copy.67), calls=%async_computation.3 | async-start | bytes 786432 | tf_op jit(solution)/shard_map/all_to_all | solution.py:30

commit v12 on v10

--- a/solution.py
+++ b/solution.py
@@ -187,7 +187,7 @@
     return (attended, dquery, dkey, dvalue)
 
 
-def attention_kernel(q_ref, do_ref, k_ref, v_ref, qseg_ref, kseg_ref, out_ref, dq_ref, dkv_ref):
+def attention_kernel(pos_ref, gain_ref, q_ref, do_ref, k_ref, v_ref, out_ref, dq_ref, dkv_ref):
     rows = q_ref.shape[0]
     block = 256
     span = block + WINDOW
@@ -200,12 +200,16 @@
         v = v_ref[pl.ds(r0, span), :]
         row = lax.broadcasted_iota(jnp.int32, (block, span), 0)
         col = lax.broadcasted_iota(jnp.int32, (block, span), 1)
-        allowed = (col <= row + WINDOW) & (col > row)
-        allowed = allowed & (qseg_ref[pl.ds(r0, block), :] == kseg_ref[:, pl.ds(r0, span)])
+        query_pos = pos_ref[0] + r0 + row
+        key_pos = pos_ref[0] - WINDOW + r0 + col
+        allowed = (col <= row + WINDOW) & (col > row) & (key_pos >= 0)
+        allowed = allowed & ((key_pos < pos_ref[1]) == (query_pos < pos_ref[1]))
         dk_acc = jnp.zeros((span, HD), jnp.float32)
         dv_acc = jnp.zeros((span, HD), jnp.float32)
         for g in range(2):
-            q = q_ref[pl.ds(r0, block), pl.ds(g * HD, HD)]
+            raw = q_ref[pl.ds(r0, block), pl.ds(g * HD, HD)].astype(jnp.float32)
+            mean_sq = jnp.mean(raw * raw, axis=1, keepdims=True)
+            q = (raw * lax.rsqrt(mean_sq + epsilon) * gain_ref[...] * query_scale).astype(jnp.bfloat16)
             do = do_ref[pl.ds(r0, block), pl.ds(g * HD, HD)]
             scores = lax.dot_general(q, k, nt, preferred_element_type=jnp.float32)
             exp_scores = jnp.where(allowed, jnp.exp(scores), 0.0)
@@ -226,8 +230,8 @@
         dkv_ref[1, pl.ds(r0, span), :] += dv_acc
 
 
-def attend(queries, grad_out, keys, values, query_seg, key_seg):
-    rows = queries.shape[0]
+def attend(positions, gain, q_raw, grad_out, keys, values):
+    rows = q_raw.shape[0]
     spec = pl.BlockSpec(memory_space=pltpu.VMEM)
     return pl.pallas_call(
         attention_kernel,
@@ -236,13 +240,13 @@
             jax.ShapeDtypeStruct((rows, 2 * HD), jnp.float32),
             jax.ShapeDtypeStruct((2, keys.shape[0], HD), jnp.float32),
         ),
-        in_specs=[spec] * 6,
+        in_specs=[pl.BlockSpec(memory_space=pltpu.SMEM)] + [spec] * 5,
         out_specs=(spec, spec, spec),
         cost_estimate=pl.CostEstimate(
             flops=12 * rows * (rows + WINDOW) * HD * 2, transcendentals=2 * rows * (rows + WINDOW),
             bytes_accessed=16 * rows * HD * 4,
         ),
-    )(queries, grad_out, keys, values, query_seg, key_seg)
+    )(positions, gain, q_raw, grad_out, keys, values)
 
 
 def body(normed, q_raw, key_weight, value_weight, q_gain, k_gain, segment_ids, grad_out):
@@ -273,16 +277,15 @@
     stacked = jnp.stack([keys_bf, values_bf])
     behind = from_behind(stacked, SEQ, 1)
     extended = jnp.concatenate([behind, stacked], axis=1).reshape(2, WINDOW + rows_here, HD)
-    seg_pad = jnp.concatenate([jnp.full((WINDOW,), -1, jnp.int32), segment_ids])
-    query_seg = lax.dynamic_slice_in_dim(segment_ids, base_row, rows_here, 0)
-    key_seg = lax.dynamic_slice_in_dim(seg_pad, base_row, WINDOW + rows_here, 0)
+    boundary = jnp.sum((segment_ids == 0).astype(jnp.int32))
+    positions = jnp.stack([base_row.astype(jnp.int32), boundary])
     attention, dquery, grad_acc = attend(
-        queries.reshape(rows_here, 2 * HD),
+        positions,
+        q_gain.reshape(1, HD),
+        q_raw,
         grad_out,
         extended[0],
         extended[1],
-        query_seg.reshape(rows_here, 1),
-        key_seg.reshape(1, WINDOW + rows_here),
     )
     dquery = dquery.reshape(rows_here, heads_here, 2, HD)
     grad_acc = grad_acc.reshape(2, WINDOW + rows_here, heads_here, HD)

time: 281 us -> 267 us (0.950)
  blocking collectives: 0 us -> 55.2 us
  waiting for transfers between devices: 124 us -> 71.9 us
  starting transfers between devices: 31.8 us -> 24.8 us
  local copies, waits for them, and re-layouts: 32.8 us -> 26.7 us
  other arithmetic: 23.9 us -> 18.9 us
    all_to_all x4 -> x3, waiting for transfers between devices: 114 us -> 57.7 us  [exchange(): return lax.all_to_all(blocks, axis, 0, 0)]
    all_to_all x0 -> x1, blocking collectives: none -> 55.2 us  [exchange(): return lax.all_to_all(blocks, axis, 0, 0)]
    all_to_all x4 -> x3, starting transfers between devices: 26.1 us -> 20.6 us  [exchange(): return lax.all_to_all(blocks, axis, 0, 0)]
    ppermute x2, waiting for transfers between devices: 6.92 us -> 12.2 us  [from_behind(): return lax.ppermute(array, axis, pairs)]
    unnamed x20 -> x12, local copies, waits for them, and re-layouts: 4.74 us -> 0.39 us
    reduce_sum x2, other arithmetic: 1.36 us -> 5.04 us  [normalize(): mean_sq = jnp.mean(raw_vals * raw_vals, axis=-1, keepdims=True)]
  transfers between devices with their start and end apart: 7 -> 6, of which waited for: 7 -> 6; matrix products, arithmetic and copies ran while one was open for 9% -> 11% of each run, Pallas kernels for 0% -> 0%
where the time goes in v12:
time: 267 us; the launch traced here: 266 us
  waiting for transfers between devices  71.9 us (27%)
  blocking collectives  55.2 us (21%)
  Pallas kernels  48.6 us (18%)
  local copies, waits for them, and re-layouts  26.7 us (10%)
  starting transfers between devices  24.8 us (9%)
  matrix products  19.3 us (7%)
  other arithmetic  18.9 us (7%)
    all_to_all x3, waiting for transfers between devices, exchange(): return lax.all_to_all(blocks, axis, 0, 0)  57.7 us
    all_to_all x1, blocking collectives, exchange(): return lax.all_to_all(blocks, axis, 0, 0)  55.2 us
    pallas_call x1, Pallas kernels, gather_seq(): pl.pallas_call(functools.partial(gather_kernel, levels, rows), out_shape=...  32 us
    all_to_all x3, starting transfers between devices, exchange(): return lax.all_to_all(blocks, axis, 0, 0)  20.6 us
    pallas_call x1, Pallas kernels, attend(): pl.pallas_call(attention_kernel, out_shape=(jax.ShapeDtypeStruct((rows, 2...  16.6 us
    ppermute x2, waiting for transfers between devices, from_behind(): return lax.ppermute(array, axis, pairs)  12.2 us
    dot_general x1, matrix products, body(): jnp.einsum('htkc,khcf->tf', grads_all, weight_heads, preferred_element_ty...  7.3 us
    dot_general x1, matrix products, body(): jnp.einsum('htkc,tf->khcf', grads_all, normed, preferred_element_type=jnp...  6.48 us
  transfers between devices with their start and end apart: 6, of which 6 were waited for; matrix products, arithmetic and copies ran while one was open for 11% of the time, Pallas kernels for 0%

profile of v12, /device:TPU:2, one launch (start us, length us, event | category | flops | bytes accessed | tf_op | source)
XLA Modules:
  0.0 266.3 jit_solution(4730633228521078419)
XLA Ops:
  0.6 1.6 maximum_bitcast_fusion.x_ref
  2.2 32.0 %shard_map.124 = bf16[2,32,32,672]{3,2,1,0:T(8,128)(2,1)} custom-call(bf16[2,1,32,672]{3,2,1,0:T(8,128)(2,1)} %maximum_bitcast_fusion.x_ref), custom_call_target="tpu_custom_call" | custom-call | tf_op jit(solution)/shard_map/pallas_call | solution.py:132
  34.3 5.5 %convolution_convert_fusion = bf16[2,1024,1024]{2,1,0:T(8,128)(2,1)S(1)} fusion(bf16[2,1024,672]{2,1,0:T(8,128)(2,1)} %bitcast.103, bf16[1024,672]{0,1:T(8,128)(2,1)S(1)} %copy-done), kind=kOutput, calls=%fused_computation.7 | convolution fusion | flops 2820669440 | bytes 8323072 | tf_op jit(solution)/shard_map/dot_general | solution.py:263
  39.8 0.6 copy.89
  40.4 55.2 %all_to_all.20 = bf16[8,1024,2,128]{1,3,2,0:T(8,128)(2,1)S(1)} all-to-all(bf16[8,1024,2,128]{1,3,2,0:T(8,128)(2,1)S(1)} %bitcast.95), channel_id=1, replica_groups=mesh['level'=4,'row'=4,'core'=2,'uly'=8] {'uly'}, dimensions={0} | all-to-all | bytes 8388608 | tf_op jit(solution)/shard_map/all_to_all | solution.py:30
  95.6 0.8 convert_reduce_fusion
  96.5 0.2 copy.77
  96.9 0.2 multiply_reduce_fusion.3
  97.2 0.2 fusion.10
  97.4 2.1 collective-permute-start
  99.6 1.6 convert_reduce_fusion.2
  101.1 1.2 pad_add_fusion.pos_ref
  102.4 5.6 %collective-permute-done = bf16[2,1024,1,128]{3,1,2,0:T(8,128)(2,1)S(1)} collective-permute-done((bf16[2,1024,1,128]{3,1,2,0:T(8,128)(2,1)S(1)}, bf16[2,1024,1,128]{3,1,2,0:T(8,128)(2,1)S(1)}, u32[]{:S(2)}, u32[]{:S(2)}) %collective-permute-start) | collective-permute-done | bytes 524320 | tf_op jit(solution)/shard_map/ppermute | solution.py:21
  108.0 1.0 slice_bitcast_fusion.1
  109.0 16.6 %shard_map.125 = (bf16[1024,256]{1,0:T(8,128)(2,1)}, f32[1024,256]{1,0:T(8,128)}, f32[2,2048,128]{2,1,0:T(8,128)}) custom-call(s32[2]{0:T(128)} %pad_add_fusion.pos_ref, f32[1,128]{1,0:T(1,128)} %bitcast.111, bf16[1024,256]{1,0:T(8,128)(2,1)} %q_ref.1, bf16[1024,256]{1,0:T(8,128)(2,1)} %do_ref.1, bf16[2048,128]{1,0:T(8,128)(2,1)} %get-tuple-element.46.k_ref, ...), custom_call_target="tpu_custom_call" | custom-call | flops 6442450944 | bytes 8388608 | tf_op jit(solution)/shard_map/pallas_call | solution.py:236
  125.6 1.3 slice.108
  126.9 1.9 collective-permute-start.1
  128.9 6.7 %collective-permute-done.1 = bf16[2,1024,1,128]{3,1,2,0:T(8,128)(2,1)S(1)} collective-permute-done((bf16[2,1024,1,128]{3,1,2,0:T(8,128)(2,1)S(1)}, bf16[2,1024,1,128]{3,1,2,0:T(8,128)(2,1)S(1)}, u32[]{:S(2)}, u32[]{:S(2)}) %collective-permute-start.1) | collective-permute-done | bytes 524320 | tf_op jit(solution)/shard_map/ppermute | solution.py:21
  135.5 1.3 slice_add_fusion
  136.9 0.2 multiply_reduce_fusion.2
  137.1 0.3 fusion.8
  137.5 2.8 %broadcast_in_dim.36 = bf16[8,1024,2,128]{3,1,2,0:T(8,128)(2,1)} broadcast(bf16[1024,2,128]{2,0,1:T(8,128)(2,1)S(1)} %pad_maximum_fusion.1), dimensions={1,2,3} | broadcast | bytes 4718592 | tf_op jit(solution)/shard_map/broadcast_in_dim | solution.py:35
  140.3 4.5 %all-to-all-start.1 = ((bf16[8,1024,2,128]{3,1,2,0:T(8,128)(2,1)}), bf16[8,1024,2,128]{3,1,2,0:T(8,128)(2,1)}, u32[]{:S(2)}, u32[]{:S(2)}) async-start(bf16[8,1024,2,128]{3,1,2,0:T(8,128)(2,1)} %broadcast_in_dim.36), calls=%async_computation.1 | async-start | bytes 8388608 | tf_op jit(solution)/shard_map/all_to_all | solution.py:30
  144.9 50.5 %all-to-all-done.1 = bf16[8,1024,2,128]{3,1,2,0:T(8,128)(2,1)} async-done(((bf16[8,1024,2,128]{3,1,2,0:T(8,128)(2,1)}), bf16[8,1024,2,128]{3,1,2,0:T(8,128)(2,1)}, u32[]{:S(2)}, u32[]{:S(2)}) %all-to-all-start.1) | async-done | bytes 4194336 | tf_op jit(solution)/shard_map/all_to_all | solution.py:30
  195.4 6.5 %convert_bitcast_fusion = bf16[2,8,128,672]{2,3,0,1:T(8,128)(2,1)} fusion(bf16[8,1024,2,128]{3,1,2,0:T(8,128)(2,1)} %all-to-all-done.1, bf16[1024,672]{0,1:T(8,128)(2,1)S(1)} %copy-done), kind=kOutput, calls=%fused_computation.6 | convolution fusion | flops 2819948544 | bytes 8323072 | tf_op jit(solution)/shard_map/htkc,tf->khcf/dot_general | solution.py:310
  201.9 4.6 %copy.64 = bf16[2,8,128,672]{3,2,1,0:T(8,128)(2,1)} copy(bf16[2,8,128,672]{2,3,0,1:T(8,128)(2,1)} %convert_bitcast_fusion) | data formatting | bytes 5505024 | tf_op jit(solution)/shard_map/convert_element_type | solution.py:312
  206.5 2.8 %select_bitcast_fusion = bf16[2,16,32,672]{3,2,1,0:T(8,128)(2,1)} fusion(bf16[2,16,2,32,672]{4,3,2,1,0:T(8,128)(2,1)} %bitcast.96, s32[]{:T(128)S(6)} %select_n.15, pred[]{:T(512)S(6)} %and.16), kind=kLoop, calls=%fused_computation.11 | loop fusion | flops 688128 | bytes 2752517 | tf_op jit(solution)/shard_map/jit(_take)/select_n | solution.py:155
  209.4 1.5 reshape.275
  210.9 2.0 collective-permute-done.2
  212.9 2.0 add_convert_fusion
  214.9 1.3 copy.90
  216.2 4.9 %all-to-all-start.2 = ((bf16[4,4,2,32,672]{4,3,1,2,0:T(8,128)(2,1)}), bf16[4,4,2,32,672]{4,3,1,2,0:T(8,128)(2,1)S(1)}, u32[]{:S(2)}, u32[]{:S(2)}) async-start(bf16[4,4,2,32,672]{4,3,1,2,0:T(8,128)(2,1)} %bitcast.98), calls=%async_computation.2 | async-start | bytes 3145728 | tf_op jit(solution)/shard_map/all_to_all | solution.py:30
  221.0 2.7 %reshape.276 = f32[1024,1,2,128]{3,2,0,1:T(2,128)} reshape(f32[1024,256]{1,0:T(8,128)} %get-tuple-element.31) | data formatting | bytes 2097152 | tf_op jit(solution)/shard_map/reshape | solution.py:290
  223.8 4.8 %multiply_reduce_fusion.1 = (f32[1024,2]{1,0:T(8,128)}, f32[1024,2]{1,0:T(8,128)}) fusion(f32[1024,1,2,128]{3,2,0,1:T(2,128)} %reshape.275, f32[1024,1,2,128]{3,2,0,1:T(2,128)} %reshape.276, f32[128]{0:T(128)S(1)} %broadcast_multiply_fusion), kind=kLoop, calls=%fused_computation.22 | loop fusion | flops 1306624 | bytes 2114048 | tf_op jit(solution)/shard_map/jvp()/reduce_sum | solution.py:25
  228.6 1.2 copy.60
  229.8 1.2 copy.62
  231.1 1.0 copy.61
  232.2 1.0 copy.63
  233.2 2.3 mul.198
  235.5 2.2 broadcast_in_dim.37
  237.7 1.1 fusion.7
  238.8 2.0 all-to-all-done.2
  240.8 0.3 reduce_sum.93
  241.2 0.8 copy.68
  241.9 11.2 %all-to-all-start.3 = ((bf16[4,2,32,672]{3,2,1,0:T(8,128)(2,1)}), bf16[4,2,32,672]{3,2,1,0:T(8,128)(2,1)S(1)}, u32[]{:S(2)}, u32[]{:S(2)}) async-start(bf16[4,2,32,672]{3,2,1,0:T(8,128)(2,1)} %copy.68), calls=%async_computation.3 | async-start | bytes 786432 | tf_op jit(solution)/shard_map/all_to_all | solution.py:30
  253.2 7.3 %bitcast_convert_fusion = bf16[1024,672]{0,1:T(8,128)(2,1)} fusion(bf16[8,1024,2,128]{3,1,2,0:T(8,128)(2,1)} %all-to-all-done.1, bf16[2,8,128,672]{3,2,1,0:T(8,128)(2,1)} %bitcast.104), kind=kOutput, calls=%fused_computation.5 | convolution fusion | flops 2819260416 | bytes 8323072 | tf_op jit(solution)/shard_map/htkc,khcf->tf/dot_general | solution.py:307
  260.5 5.1 %all-to-all-done.3 = bf16[4,2,32,672]{3,2,1,0:T(8,128)(2,1)S(1)} async-done(((bf16[4,2,32,672]{3,2,1,0:T(8,128)(2,1)}), bf16[4,2,32,672]{3,2,1,0:T(8,128)(2,1)S(1)}, u32[]{:S(2)}, u32[]{:S(2)}) %all-to-all-start.3) | async-done | bytes 344096 | tf_op jit(solution)/shard_map/all_to_all | solution.py:30
  265.6 0.7 slice_bitcast_fusion.3
  (24 shorter events, 0.7 us)
Async XLA Ops:
  0.6 33.6 %copy-start = (bf16[1024,672]{0,1:T(8,128)(2,1)S(1)}, bf16[1024,672]{0,1:T(8,128)(2,1)}, u32[]{:S(2)}) copy-start(bf16[1024,672]{0,1:T(8,128)(2,1)} %param.14) | copy-start | bytes 4128772
  96.5 0.7 copy-start.3
  97.4 10.5 %collective-permute-start = (bf16[2,1024,1,128]{3,1,2,0:T(8,128)(2,1)S(1)}, bf16[2,1024,1,128]{3,1,2,0:T(8,128)(2,1)S(1)}, u32[]{:S(2)}, u32[]{:S(2)}) collective-permute-start(bf16[2,1024,1,128]{3,1,2,0:T(8,128)(2,1)S(1)} %pad_maximum_fusion), channel_id=1, source_target_pairs={{0,8},{8,16},{16,24},{24,32},{32,40},{40,48},{48,56},{56,64},{64,7... | collective-permute-start | bytes 1572872 | tf_op jit(solution)/shard_map/ppermute | solution.py:21
  126.9 8.6 %collective-permute-start.1 = (bf16[2,1024,1,128]{3,1,2,0:T(8,128)(2,1)S(1)}, bf16[2,1024,1,128]{3,1,2,0:T(8,128)(2,1)S(1)}, u32[]{:S(2)}, u32[]{:S(2)}) collective-permute-start(bf16[2,1024,1,128]{3,1,2,0:T(8,128)(2,1)S(1)} %slice.108), channel_id=1, source_target_pairs={{8,0},{16,8},{24,16},{32,24},{40,32},{48,40},{56,48},{64,56},{72,6... | collective-permute-start | bytes 1572872 | tf_op jit(solution)/shard_map/ppermute | solution.py:21
  140.3 55.1 %all-to-all-start.1 = ((bf16[8,1024,2,128]{3,1,2,0:T(8,128)(2,1)}), bf16[8,1024,2,128]{3,1,2,0:T(8,128)(2,1)}, u32[]{:S(2)}, u32[]{:S(2)}) async-start(bf16[8,1024,2,128]{3,1,2,0:T(8,128)(2,1)} %broadcast_in_dim.36), calls=%async_computation.1 | async-start | bytes 8388608 | tf_op jit(solution)/shard_map/all_to_all | solution.py:30
  206.5 3.0 %copy-start.2 = (bf16[1024,256]{1,0:T(8,128)(2,1)S(1)}, bf16[1024,256]{1,0:T(8,128)(2,1)}, u32[]{:S(2)}) copy-start(bf16[1024,256]{1,0:T(8,128)(2,1)} %q_ref.1) | copy-start | bytes 1572868
  206.5 4.5 %copy-start.4 = (f32[128]{0:T(128)S(1)}, f32[128]{0:T(128)}, u32[]{:S(2)}) copy-start(f32[128]{0:T(128)} %param.18) | copy-start | bytes 1540
  209.3 3.6 %collective-permute-start.2 = (bf16[2,16,32,672]{3,2,1,0:T(8,128)(2,1)}, bf16[2,16,32,672]{3,2,1,0:T(8,128)(2,1)S(1)}, u32[]{:S(2)}, u32[]{:S(2)}) collective-permute-start(bf16[2,16,32,672]{3,2,1,0:T(8,128)(2,1)} %select_bitcast_fusion), channel_id=1, source_target_pairs={{0,8},{8,0},{1,9},{9,1},{2,10},{10,2},{3,11},{11,3},{4,12},{12,4},... | collective-permute-start | bytes 4128776 | tf_op jit(solution)/shard_map/ppermute | solution.py:156
  216.2 24.7 %all-to-all-start.2 = ((bf16[4,4,2,32,672]{4,3,1,2,0:T(8,128)(2,1)}), bf16[4,4,2,32,672]{4,3,1,2,0:T(8,128)(2,1)S(1)}, u32[]{:S(2)}, u32[]{:S(2)}) async-start(bf16[4,4,2,32,672]{4,3,1,2,0:T(8,128)(2,1)} %bitcast.98), calls=%async_computation.2 | async-start | bytes 3145728 | tf_op jit(solution)/shard_map/all_to_all | solution.py:30
  233.2 4.5 %copy-start.1 = (f32[1024,256]{1,0:T(8,128)S(1)}, f32[1024,256]{1,0:T(8,128)}, u32[]{:S(2)}) copy-start(f32[1024,256]{1,0:T(8,128)} %get-tuple-element.31) | copy-start | bytes 3145732
  241.9 23.6 %all-to-all-start.3 = ((bf16[4,2,32,672]{3,2,1,0:T(8,128)(2,1)}), bf16[4,2,32,672]{3,2,1,0:T(8,128)(2,1)S(1)}, u32[]{:S(2)}, u32[]{:S(2)}) async-start(bf16[4,2,32,672]{3,2,1,0:T(8,128)(2,1)} %copy.68), calls=%async_computation.3 | async-start | bytes 786432 | tf_op jit(solution)/shard_map/all_to_all | solution.py:30

commit v13 on v12

--- a/solution.py
+++ b/solution.py
@@ -147,14 +147,13 @@
     )(block[:, None])
 
 
-def reduce_seq(blocks):
-    chips = blocks.shape[1] // 2
-    split = blocks.reshape((blocks.shape[0], chips, 2) + blocks.shape[2:])
+def reduce_seq(halves):
     core = lax.axis_index("core")
-    keep = jnp.take(split, core, axis=2)
-    send = jnp.take(split, 1 - core, axis=2)
+    keep = lax.dynamic_index_in_dim(halves, core, 0, keepdims=False)
+    send = lax.dynamic_index_in_dim(halves, 1 - core, 0, keepdims=False)
     pair = (keep.astype(jnp.float32) + lax.ppermute(send, "core", SWAP).astype(jnp.float32))
     pair = pair.astype(jnp.bfloat16).transpose(1, 0, 2, 3)
+    chips = pair.shape[0]
     levels = lax.axis_size("level")
     by_row = pair.reshape((levels, chips // levels) + pair.shape[1:]).transpose(1, 0, 2, 3, 4)
     part = jnp.sum(exchange(by_row, "row").astype(jnp.float32), axis=0)
@@ -307,10 +306,12 @@
     grad_normed = jnp.einsum(
         "htkc,khcf->tf", grads_all, weight_heads, preferred_element_type=jnp.float32
     ).astype(jnp.bfloat16)
-    weight_part = jnp.einsum(
-        "htkc,tf->khcf", grads_all, normed, preferred_element_type=jnp.float32
+    per_head = HD // col_block
+    g6 = grads_all.reshape(n_uly, rows_here, 2, per_head // 2, 2, col_block)
+    halves = jnp.einsum(
+        "htkaoc,tf->okhacf", g6, normed, preferred_element_type=jnp.float32
     ).astype(jnp.bfloat16)
-    summed = reduce_seq(weight_part.reshape(2, n_seq, col_block, feats))
+    summed = reduce_seq(halves.reshape(2, 2, n_seq // 2, col_block, feats))
     grad_key_weight = summed[0].T
     grad_value_weight = summed[1].T
     return (attention, grad_normed, grad_q, grad_key_weight, grad_value_weight)

time: 267 us -> 269 us (level)
  local copies, waits for them, and re-layouts: 26.7 us -> 30.5 us
  other arithmetic: 18.9 us -> 16.1 us
    all_to_all x0 -> x1, local copies, waits for them, and re-layouts: none -> 6.46 us  [exchange(): return lax.all_to_all(blocks, axis, 0, 0)]
    convert_element_type x1, local copies, waits for them, and re-layouts: 4.58 us -> 0.28 us  [body(): halves = jnp.einsum('htkaoc,tf->okhacf', g6, normed, preferred_element_ty...]
    select_n x1 -> x0, other arithmetic: 2.81 us -> none  [reduce_seq(): send = jnp.take(split, 1 - core, axis=2)]
  transfers between devices with their start and end apart: 6 -> 6, of which waited for: 6 -> 6; matrix products, arithmetic and copies ran while one was open for 11% -> 10% of each run, Pallas kernels for 0% -> 0%
where the time goes in v13:
time: 269 us; the launch traced here: 268 us
  waiting for transfers between devices  73.1 us (27%)
  blocking collectives  55.2 us (21%)
  Pallas kernels  48.6 us (18%)
  local copies, waits for them, and re-layouts  30.5 us (11%)
  starting transfers between devices  24.8 us (9%)
  matrix products  18.6 us (7%)
  other arithmetic  16.1 us (6%)
    all_to_all x3, waiting for transfers between devices, exchange(): return lax.all_to_all(blocks, axis, 0, 0)  58.9 us
    all_to_all x1, blocking collectives, exchange(): return lax.all_to_all(blocks, axis, 0, 0)  55.2 us
    pallas_call x1, Pallas kernels, gather_seq(): pl.pallas_call(functools.partial(gather_kernel, levels, rows), out_shape=...  32 us
    all_to_all x3, starting transfers between devices, exchange(): return lax.all_to_all(blocks, axis, 0, 0)  20.6 us
    pallas_call x1, Pallas kernels, attend(): pl.pallas_call(attention_kernel, out_shape=(jax.ShapeDtypeStruct((rows, 2...  16.6 us
    ppermute x2, waiting for transfers between devices, from_behind(): return lax.ppermute(array, axis, pairs)  12.2 us
    dot_general x1, matrix products, body(): jnp.einsum('htkc,khcf->tf', grads_all, weight_heads, preferred_element_ty...  7.39 us
    all_to_all x1, local copies, waits for them, and re-layouts, exchange(): return lax.all_to_all(blocks, axis, 0, 0)  6.46 us
  transfers between devices with their start and end apart: 6, of which 6 were waited for; matrix products, arithmetic and copies ran while one was open for 10% of the time, Pallas kernels for 0%

profile of v13, /device:TPU:2, one launch (start us, length us, event | category | flops | bytes accessed | tf_op | source)
XLA Modules:
  0.0 267.8 jit_solution(13757476343795993297)
XLA Ops:
  0.6 1.6 maximum_bitcast_fusion.x_ref
  2.2 32.0 %shard_map.124 = bf16[2,32,32,672]{3,2,1,0:T(8,128)(2,1)} custom-call(bf16[2,1,32,672]{3,2,1,0:T(8,128)(2,1)} %maximum_bitcast_fusion.x_ref), custom_call_target="tpu_custom_call" | custom-call | tf_op jit(solution)/shard_map/pallas_call | solution.py:132
  34.3 5.5 %convolution_convert_fusion = bf16[2,1024,1024]{2,1,0:T(8,128)(2,1)S(1)} fusion(bf16[2,1024,672]{2,1,0:T(8,128)(2,1)} %bitcast.98, bf16[1024,672]{0,1:T(8,128)(2,1)S(1)} %copy-done), kind=kOutput, calls=%fused_computation.8 | convolution fusion | flops 2820669440 | bytes 8323072 | tf_op jit(solution)/shard_map/dot_general | solution.py:262
  39.8 0.6 copy.88
  40.4 55.2 %all_to_all.20 = bf16[8,1024,2,128]{1,3,2,0:T(8,128)(2,1)S(1)} all-to-all(bf16[8,1024,2,128]{1,3,2,0:T(8,128)(2,1)S(1)} %bitcast.89), channel_id=1, replica_groups=mesh['level'=4,'row'=4,'core'=2,'uly'=8] {'uly'}, dimensions={0} | all-to-all | bytes 8388608 | tf_op jit(solution)/shard_map/all_to_all | solution.py:30
  95.6 0.8 convert_reduce_fusion
  96.9 0.2 multiply_reduce_fusion.3
  97.4 2.1 collective-permute-start
  99.6 1.6 convert_reduce_fusion.2
  101.1 1.2 pad_add_fusion.pos_ref
  102.4 5.6 %collective-permute-done = bf16[2,1024,1,128]{3,1,2,0:T(8,128)(2,1)S(1)} collective-permute-done((bf16[2,1024,1,128]{3,1,2,0:T(8,128)(2,1)S(1)}, bf16[2,1024,1,128]{3,1,2,0:T(8,128)(2,1)S(1)}, u32[]{:S(2)}, u32[]{:S(2)}) %collective-permute-start) | collective-permute-done | bytes 524320 | tf_op jit(solution)/shard_map/ppermute | solution.py:21
  108.0 1.0 slice_bitcast_fusion.1
  109.0 16.6 %shard_map.125 = (bf16[1024,256]{1,0:T(8,128)(2,1)}, f32[1024,256]{1,0:T(8,128)}, f32[2,2048,128]{2,1,0:T(8,128)}) custom-call(s32[2]{0:T(128)} %pad_add_fusion.pos_ref, f32[1,128]{1,0:T(1,128)} %bitcast.106, bf16[1024,256]{1,0:T(8,128)(2,1)} %q_ref.1, bf16[1024,256]{1,0:T(8,128)(2,1)} %do_ref.1, bf16[2048,128]{1,0:T(8,128)(2,1)} %get-tuple-element.34.k_ref, ...), custom_call_target="tpu_custom_call" | custom-call | flops 6442450944 | bytes 8388608 | tf_op jit(solution)/shard_map/pallas_call | solution.py:235
  125.6 1.3 slice.95
  126.9 1.9 collective-permute-start.1
  128.9 6.7 %collective-permute-done.1 = bf16[2,1024,1,128]{3,1,2,0:T(8,128)(2,1)S(1)} collective-permute-done((bf16[2,1024,1,128]{3,1,2,0:T(8,128)(2,1)S(1)}, bf16[2,1024,1,128]{3,1,2,0:T(8,128)(2,1)S(1)}, u32[]{:S(2)}, u32[]{:S(2)}) %collective-permute-start.1) | collective-permute-done | bytes 524320 | tf_op jit(solution)/shard_map/ppermute | solution.py:21
  135.5 1.3 slice_add_fusion
  136.9 0.2 multiply_reduce_fusion.2
  137.1 0.3 fusion.8
  137.5 2.8 %broadcast_in_dim.12 = bf16[8,1024,2,128]{3,1,2,0:T(8,128)(2,1)} broadcast(bf16[1024,2,128]{2,0,1:T(8,128)(2,1)S(1)} %pad_maximum_fusion.1), dimensions={1,2,3} | broadcast | bytes 4718592 | tf_op jit(solution)/shard_map/broadcast_in_dim | solution.py:35
  140.3 4.5 %all-to-all-start.1 = ((bf16[8,1024,2,128]{3,1,2,0:T(8,128)(2,1)}), bf16[8,1024,2,128]{3,1,2,0:T(8,128)(2,1)}, u32[]{:S(2)}, u32[]{:S(2)}) async-start(bf16[8,1024,2,128]{3,1,2,0:T(8,128)(2,1)} %broadcast_in_dim.12), calls=%async_computation.1 | async-start | bytes 8388608 | tf_op jit(solution)/shard_map/all_to_all | solution.py:30
  144.9 50.5 %all-to-all-done.1 = bf16[8,1024,2,128]{3,1,2,0:T(8,128)(2,1)} async-done(((bf16[8,1024,2,128]{3,1,2,0:T(8,128)(2,1)}), bf16[8,1024,2,128]{3,1,2,0:T(8,128)(2,1)}, u32[]{:S(2)}, u32[]{:S(2)}) %all-to-all-start.1) | async-done | bytes 4194336 | tf_op jit(solution)/shard_map/all_to_all | solution.py:30
  195.4 6.5 %copy.64 = bf16[8,1024,2,128]{1,3,2,0:T(8,128)(2,1)} copy(bf16[8,1024,2,128]{3,1,2,0:T(8,128)(2,1)} %all-to-all-done.1) | data formatting | bytes 8388608 | tf_op jit(solution)/shard_map/all_to_all | solution.py:30
  201.9 5.7 %convert_bitcast_fusion = bf16[2,2,8,2,32,672]{5,4,0,3,1,2:T(8,128)(2,1)S(1)} fusion(bf16[8,1024,2,2,2,32]{1,5,4,3,2,0:T(8,128)(2,1)} %bitcast.97, bf16[1024,672]{0,1:T(8,128)(2,1)S(1)} %copy-done), kind=kOutput, calls=%fused_computation.6 | convolution fusion | flops 2819948544 | bytes 8323072 | tf_op jit(solution)/shard_map/htkaoc,tf->okhacf/dot_general | solution.py:311
  207.6 0.3 copy.65
  207.9 1.6 copy-done.2
  209.5 1.3 dynamic-slice_bitcast_fusion
  211.0 1.5 reshape.282
  212.5 2.0 collective-permute-done.2
  214.4 1.9 fusion
  216.4 1.3 copy.89
  217.7 4.9 %all-to-all-start.2 = ((bf16[4,4,2,32,672]{4,3,1,2,0:T(8,128)(2,1)}), bf16[4,4,2,32,672]{4,3,1,2,0:T(8,128)(2,1)S(1)}, u32[]{:S(2)}, u32[]{:S(2)}) async-start(bf16[4,4,2,32,672]{4,3,1,2,0:T(8,128)(2,1)} %bitcast.92), calls=%async_computation.2 | async-start | bytes 3145728 | tf_op jit(solution)/shard_map/all_to_all | solution.py:30
  222.5 1.5 reshape.283
  224.0 4.8 %multiply_reduce_fusion.1 = (f32[1024,2]{1,0:T(8,128)}, f32[1024,2]{1,0:T(8,128)}) fusion(f32[1024,1,2,128]{3,2,0,1:T(2,128)} %reshape.282, f32[1024,1,2,128]{3,2,0,1:T(2,128)} %reshape.283, f32[128]{0:T(128)S(1)} %broadcast_multiply_fusion), kind=kLoop, calls=%fused_computation.21 | loop fusion | flops 1306624 | bytes 2114048 | tf_op jit(solution)/shard_map/jvp()/reduce_sum | solution.py:25
  228.9 1.2 copy.60
  230.1 1.2 copy.62
  231.3 1.0 copy.61
  232.4 1.0 copy.63
  233.4 2.2 mul.198
  235.6 2.2 broadcast_in_dim.13
  237.8 1.2 fusion.7
  239.0 3.4 %all-to-all-done.2 = bf16[4,4,2,32,672]{4,3,1,2,0:T(8,128)(2,1)S(1)} async-done(((bf16[4,4,2,32,672]{4,3,1,2,0:T(8,128)(2,1)}), bf16[4,4,2,32,672]{4,3,1,2,0:T(8,128)(2,1)S(1)}, u32[]{:S(2)}, u32[]{:S(2)}) %all-to-all-start.2) | async-done | bytes 1376288 | tf_op jit(solution)/shard_map/all_to_all | solution.py:30
  242.3 0.3 reduce_sum.93
  242.6 0.8 copy.68
  243.4 11.2 %all-to-all-start.3 = ((bf16[4,2,32,672]{3,2,1,0:T(8,128)(2,1)}), bf16[4,2,32,672]{3,2,1,0:T(8,128)(2,1)S(1)}, u32[]{:S(2)}, u32[]{:S(2)}) async-start(bf16[4,2,32,672]{3,2,1,0:T(8,128)(2,1)} %copy.68), calls=%async_computation.3 | async-start | bytes 786432 | tf_op jit(solution)/shard_map/all_to_all | solution.py:30
  254.7 7.4 %bitcast_convert_fusion = bf16[1024,672]{0,1:T(8,128)(2,1)} fusion(bf16[8,1024,2,128]{3,1,2,0:T(8,128)(2,1)} %all-to-all-done.1, bf16[2,8,128,672]{3,2,1,0:T(8,128)(2,1)} %bitcast.99), kind=kOutput, calls=%fused_computation.7 | convolution fusion | flops 2819260416 | bytes 8323072 | tf_op jit(solution)/shard_map/htkc,khcf->tf/dot_general | solution.py:306
  262.0 5.0 %all-to-all-done.3 = bf16[4,2,32,672]{3,2,1,0:T(8,128)(2,1)S(1)} async-done(((bf16[4,2,32,672]{3,2,1,0:T(8,128)(2,1)}), bf16[4,2,32,672]{3,2,1,0:T(8,128)(2,1)S(1)}, u32[]{:S(2)}, u32[]{:S(2)}) %all-to-all-start.3) | async-done | bytes 344096 | tf_op jit(solution)/shard_map/all_to_all | solution.py:30
  267.1 0.7 slice_bitcast_fusion.3
  (29 shorter events, 1.1 us)
Async XLA Ops:
  0.6 33.6 %copy-start = (bf16[1024,672]{0,1:T(8,128)(2,1)S(1)}, bf16[1024,672]{0,1:T(8,128)(2,1)}, u32[]{:S(2)}) copy-start(bf16[1024,672]{0,1:T(8,128)(2,1)} %param.12) | copy-start | bytes 4128772
  96.5 0.7 copy-start.5
  97.4 10.5 %collective-permute-start = (bf16[2,1024,1,128]{3,1,2,0:T(8,128)(2,1)S(1)}, bf16[2,1024,1,128]{3,1,2,0:T(8,128)(2,1)S(1)}, u32[]{:S(2)}, u32[]{:S(2)}) collective-permute-start(bf16[2,1024,1,128]{3,1,2,0:T(8,128)(2,1)S(1)} %pad_maximum_fusion), channel_id=1, source_target_pairs={{0,8},{8,16},{16,24},{24,32},{32,40},{40,48},{48,56},{56,64},{64,7... | collective-permute-start | bytes 1572872 | tf_op jit(solution)/shard_map/ppermute | solution.py:21
  126.9 8.6 %collective-permute-start.1 = (bf16[2,1024,1,128]{3,1,2,0:T(8,128)(2,1)S(1)}, bf16[2,1024,1,128]{3,1,2,0:T(8,128)(2,1)S(1)}, u32[]{:S(2)}, u32[]{:S(2)}) collective-permute-start(bf16[2,1024,1,128]{3,1,2,0:T(8,128)(2,1)S(1)} %slice.95), channel_id=1, source_target_pairs={{8,0},{16,8},{24,16},{32,24},{40,32},{48,40},{56,48},{64,56},{72,6... | collective-permute-start | bytes 1572872 | tf_op jit(solution)/shard_map/ppermute | solution.py:21
  140.3 55.1 %all-to-all-start.1 = ((bf16[8,1024,2,128]{3,1,2,0:T(8,128)(2,1)}), bf16[8,1024,2,128]{3,1,2,0:T(8,128)(2,1)}, u32[]{:S(2)}, u32[]{:S(2)}) async-start(bf16[8,1024,2,128]{3,1,2,0:T(8,128)(2,1)} %broadcast_in_dim.12), calls=%async_computation.1 | async-start | bytes 8388608 | tf_op jit(solution)/shard_map/all_to_all | solution.py:30
  207.8 1.7 copy-start.2
  207.9 3.1 %copy-start.4 = (bf16[1024,256]{1,0:T(8,128)(2,1)S(1)}, bf16[1024,256]{1,0:T(8,128)(2,1)}, u32[]{:S(2)}) copy-start(bf16[1024,256]{1,0:T(8,128)(2,1)} %q_ref.1) | copy-start | bytes 1572868
  207.9 4.6 %copy-start.6 = (f32[128]{0:T(128)S(1)}, f32[128]{0:T(128)}, u32[]{:S(2)}) copy-start(f32[128]{0:T(128)} %param.16) | copy-start | bytes 1540
  210.8 3.6 %collective-permute-start.2 = (bf16[2,16,32,672]{3,2,1,0:T(8,128)(2,1)}, bf16[2,16,32,672]{3,2,1,0:T(8,128)(2,1)S(1)}, u32[]{:S(2)}, u32[]{:S(2)}) collective-permute-start(bf16[2,16,32,672]{3,2,1,0:T(8,128)(2,1)} %dynamic-slice_bitcast_fusion), channel_id=1, source_target_pairs={{0,8},{8,0},{1,9},{9,1},{2,10},{10,2},{3,11},{11,3},{4,12},{12,4},... | collective-permute-start | bytes 4128776 | tf_op jit(solution)/shard_map/ppermute | solution.py:154
  216.4 6.2 %copy-start.3 = (f32[1024,256]{1,0:T(8,128)S(1)}, f32[1024,256]{1,0:T(8,128)}, u32[]{:S(2)}) copy-start(f32[1024,256]{1,0:T(8,128)} %get-tuple-element.30) | copy-start | bytes 3145732
  217.7 24.6 %all-to-all-start.2 = ((bf16[4,4,2,32,672]{4,3,1,2,0:T(8,128)(2,1)}), bf16[4,4,2,32,672]{4,3,1,2,0:T(8,128)(2,1)S(1)}, u32[]{:S(2)}, u32[]{:S(2)}) async-start(bf16[4,4,2,32,672]{4,3,1,2,0:T(8,128)(2,1)} %bitcast.92), calls=%async_computation.2 | async-start | bytes 3145728 | tf_op jit(solution)/shard_map/all_to_all | solution.py:30
  243.4 23.6 %all-to-all-start.3 = ((bf16[4,2,32,672]{3,2,1,0:T(8,128)(2,1)}), bf16[4,2,32,672]{3,2,1,0:T(8,128)(2,1)S(1)}, u32[]{:S(2)}, u32[]{:S(2)}) async-start(bf16[4,2,32,672]{3,2,1,0:T(8,128)(2,1)} %copy.68), calls=%async_computation.3 | async-start | bytes 786432 | tf_op jit(solution)/shard_map/all_to_all | solution.py:30
  254.7 13.2 %copy-start.1 = (bf16[1024,672]{0,1:T(8,128)(2,1)S(1)}, bf16[1024,672]{0,1:T(8,128)(2,1)}, u32[]{:S(2)}) copy-start(bf16[1024,672]{0,1:T(8,128)(2,1)} %param.12) | copy-start | bytes 4128772

commit v14 on v12

--- a/solution.py
+++ b/solution.py
@@ -189,7 +189,7 @@
 
 def attention_kernel(pos_ref, gain_ref, q_ref, do_ref, k_ref, v_ref, out_ref, dq_ref, dkv_ref):
     rows = q_ref.shape[0]
-    block = 256
+    block = 128
     span = block + WINDOW
     dkv_ref[...] = jnp.zeros(dkv_ref.shape, jnp.float32)
     nt = (((1,), (1,)), ((), ()))

time: 267 us -> 270 us (1.011)
  Pallas kernels: 48.6 us -> 51.6 us
    pallas_call x1, Pallas kernels: 16.6 us -> 19.6 us  [attend(): pl.pallas_call(attention_kernel, out_shape=(jax.ShapeDtypeStruct((rows, 2...]
where the time goes in v14:
time: 270 us; the launch traced here: 269 us
  waiting for transfers between devices  71.9 us (27%)
  blocking collectives  55.2 us (20%)
  Pallas kernels  51.6 us (19%)
  local copies, waits for them, and re-layouts  26.7 us (10%)
  starting transfers between devices  24.8 us (9%)
  matrix products  19.3 us (7%)
  other arithmetic  18.9 us (7%)
    all_to_all x3, waiting for transfers between devices, exchange(): return lax.all_to_all(blocks, axis, 0, 0)  57.7 us
    all_to_all x1, blocking collectives, exchange(): return lax.all_to_all(blocks, axis, 0, 0)  55.2 us
    pallas_call x1, Pallas kernels, gather_seq(): pl.pallas_call(functools.partial(gather_kernel, levels, rows), out_shape=...  32 us
    all_to_all x3, starting transfers between devices, exchange(): return lax.all_to_all(blocks, axis, 0, 0)  20.6 us
    pallas_call x1, Pallas kernels, attend(): pl.pallas_call(attention_kernel, out_shape=(jax.ShapeDtypeStruct((rows, 2...  19.6 us
    ppermute x2, waiting for transfers between devices, from_behind(): return lax.ppermute(array, axis, pairs)  12.2 us
    dot_general x1, matrix products, body(): jnp.einsum('htkc,khcf->tf', grads_all, weight_heads, preferred_element_ty...  7.3 us
    dot_general x1, matrix products, body(): jnp.einsum('htkc,tf->khcf', grads_all, normed, preferred_element_type=jnp...  6.48 us
  transfers between devices with their start and end apart: 6, of which 6 were waited for; matrix products, arithmetic and copies ran while one was open for 11% of the time, Pallas kernels for 0%

profile of v14, /device:TPU:2, one launch (start us, length us, event | category | flops | bytes accessed | tf_op | source)
XLA Modules:
  0.0 269.3 jit_solution(9116418449663770110)
XLA Ops:
  0.6 1.6 maximum_bitcast_fusion.x_ref
  2.2 32.0 %shard_map.124 = bf16[2,32,32,672]{3,2,1,0:T(8,128)(2,1)} custom-call(bf16[2,1,32,672]{3,2,1,0:T(8,128)(2,1)} %maximum_bitcast_fusion.x_ref), custom_call_target="tpu_custom_call" | custom-call | tf_op jit(solution)/shard_map/pallas_call | solution.py:132
  34.3 5.5 %convolution_convert_fusion = bf16[2,1024,1024]{2,1,0:T(8,128)(2,1)S(1)} fusion(bf16[2,1024,672]{2,1,0:T(8,128)(2,1)} %bitcast.103, bf16[1024,672]{0,1:T(8,128)(2,1)S(1)} %copy-done), kind=kOutput, calls=%fused_computation.7 | convolution fusion | flops 2820669440 | bytes 8323072 | tf_op jit(solution)/shard_map/dot_general | solution.py:263
  39.8 0.6 copy.89
  40.4 55.2 %all_to_all.20 = bf16[8,1024,2,128]{1,3,2,0:T(8,128)(2,1)S(1)} all-to-all(bf16[8,1024,2,128]{1,3,2,0:T(8,128)(2,1)S(1)} %bitcast.95), channel_id=1, replica_groups=mesh['level'=4,'row'=4,'core'=2,'uly'=8] {'uly'}, dimensions={0} | all-to-all | bytes 8388608 | tf_op jit(solution)/shard_map/all_to_all | solution.py:30
  95.6 0.8 convert_reduce_fusion
  96.5 0.2 copy.77
  96.9 0.2 multiply_reduce_fusion.3
  97.2 0.2 fusion.10
  97.4 2.1 collective-permute-start
  99.6 1.6 convert_reduce_fusion.2
  101.1 1.2 pad_add_fusion.pos_ref
  102.4 5.6 %collective-permute-done = bf16[2,1024,1,128]{3,1,2,0:T(8,128)(2,1)S(1)} collective-permute-done((bf16[2,1024,1,128]{3,1,2,0:T(8,128)(2,1)S(1)}, bf16[2,1024,1,128]{3,1,2,0:T(8,128)(2,1)S(1)}, u32[]{:S(2)}, u32[]{:S(2)}) %collective-permute-start) | collective-permute-done | bytes 524320 | tf_op jit(solution)/shard_map/ppermute | solution.py:21
  108.0 1.0 slice_bitcast_fusion.1
  109.0 19.6 %shard_map.125 = (bf16[1024,256]{1,0:T(8,128)(2,1)}, f32[1024,256]{1,0:T(8,128)}, f32[2,2048,128]{2,1,0:T(8,128)}) custom-call(s32[2]{0:T(128)} %pad_add_fusion.pos_ref, f32[1,128]{1,0:T(1,128)} %bitcast.111, bf16[1024,256]{1,0:T(8,128)(2,1)} %q_ref.1, bf16[1024,256]{1,0:T(8,128)(2,1)} %do_ref.1, bf16[2048,128]{1,0:T(8,128)(2,1)} %get-tuple-element.46.k_ref, ...), custom_call_target="tpu_custom_call" | custom-call | flops 6442450944 | bytes 8388608 | tf_op jit(solution)/shard_map/pallas_call | solution.py:236
  128.6 1.3 slice.108
  129.9 1.9 collective-permute-start.1
  131.8 6.7 %collective-permute-done.1 = bf16[2,1024,1,128]{3,1,2,0:T(8,128)(2,1)S(1)} collective-permute-done((bf16[2,1024,1,128]{3,1,2,0:T(8,128)(2,1)S(1)}, bf16[2,1024,1,128]{3,1,2,0:T(8,128)(2,1)S(1)}, u32[]{:S(2)}, u32[]{:S(2)}) %collective-permute-start.1) | collective-permute-done | bytes 524320 | tf_op jit(solution)/shard_map/ppermute | solution.py:21
  138.5 1.3 slice_add_fusion
  139.8 0.2 multiply_reduce_fusion.2
  140.1 0.3 fusion.8
  140.5 2.8 %broadcast_in_dim.36 = bf16[8,1024,2,128]{3,1,2,0:T(8,128)(2,1)} broadcast(bf16[1024,2,128]{2,0,1:T(8,128)(2,1)S(1)} %pad_maximum_fusion.1), dimensions={1,2,3} | broadcast | bytes 4718592 | tf_op jit(solution)/shard_map/broadcast_in_dim | solution.py:35
  143.3 4.5 %all-to-all-start.1 = ((bf16[8,1024,2,128]{3,1,2,0:T(8,128)(2,1)}), bf16[8,1024,2,128]{3,1,2,0:T(8,128)(2,1)}, u32[]{:S(2)}, u32[]{:S(2)}) async-start(bf16[8,1024,2,128]{3,1,2,0:T(8,128)(2,1)} %broadcast_in_dim.36), calls=%async_computation.1 | async-start | bytes 8388608 | tf_op jit(solution)/shard_map/all_to_all | solution.py:30
  147.9 50.5 %all-to-all-done.1 = bf16[8,1024,2,128]{3,1,2,0:T(8,128)(2,1)} async-done(((bf16[8,1024,2,128]{3,1,2,0:T(8,128)(2,1)}), bf16[8,1024,2,128]{3,1,2,0:T(8,128)(2,1)}, u32[]{:S(2)}, u32[]{:S(2)}) %all-to-all-start.1) | async-done | bytes 4194336 | tf_op jit(solution)/shard_map/all_to_all | solution.py:30
  198.4 6.5 %convert_bitcast_fusion = bf16[2,8,128,672]{2,3,0,1:T(8,128)(2,1)} fusion(bf16[8,1024,2,128]{3,1,2,0:T(8,128)(2,1)} %all-to-all-done.1, bf16[1024,672]{0,1:T(8,128)(2,1)S(1)} %copy-done), kind=kOutput, calls=%fused_computation.6 | convolution fusion | flops 2819948544 | bytes 8323072 | tf_op jit(solution)/shard_map/htkc,tf->khcf/dot_general | solution.py:310
  204.9 4.6 %copy.64 = bf16[2,8,128,672]{3,2,1,0:T(8,128)(2,1)} copy(bf16[2,8,128,672]{2,3,0,1:T(8,128)(2,1)} %convert_bitcast_fusion) | data formatting | bytes 5505024 | tf_op jit(solution)/shard_map/convert_element_type | solution.py:312
  209.5 2.8 %select_bitcast_fusion = bf16[2,16,32,672]{3,2,1,0:T(8,128)(2,1)} fusion(bf16[2,16,2,32,672]{4,3,2,1,0:T(8,128)(2,1)} %bitcast.96, s32[]{:T(128)S(6)} %select_n.15, pred[]{:T(512)S(6)} %and.16), kind=kLoop, calls=%fused_computation.11 | loop fusion | flops 688128 | bytes 2752517 | tf_op jit(solution)/shard_map/jit(_take)/select_n | solution.py:155
  212.4 1.5 reshape.275
  213.9 2.0 collective-permute-done.2
  215.9 2.0 add_convert_fusion
  217.9 1.3 copy.90
  219.1 4.9 %all-to-all-start.2 = ((bf16[4,4,2,32,672]{4,3,1,2,0:T(8,128)(2,1)}), bf16[4,4,2,32,672]{4,3,1,2,0:T(8,128)(2,1)S(1)}, u32[]{:S(2)}, u32[]{:S(2)}) async-start(bf16[4,4,2,32,672]{4,3,1,2,0:T(8,128)(2,1)} %bitcast.98), calls=%async_computation.2 | async-start | bytes 3145728 | tf_op jit(solution)/shard_map/all_to_all | solution.py:30
  224.0 2.7 %reshape.276 = f32[1024,1,2,128]{3,2,0,1:T(2,128)} reshape(f32[1024,256]{1,0:T(8,128)} %get-tuple-element.31) | data formatting | bytes 2097152 | tf_op jit(solution)/shard_map/reshape | solution.py:290
  226.7 4.8 %multiply_reduce_fusion.1 = (f32[1024,2]{1,0:T(8,128)}, f32[1024,2]{1,0:T(8,128)}) fusion(f32[1024,1,2,128]{3,2,0,1:T(2,128)} %reshape.275, f32[1024,1,2,128]{3,2,0,1:T(2,128)} %reshape.276, f32[128]{0:T(128)S(1)} %broadcast_multiply_fusion), kind=kLoop, calls=%fused_computation.22 | loop fusion | flops 1306624 | bytes 2114048 | tf_op jit(solution)/shard_map/jvp()/reduce_sum | solution.py:25
  231.6 1.2 copy.60
  232.8 1.2 copy.62
  234.1 1.0 copy.61
  235.1 1.0 copy.63
  236.1 2.3 mul.198
  238.4 2.2 broadcast_in_dim.37
  240.6 1.1 fusion.7
  241.7 2.0 all-to-all-done.2
  243.8 0.3 reduce_sum.93
  244.1 0.8 copy.68
  244.9 11.2 %all-to-all-start.3 = ((bf16[4,2,32,672]{3,2,1,0:T(8,128)(2,1)}), bf16[4,2,32,672]{3,2,1,0:T(8,128)(2,1)S(1)}, u32[]{:S(2)}, u32[]{:S(2)}) async-start(bf16[4,2,32,672]{3,2,1,0:T(8,128)(2,1)} %copy.68), calls=%async_computation.3 | async-start | bytes 786432 | tf_op jit(solution)/shard_map/all_to_all | solution.py:30
  256.1 7.3 %bitcast_convert_fusion = bf16[1024,672]{0,1:T(8,128)(2,1)} fusion(bf16[8,1024,2,128]{3,1,2,0:T(8,128)(2,1)} %all-to-all-done.1, bf16[2,8,128,672]{3,2,1,0:T(8,128)(2,1)} %bitcast.104), kind=kOutput, calls=%fused_computation.5 | convolution fusion | flops 2819260416 | bytes 8323072 | tf_op jit(solution)/shard_map/htkc,khcf->tf/dot_general | solution.py:307
  263.4 5.1 %all-to-all-done.3 = bf16[4,2,32,672]{3,2,1,0:T(8,128)(2,1)S(1)} async-done(((bf16[4,2,32,672]{3,2,1,0:T(8,128)(2,1)}), bf16[4,2,32,672]{3,2,1,0:T(8,128)(2,1)S(1)}, u32[]{:S(2)}, u32[]{:S(2)}) %all-to-all-start.3) | async-done | bytes 344096 | tf_op jit(solution)/shard_map/all_to_all | solution.py:30
  268.6 0.7 slice_bitcast_fusion.3
  (24 shorter events, 0.7 us)
Async XLA Ops:
  0.6 33.6 %copy-start = (bf16[1024,672]{0,1:T(8,128)(2,1)S(1)}, bf16[1024,672]{0,1:T(8,128)(2,1)}, u32[]{:S(2)}) copy-start(bf16[1024,672]{0,1:T(8,128)(2,1)} %param.14) | copy-start | bytes 4128772
  96.5 0.7 copy-start.3
  97.4 10.5 %collective-permute-start = (bf16[2,1024,1,128]{3,1,2,0:T(8,128)(2,1)S(1)}, bf16[2,1024,1,128]{3,1,2,0:T(8,128)(2,1)S(1)}, u32[]{:S(2)}, u32[]{:S(2)}) collective-permute-start(bf16[2,1024,1,128]{3,1,2,0:T(8,128)(2,1)S(1)} %pad_maximum_fusion), channel_id=1, source_target_pairs={{0,8},{8,16},{16,24},{24,32},{32,40},{40,48},{48,56},{56,64},{64,7... | collective-permute-start | bytes 1572872 | tf_op jit(solution)/shard_map/ppermute | solution.py:21
  129.9 8.6 %collective-permute-start.1 = (bf16[2,1024,1,128]{3,1,2,0:T(8,128)(2,1)S(1)}, bf16[2,1024,1,128]{3,1,2,0:T(8,128)(2,1)S(1)}, u32[]{:S(2)}, u32[]{:S(2)}) collective-permute-start(bf16[2,1024,1,128]{3,1,2,0:T(8,128)(2,1)S(1)} %slice.108), channel_id=1, source_target_pairs={{8,0},{16,8},{24,16},{32,24},{40,32},{48,40},{56,48},{64,56},{72,6... | collective-permute-start | bytes 1572872 | tf_op jit(solution)/shard_map/ppermute | solution.py:21
  143.3 55.1 %all-to-all-start.1 = ((bf16[8,1024,2,128]{3,1,2,0:T(8,128)(2,1)}), bf16[8,1024,2,128]{3,1,2,0:T(8,128)(2,1)}, u32[]{:S(2)}, u32[]{:S(2)}) async-start(bf16[8,1024,2,128]{3,1,2,0:T(8,128)(2,1)} %broadcast_in_dim.36), calls=%async_computation.1 | async-start | bytes 8388608 | tf_op jit(solution)/shard_map/all_to_all | solution.py:30
  209.5 3.0 %copy-start.2 = (bf16[1024,256]{1,0:T(8,128)(2,1)S(1)}, bf16[1024,256]{1,0:T(8,128)(2,1)}, u32[]{:S(2)}) copy-start(bf16[1024,256]{1,0:T(8,128)(2,1)} %q_ref.1) | copy-start | bytes 1572868
  209.5 4.5 %copy-start.4 = (f32[128]{0:T(128)S(1)}, f32[128]{0:T(128)}, u32[]{:S(2)}) copy-start(f32[128]{0:T(128)} %param.18) | copy-start | bytes 1540
  212.3 3.6 %collective-permute-start.2 = (bf16[2,16,32,672]{3,2,1,0:T(8,128)(2,1)}, bf16[2,16,32,672]{3,2,1,0:T(8,128)(2,1)S(1)}, u32[]{:S(2)}, u32[]{:S(2)}) collective-permute-start(bf16[2,16,32,672]{3,2,1,0:T(8,128)(2,1)} %select_bitcast_fusion), channel_id=1, source_target_pairs={{0,8},{8,0},{1,9},{9,1},{2,10},{10,2},{3,11},{11,3},{4,12},{12,4},... | collective-permute-start | bytes 4128776 | tf_op jit(solution)/shard_map/ppermute | solution.py:156
  219.1 24.6 %all-to-all-start.2 = ((bf16[4,4,2,32,672]{4,3,1,2,0:T(8,128)(2,1)}), bf16[4,4,2,32,672]{4,3,1,2,0:T(8,128)(2,1)S(1)}, u32[]{:S(2)}, u32[]{:S(2)}) async-start(bf16[4,4,2,32,672]{4,3,1,2,0:T(8,128)(2,1)} %bitcast.98), calls=%async_computation.2 | async-start | bytes 3145728 | tf_op jit(solution)/shard_map/all_to_all | solution.py:30
  236.1 4.5 %copy-start.1 = (f32[1024,256]{1,0:T(8,128)S(1)}, f32[1024,256]{1,0:T(8,128)}, u32[]{:S(2)}) copy-start(f32[1024,256]{1,0:T(8,128)} %get-tuple-element.31) | copy-start | bytes 3145732
  244.9 23.6 %all-to-all-start.3 = ((bf16[4,2,32,672]{3,2,1,0:T(8,128)(2,1)}), bf16[4,2,32,672]{3,2,1,0:T(8,128)(2,1)S(1)}, u32[]{:S(2)}, u32[]{:S(2)}) async-start(bf16[4,2,32,672]{3,2,1,0:T(8,128)(2,1)} %copy.68), calls=%async_computation.3 | async-start | bytes 786432 | tf_op jit(solution)/shard_map/all_to_all | solution.py:30

commit v15 on v14

--- a/solution.py
+++ b/solution.py
@@ -189,7 +189,7 @@
 
 def attention_kernel(pos_ref, gain_ref, q_ref, do_ref, k_ref, v_ref, out_ref, dq_ref, dkv_ref):
     rows = q_ref.shape[0]
-    block = 128
+    block = 512
     span = block + WINDOW
     dkv_ref[...] = jnp.zeros(dkv_ref.shape, jnp.float32)
     nt = (((1,), (1,)), ((), ()))

time: 270 us -> 267 us (0.989)
  Pallas kernels: 51.6 us -> 48.5 us
    pallas_call x1, Pallas kernels: 19.6 us -> 16.5 us  [attend(): pl.pallas_call(attention_kernel, out_shape=(jax.ShapeDtypeStruct((rows, 2...]
where the time goes in v15:
time: 267 us; the launch traced here: 266 us
  waiting for transfers between devices  71.9 us (27%)
  blocking collectives  55.2 us (21%)
  Pallas kernels  48.5 us (18%)
  local copies, waits for them, and re-layouts  26.7 us (10%)
  starting transfers between devices  24.8 us (9%)
  matrix products  19.3 us (7%)
  other arithmetic  18.9 us (7%)
    all_to_all x3, waiting for transfers between devices, exchange(): return lax.all_to_all(blocks, axis, 0, 0)  57.7 us
    all_to_all x1, blocking collectives, exchange(): return lax.all_to_all(blocks, axis, 0, 0)  55.2 us
    pallas_call x1, Pallas kernels, gather_seq(): pl.pallas_call(functools.partial(gather_kernel, levels, rows), out_shape=...  32 us
    all_to_all x3, starting transfers between devices, exchange(): return lax.all_to_all(blocks, axis, 0, 0)  20.6 us
    pallas_call x1, Pallas kernels, attend(): pl.pallas_call(attention_kernel, out_shape=(jax.ShapeDtypeStruct((rows, 2...  16.5 us
    ppermute x2, waiting for transfers between devices, from_behind(): return lax.ppermute(array, axis, pairs)  12.2 us
    dot_general x1, matrix products, body(): jnp.einsum('htkc,khcf->tf', grads_all, weight_heads, preferred_element_ty...  7.3 us
    dot_general x1, matrix products, body(): jnp.einsum('htkc,tf->khcf', grads_all, normed, preferred_element_type=jnp...  6.48 us
  transfers between devices with their start and end apart: 6, of which 6 were waited for; matrix products, arithmetic and copies ran while one was open for 11% of the time, Pallas kernels for 0%

profile of v15, /device:TPU:2, one launch (start us, length us, event | category | flops | bytes accessed | tf_op | source)
XLA Modules:
  0.0 266.2 jit_solution(17039394040676168957)
XLA Ops:
  0.6 1.6 maximum_bitcast_fusion.x_ref
  2.2 32.0 %shard_map.124 = bf16[2,32,32,672]{3,2,1,0:T(8,128)(2,1)} custom-call(bf16[2,1,32,672]{3,2,1,0:T(8,128)(2,1)} %maximum_bitcast_fusion.x_ref), custom_call_target="tpu_custom_call" | custom-call | tf_op jit(solution)/shard_map/pallas_call | solution.py:132
  34.3 5.5 %convolution_convert_fusion = bf16[2,1024,1024]{2,1,0:T(8,128)(2,1)S(1)} fusion(bf16[2,1024,672]{2,1,0:T(8,128)(2,1)} %bitcast.103, bf16[1024,672]{0,1:T(8,128)(2,1)S(1)} %copy-done), kind=kOutput, calls=%fused_computation.7 | convolution fusion | flops 2820669440 | bytes 8323072 | tf_op jit(solution)/shard_map/dot_general | solution.py:263
  39.8 0.6 copy.89
  40.4 55.2 %all_to_all.20 = bf16[8,1024,2,128]{1,3,2,0:T(8,128)(2,1)S(1)} all-to-all(bf16[8,1024,2,128]{1,3,2,0:T(8,128)(2,1)S(1)} %bitcast.95), channel_id=1, replica_groups=mesh['level'=4,'row'=4,'core'=2,'uly'=8] {'uly'}, dimensions={0} | all-to-all | bytes 8388608 | tf_op jit(solution)/shard_map/all_to_all | solution.py:30
  95.6 0.8 convert_reduce_fusion
  96.5 0.2 copy.77
  96.9 0.2 multiply_reduce_fusion.3
  97.2 0.2 fusion.10
  97.4 2.1 collective-permute-start
  99.6 1.6 convert_reduce_fusion.2
  101.1 1.2 pad_add_fusion.pos_ref
  102.4 5.6 %collective-permute-done = bf16[2,1024,1,128]{3,1,2,0:T(8,128)(2,1)S(1)} collective-permute-done((bf16[2,1024,1,128]{3,1,2,0:T(8,128)(2,1)S(1)}, bf16[2,1024,1,128]{3,1,2,0:T(8,128)(2,1)S(1)}, u32[]{:S(2)}, u32[]{:S(2)}) %collective-permute-start) | collective-permute-done | bytes 524320 | tf_op jit(solution)/shard_map/ppermute | solution.py:21
  108.0 1.0 slice_bitcast_fusion.1
  109.0 16.5 %shard_map.125 = (bf16[1024,256]{1,0:T(8,128)(2,1)}, f32[1024,256]{1,0:T(8,128)}, f32[2,2048,128]{2,1,0:T(8,128)}) custom-call(s32[2]{0:T(128)} %pad_add_fusion.pos_ref, f32[1,128]{1,0:T(1,128)} %bitcast.111, bf16[1024,256]{1,0:T(8,128)(2,1)} %q_ref.1, bf16[1024,256]{1,0:T(8,128)(2,1)} %do_ref.1, bf16[2048,128]{1,0:T(8,128)(2,1)} %get-tuple-element.46.k_ref, ...), custom_call_target="tpu_custom_call" | custom-call | flops 6442450944 | bytes 8388608 | tf_op jit(solution)/shard_map/pallas_call | solution.py:236
  125.5 1.3 slice.108
  126.8 1.9 collective-permute-start.1
  128.8 6.7 %collective-permute-done.1 = bf16[2,1024,1,128]{3,1,2,0:T(8,128)(2,1)S(1)} collective-permute-done((bf16[2,1024,1,128]{3,1,2,0:T(8,128)(2,1)S(1)}, bf16[2,1024,1,128]{3,1,2,0:T(8,128)(2,1)S(1)}, u32[]{:S(2)}, u32[]{:S(2)}) %collective-permute-start.1) | collective-permute-done | bytes 524320 | tf_op jit(solution)/shard_map/ppermute | solution.py:21
  135.4 1.3 slice_add_fusion
  136.8 0.2 multiply_reduce_fusion.2
  137.0 0.3 fusion.8
  137.4 2.8 %broadcast_in_dim.36 = bf16[8,1024,2,128]{3,1,2,0:T(8,128)(2,1)} broadcast(bf16[1024,2,128]{2,0,1:T(8,128)(2,1)S(1)} %pad_maximum_fusion.1), dimensions={1,2,3} | broadcast | bytes 4718592 | tf_op jit(solution)/shard_map/broadcast_in_dim | solution.py:35
  140.2 4.5 %all-to-all-start.1 = ((bf16[8,1024,2,128]{3,1,2,0:T(8,128)(2,1)}), bf16[8,1024,2,128]{3,1,2,0:T(8,128)(2,1)}, u32[]{:S(2)}, u32[]{:S(2)}) async-start(bf16[8,1024,2,128]{3,1,2,0:T(8,128)(2,1)} %broadcast_in_dim.36), calls=%async_computation.1 | async-start | bytes 8388608 | tf_op jit(solution)/shard_map/all_to_all | solution.py:30
  144.8 50.5 %all-to-all-done.1 = bf16[8,1024,2,128]{3,1,2,0:T(8,128)(2,1)} async-done(((bf16[8,1024,2,128]{3,1,2,0:T(8,128)(2,1)}), bf16[8,1024,2,128]{3,1,2,0:T(8,128)(2,1)}, u32[]{:S(2)}, u32[]{:S(2)}) %all-to-all-start.1) | async-done | bytes 4194336 | tf_op jit(solution)/shard_map/all_to_all | solution.py:30
  195.3 6.5 %convert_bitcast_fusion = bf16[2,8,128,672]{2,3,0,1:T(8,128)(2,1)} fusion(bf16[8,1024,2,128]{3,1,2,0:T(8,128)(2,1)} %all-to-all-done.1, bf16[1024,672]{0,1:T(8,128)(2,1)S(1)} %copy-done), kind=kOutput, calls=%fused_computation.6 | convolution fusion | flops 2819948544 | bytes 8323072 | tf_op jit(solution)/shard_map/htkc,tf->khcf/dot_general | solution.py:310
  201.8 4.6 %copy.64 = bf16[2,8,128,672]{3,2,1,0:T(8,128)(2,1)} copy(bf16[2,8,128,672]{2,3,0,1:T(8,128)(2,1)} %convert_bitcast_fusion) | data formatting | bytes 5505024 | tf_op jit(solution)/shard_map/convert_element_type | solution.py:312
  206.4 2.8 %select_bitcast_fusion = bf16[2,16,32,672]{3,2,1,0:T(8,128)(2,1)} fusion(bf16[2,16,2,32,672]{4,3,2,1,0:T(8,128)(2,1)} %bitcast.96, s32[]{:T(128)S(6)} %select_n.15, pred[]{:T(512)S(6)} %and.16), kind=kLoop, calls=%fused_computation.11 | loop fusion | flops 688128 | bytes 2752517 | tf_op jit(solution)/shard_map/jit(_take)/select_n | solution.py:155
  209.3 1.5 reshape.275
  210.8 2.0 collective-permute-done.2
  212.8 2.0 add_convert_fusion
  214.8 1.3 copy.90
  216.1 4.9 %all-to-all-start.2 = ((bf16[4,4,2,32,672]{4,3,1,2,0:T(8,128)(2,1)}), bf16[4,4,2,32,672]{4,3,1,2,0:T(8,128)(2,1)S(1)}, u32[]{:S(2)}, u32[]{:S(2)}) async-start(bf16[4,4,2,32,672]{4,3,1,2,0:T(8,128)(2,1)} %bitcast.98), calls=%async_computation.2 | async-start | bytes 3145728 | tf_op jit(solution)/shard_map/all_to_all | solution.py:30
  220.9 2.7 %reshape.276 = f32[1024,1,2,128]{3,2,0,1:T(2,128)} reshape(f32[1024,256]{1,0:T(8,128)} %get-tuple-element.31) | data formatting | bytes 2097152 | tf_op jit(solution)/shard_map/reshape | solution.py:290
  223.7 4.8 %multiply_reduce_fusion.1 = (f32[1024,2]{1,0:T(8,128)}, f32[1024,2]{1,0:T(8,128)}) fusion(f32[1024,1,2,128]{3,2,0,1:T(2,128)} %reshape.275, f32[1024,1,2,128]{3,2,0,1:T(2,128)} %reshape.276, f32[128]{0:T(128)S(1)} %broadcast_multiply_fusion), kind=kLoop, calls=%fused_computation.22 | loop fusion | flops 1306624 | bytes 2114048 | tf_op jit(solution)/shard_map/jvp()/reduce_sum | solution.py:25
  228.5 1.2 copy.60
  229.7 1.2 copy.62
  231.0 1.0 copy.61
  232.0 1.0 copy.63
  233.1 2.3 mul.198
  235.3 2.2 broadcast_in_dim.37
  237.5 1.1 fusion.7
  238.7 2.0 all-to-all-done.2
  240.7 0.3 reduce_sum.93
  241.0 0.8 copy.68
  241.8 11.2 %all-to-all-start.3 = ((bf16[4,2,32,672]{3,2,1,0:T(8,128)(2,1)}), bf16[4,2,32,672]{3,2,1,0:T(8,128)(2,1)S(1)}, u32[]{:S(2)}, u32[]{:S(2)}) async-start(bf16[4,2,32,672]{3,2,1,0:T(8,128)(2,1)} %copy.68), calls=%async_computation.3 | async-start | bytes 786432 | tf_op jit(solution)/shard_map/all_to_all | solution.py:30
  253.0 7.3 %bitcast_convert_fusion = bf16[1024,672]{0,1:T(8,128)(2,1)} fusion(bf16[8,1024,2,128]{3,1,2,0:T(8,128)(2,1)} %all-to-all-done.1, bf16[2,8,128,672]{3,2,1,0:T(8,128)(2,1)} %bitcast.104), kind=kOutput, calls=%fused_computation.5 | convolution fusion | flops 2819260416 | bytes 8323072 | tf_op jit(solution)/shard_map/htkc,khcf->tf/dot_general | solution.py:307
  260.3 5.1 %all-to-all-done.3 = bf16[4,2,32,672]{3,2,1,0:T(8,128)(2,1)S(1)} async-done(((bf16[4,2,32,672]{3,2,1,0:T(8,128)(2,1)}), bf16[4,2,32,672]{3,2,1,0:T(8,128)(2,1)S(1)}, u32[]{:S(2)}, u32[]{:S(2)}) %all-to-all-start.3) | async-done | bytes 344096 | tf_op jit(solution)/shard_map/all_to_all | solution.py:30
  265.5 0.7 slice_bitcast_fusion.3
  (24 shorter events, 0.7 us)
Async XLA Ops:
  0.6 33.6 %copy-start = (bf16[1024,672]{0,1:T(8,128)(2,1)S(1)}, bf16[1024,672]{0,1:T(8,128)(2,1)}, u32[]{:S(2)}) copy-start(bf16[1024,672]{0,1:T(8,128)(2,1)} %param.14) | copy-start | bytes 4128772
  96.5 0.7 copy-start.3
  97.4 10.5 %collective-permute-start = (bf16[2,1024,1,128]{3,1,2,0:T(8,128)(2,1)S(1)}, bf16[2,1024,1,128]{3,1,2,0:T(8,128)(2,1)S(1)}, u32[]{:S(2)}, u32[]{:S(2)}) collective-permute-start(bf16[2,1024,1,128]{3,1,2,0:T(8,128)(2,1)S(1)} %pad_maximum_fusion), channel_id=1, source_target_pairs={{0,8},{8,16},{16,24},{24,32},{32,40},{40,48},{48,56},{56,64},{64,7... | collective-permute-start | bytes 1572872 | tf_op jit(solution)/shard_map/ppermute | solution.py:21
  126.8 8.6 %collective-permute-start.1 = (bf16[2,1024,1,128]{3,1,2,0:T(8,128)(2,1)S(1)}, bf16[2,1024,1,128]{3,1,2,0:T(8,128)(2,1)S(1)}, u32[]{:S(2)}, u32[]{:S(2)}) collective-permute-start(bf16[2,1024,1,128]{3,1,2,0:T(8,128)(2,1)S(1)} %slice.108), channel_id=1, source_target_pairs={{8,0},{16,8},{24,16},{32,24},{40,32},{48,40},{56,48},{64,56},{72,6... | collective-permute-start | bytes 1572872 | tf_op jit(solution)/shard_map/ppermute | solution.py:21
  140.2 55.1 %all-to-all-start.1 = ((bf16[8,1024,2,128]{3,1,2,0:T(8,128)(2,1)}), bf16[8,1024,2,128]{3,1,2,0:T(8,128)(2,1)}, u32[]{:S(2)}, u32[]{:S(2)}) async-start(bf16[8,1024,2,128]{3,1,2,0:T(8,128)(2,1)} %broadcast_in_dim.36), calls=%async_computation.1 | async-start | bytes 8388608 | tf_op jit(solution)/shard_map/all_to_all | solution.py:30
  206.4 3.0 %copy-start.2 = (bf16[1024,256]{1,0:T(8,128)(2,1)S(1)}, bf16[1024,256]{1,0:T(8,128)(2,1)}, u32[]{:S(2)}) copy-start(bf16[1024,256]{1,0:T(8,128)(2,1)} %q_ref.1) | copy-start | bytes 1572868
  206.4 4.5 %copy-start.4 = (f32[128]{0:T(128)S(1)}, f32[128]{0:T(128)}, u32[]{:S(2)}) copy-start(f32[128]{0:T(128)} %param.18) | copy-start | bytes 1540
  209.2 3.6 %collective-permute-start.2 = (bf16[2,16,32,672]{3,2,1,0:T(8,128)(2,1)}, bf16[2,16,32,672]{3,2,1,0:T(8,128)(2,1)S(1)}, u32[]{:S(2)}, u32[]{:S(2)}) collective-permute-start(bf16[2,16,32,672]{3,2,1,0:T(8,128)(2,1)} %select_bitcast_fusion), channel_id=1, source_target_pairs={{0,8},{8,0},{1,9},{9,1},{2,10},{10,2},{3,11},{11,3},{4,12},{12,4},... | collective-permute-start | bytes 4128776 | tf_op jit(solution)/shard_map/ppermute | solution.py:156
  216.1 24.6 %all-to-all-start.2 = ((bf16[4,4,2,32,672]{4,3,1,2,0:T(8,128)(2,1)}), bf16[4,4,2,32,672]{4,3,1,2,0:T(8,128)(2,1)S(1)}, u32[]{:S(2)}, u32[]{:S(2)}) async-start(bf16[4,4,2,32,672]{4,3,1,2,0:T(8,128)(2,1)} %bitcast.98), calls=%async_computation.2 | async-start | bytes 3145728 | tf_op jit(solution)/shard_map/all_to_all | solution.py:30
  233.1 4.5 %copy-start.1 = (f32[1024,256]{1,0:T(8,128)S(1)}, f32[1024,256]{1,0:T(8,128)}, u32[]{:S(2)}) copy-start(f32[1024,256]{1,0:T(8,128)} %get-tuple-element.31) | copy-start | bytes 3145732
  241.8 23.6 %all-to-all-start.3 = ((bf16[4,2,32,672]{3,2,1,0:T(8,128)(2,1)}), bf16[4,2,32,672]{3,2,1,0:T(8,128)(2,1)S(1)}, u32[]{:S(2)}, u32[]{:S(2)}) async-start(bf16[4,2,32,672]{3,2,1,0:T(8,128)(2,1)} %copy.68), calls=%async_computation.3 | async-start | bytes 786432 | tf_op jit(solution)/shard_map/all_to_all | solution.py:30
